TPU v7x, 32 devices: a whole 2x2x4 slice. The times are simulated.
32 devices in a mesh: wide: 4 (over y, core), blk: 8 (over z, x).
Axes of the slice: x: 2, y: 2, z: 4, core: 2. Of those that a mesh axis runs over, the one named last changes fastest.
Arguments:
- flux_rows: float32 [32768, 1024], P(('wide', 'blk')), may hold values from -36 to 36
- row_signs: int32 [32768], P(('wide', 'blk')), may hold values from -1 to 1, as said below
- sample_rows: int32 [65536], P(('wide', 'blk')), may hold values from 0 to 1023
- sample_owner: int32 [65536, 1], P(('wide', 'blk')), may hold values from 0 to 7; in each aligned block of 2048 rows (0 to 2047, 2048 to 4095, ...) at most 640 rows name the same one
Outputs:
- transformed: bfloat16 [32768, 1024], P(('wide', 'blk'))
- sketch_factors: float32 [8192, 1024], P(('wide', 'blk'))
Inputs may be any that keep to these rules, and one draw needn't show every extreme that they name: `row_signs`: every entry is -1 or 1. `sample_owner`: among the 2048 sampled rows of one device, no owner is named by more than 640 rows, a bound that some block reaches.
All inputs are finite; a program needn't handle non-finite values.
Results may differ from a plain program's by a relative error of at most 0.0058.
Values may be sent and summed in bfloat16 or wider, within the bound.
No kernel may reach another device: no remote copies, remote signals or barrier semaphores. Data moves between devices by JAX's collectives and lax.ppermute only.
A program may use at most 128 MiB of HBM per device.

v0:
```python
import functools

import jax
import jax.numpy as jnp
import numpy as np
from jax import lax
from jax.experimental import pallas as pl
from jax.experimental.pallas import tpu as pltpu
from jax.sharding import PartitionSpec as P

PANEL = 256
HB = 128
NZ = 4
PIECE = 128
GROUPS = (2, 3, 2, 1)
SQRT_HALF = 0.7071067811865476
HIGHEST = lax.Precision.HIGHEST
F32 = jnp.float32
BF16 = jnp.bfloat16


def hadamard_pair():
    idx = np.arange(HB)
    common = idx[:, None] & idx[None, :]
    parity = np.zeros_like(common)
    for bit in range(HB.bit_length() - 1):
        parity ^= (common >> bit) & 1
    one = 1.0 - 2.0 * parity
    return jnp.asarray(np.kron(np.eye(2), one), BF16)


VMEM_LIMIT = 24 << 20


def params(**kw):
    return pltpu.CompilerParams(vmem_limit_bytes=VMEM_LIMIT, **kw)


def cost(flops, moved):
    return pl.CostEstimate(flops=flops, bytes_accessed=moved, transcendentals=0)


def mix_kernel(signs_ref, had_ref, x_ref, *out_refs):
    rows = x_ref.shape[0]
    size = had_ref.shape[0]
    for which, out_ref in enumerate(out_refs):

        @pl.when(pl.program_id(0) == which)
        def _(out_ref=out_ref):
            for b in range(rows // size):
                part = pl.ds(b * size, size)
                signed = (had_ref[...].astype(F32) * signs_ref[:, b * size : (b + 1) * size].astype(F32)).astype(BF16)
                x = x_ref[part, :]
                hi = x.astype(BF16)
                rest = x - hi.astype(F32)
                mid = rest.astype(BF16)
                low = (rest - mid.astype(F32)).astype(BF16)
                total = jnp.dot(signed, low, preferred_element_type=F32)
                total = total + jnp.dot(signed, mid, preferred_element_type=F32)
                total = total + jnp.dot(signed, hi, preferred_element_type=F32)
                out_ref[part, :] = (total * (HB**-0.5)).astype(BF16)


def mix_columns(signs, had, flux, chunks):
    rows = flux.shape[0]
    start, width = chunks[0]
    first, count = start // width, len(chunks)
    return pl.pallas_call(
        mix_kernel,
        grid=(count,),
        in_specs=[
            pl.BlockSpec((1, rows), lambda i: (0, 0)),
            pl.BlockSpec(had.shape, lambda i: (0, 0)),
            pl.BlockSpec((rows, width), lambda i: (0, i + first)),
        ],
        out_specs=(pl.BlockSpec((rows, width), lambda i: (0, 0)),) * count,
        out_shape=(jax.ShapeDtypeStruct((rows, width), BF16),) * count,
        cost_estimate=cost(2 * count * rows * width * had.shape[0] * 3, count * rows * width * 6),
        name="mix",
    )(signs, had, flux)


def join_kernel(sign_ref, own_ref, other_ref, *refs):
    total = (other_ref[...].astype(F32) + own_ref[...].astype(F32) * sign_ref[0]) * SQRT_HALF
    total = total.astype(BF16)
    for ref in refs[-2:]:
        ref[...] = total


def join_last(own, other, sign, start, columns, whole):
    rows, width = own.shape
    block = start // width
    tile = rows // 2
    chunk = pl.BlockSpec((tile, width), lambda i: (i, 0))
    operands, specs, alias = [sign.reshape(1), own, other], [pl.BlockSpec(memory_space=pltpu.SMEM), chunk, chunk], {}
    if whole is not None:
        operands.append(whole)
        specs.append(pl.BlockSpec(memory_space=pltpu.HBM))
        alias = {3: 1}
    return pl.pallas_call(
        join_kernel,
        grid=(rows // tile,),
        in_specs=specs,
        out_specs=(chunk, pl.BlockSpec((tile, width), lambda i: (i, block))),
        out_shape=(jax.ShapeDtypeStruct((rows, width), BF16), jax.ShapeDtypeStruct((rows, columns), BF16)),
        input_output_aliases=alias,
        compiler_params=params(),
        cost_estimate=cost(4 * rows * width, 8 * rows * width),
        name="join",
    )(*operands)


def relative_owner(q):
    return ((q & 1) << 1) | (q >> 1)


def count_kernel(nx, me_ref, rows_ref, owner_ref, *out_refs):
    listed = rows_ref.shape[1]
    rows = out_refs[0].shape[1]
    me_z, me_x = me_ref[0], me_ref[1]
    index = lax.broadcasted_iota(jnp.int32, (NZ * nx, listed), 0)
    q, s = index & (NZ - 1), index >> (NZ.bit_length() - 1)
    z = me_z ^ relative_owner(q)
    x = (me_x + s) & (nx - 1)
    by_owner = (z * nx + x == owner_ref[...]).astype(F32).astype(BF16)
    by_row = (lax.broadcasted_iota(jnp.int32, (rows, listed), 0) == rows_ref[...]).astype(F32).astype(BF16)
    total = lax.dot_general(by_owner, by_row, (((1,), (1,)), ((), ())), preferred_element_type=F32)
    for shift, ref in enumerate(out_refs):
        ref[...] = total[shift * NZ : (shift + 1) * NZ, :]


def count_samples(sample_rows, sample_owner, nx, rows, me_z, me_x):
    listed = sample_rows.shape[0]
    shape = jax.ShapeDtypeStruct((NZ, rows), F32)
    vmem = pl.BlockSpec(memory_space=pltpu.VMEM)
    return pl.pallas_call(
        functools.partial(count_kernel, nx),
        in_specs=[pl.BlockSpec(memory_space=pltpu.SMEM), vmem, vmem],
        out_shape=(shape,) * nx,
        compiler_params=params(),
        cost_estimate=cost(2 * rows * listed * NZ * nx, rows * NZ * nx * 4),
        name="counts",
    )(jnp.stack([me_z, me_x]), sample_rows.reshape(1, listed), sample_owner.reshape(1, listed))


def weigh_kernel(counts_ref, left_ref, right_ref, hi_ref, lo_ref):
    lead = jnp.concatenate([left_ref[...].astype(F32).T, right_ref[...].astype(F32).T], axis=0)
    for q in range(NZ):
        part = pl.ds(q * PANEL, PANEL)
        weighed = lead * counts_ref[q : q + 1, :]
        hi = weighed.astype(BF16)
        hi_ref[part, :] = hi
        lo_ref[part, :] = (weighed - hi.astype(F32)).astype(BF16)


def weigh(counts, left, right):
    rows = left.shape[0]
    tile = rows // 2
    out = pl.BlockSpec((NZ * PANEL, tile), lambda i: (0, i))
    shape = jax.ShapeDtypeStruct((NZ * PANEL, rows), BF16)
    return pl.pallas_call(
        weigh_kernel,
        grid=(rows // tile,),
        in_specs=[pl.BlockSpec((NZ, tile), lambda i: (0, i))] + [pl.BlockSpec((tile, PANEL // 2), lambda i: (i, 0))] * 2,
        out_specs=(out, out),
        out_shape=(shape, shape),
        compiler_params=params(),
        cost_estimate=cost(rows * PANEL * 16, rows * PANEL * 18),
        name="weigh",
    )(counts, left, right)


GRAM_TILES = 2


def gram_kernel(parts, packed, each, *refs):
    refs, (acc,) = refs[:-1], refs[-1:]
    outs = refs[parts * each :]
    keep_ref, send_ref = (outs[0], outs[1]) if packed else (outs[1], outs[2])
    step = pl.program_id(0)

    @pl.when(step == 0)
    def _():
        acc[...] = jnp.zeros_like(acc)

    for p in range(parts):
        hi_ref, lo_ref, *rows_refs = refs[each * p : each * (p + 1)]

        @pl.when(step // GRAM_TILES == p)
        def _(hi_ref=hi_ref, lo_ref=lo_ref, rows_refs=rows_refs):
            rows = jnp.concatenate([ref[...] for ref in rows_refs], axis=1)
            low = jnp.dot(lo_ref[...], rows, preferred_element_type=F32)
            acc[...] += low + jnp.dot(hi_ref[...], rows, preferred_element_type=F32)

    @pl.when(step == parts * GRAM_TILES - 1)
    def _():
        half = PANEL // 2
        middle = NZ // 2 * PANEL
        if packed:
            for q in range(NZ):
                ref, place = (keep_ref, q) if q < NZ // 2 else (send_ref, q - NZ // 2)
                base, to = q * PANEL, place * 3 * half
                ref[to : to + PANEL, :] = acc[base : base + PANEL, :half]
                ref[to + PANEL : to + 3 * half, :] = acc[base + half : base + PANEL, half:]
        else:
            before_ref, rounded_ref, squares_ref = outs[0], outs[3], outs[4]
            keep_ref[...] = acc[:middle, :]
            send_ref[...] = acc[middle:, :]
            rounded_ref[...] = acc[middle:, :].astype(BF16)
            squares = (acc[...] * acc[...]).astype(BF16)
            ones = jnp.ones((8, squares.shape[1]), BF16)
            squares_ref[...] = before_ref[...] + lax.dot_general(
                ones, squares, (((1,), (1,)), ((), ())), preferred_element_type=F32
            )


def partial_grams(weights, chunk_rows, before):
    packed = before is None
    parts = len(chunk_rows)
    rows = chunk_rows[0][0].shape[0]
    width = sum(piece.shape[1] for piece in chunk_rows[0])
    tile = rows // GRAM_TILES
    half = NZ // 2
    shape = (half * (PANEL + PANEL // 2), PANEL // 2) if packed else (half * PANEL, width)
    operands, specs = [], []
    for p, ((hi, lo), pieces) in enumerate(zip(weights, chunk_rows)):
        operands += [hi, lo, *pieces]

        def place(k, p=p):
            return jnp.clip(k - p * GRAM_TILES, 0, GRAM_TILES - 1)

        weight_spec = pl.BlockSpec((NZ * PANEL, tile), lambda k, place=place: (0, place(k)))
        specs += [weight_spec, weight_spec]
        specs += [pl.BlockSpec((tile, piece.shape[1]), lambda k, place=place: (place(k), 0)) for piece in pieces]
    each = len(operands) // parts
    out = pl.BlockSpec(shape, lambda k: (0, 0))
    out_specs = [out, out]
    out_shape = [jax.ShapeDtypeStruct(shape, F32)] * 2
    if not packed:
        squares = pl.BlockSpec(before.shape, lambda k: (0, 0))
        operands.append(before)
        specs.append(squares)
        out_specs += [out, squares]
        out_shape += [jax.ShapeDtypeStruct(shape, BF16), jax.ShapeDtypeStruct(before.shape, F32)]
    return pl.pallas_call(
        functools.partial(gram_kernel, parts, packed, each),
        grid=(parts * GRAM_TILES,),
        in_specs=specs,
        out_specs=tuple(out_specs),
        out_shape=tuple(out_shape),
        scratch_shapes=[pltpu.VMEM((NZ * PANEL, width), F32)],
        compiler_params=params(),
        cost_estimate=cost(4 * parts * NZ * PANEL * rows * width, 4 * parts * NZ * PANEL * rows + 2 * parts * rows * width),
        name="grams",
    )(*operands)


def add_kernel(keep_ref, near_ref, out_ref):
    out_ref[...] = (keep_ref[...] + near_ref[...].astype(F32)).astype(out_ref.dtype)


def far_sum(keep, near):
    rows, width = keep.shape[0] // 2, keep.shape[1]
    spec = pl.BlockSpec((rows, width), lambda i: (1, 0))
    return pl.pallas_call(
        add_kernel,
        grid=(1,),
        in_specs=[spec, spec],
        out_specs=pl.BlockSpec((rows, width), lambda i: (0, 0)),
        out_shape=jax.ShapeDtypeStruct((rows, width), near.dtype),
        compiler_params=params(),
        cost_estimate=cost(rows * width, 12 * rows * width),
        name="add",
    )(keep, near)


BAND = 64
CUT = 2
MICRO = 8


def factor_band(tile):
    row_id = lax.broadcasted_iota(jnp.int32, (BAND, 1), 0)
    for first in range(0, BAND, MICRO):
        spread = [jnp.broadcast_to(tile[:, first + t : first + t + 1], tile.shape) for t in range(MICRO)]
        for t in range(MICRO):
            j = first + t
            r = lax.rsqrt(spread[t][j : j + 1, :])
            row = tile[j : j + 1, :] * r
            below = jnp.where(row_id > j, spread[t], 0.0)
            for u in range(t + 1, MICRO):
                spread[u] = spread[u] - below * (spread[u][j : j + 1, :] * (r * r))
            tile = jnp.where(row_id == j, row, tile - below * (row * r))
    return tile


def eliminate(work, first, last):
    rb = lax.broadcasted_iota(jnp.int32, (BAND, BAND), 0)
    cb = lax.broadcasted_iota(jnp.int32, (BAND, BAND), 1)
    eye_b = (rb == cb).astype(F32)
    for k in range(first, last):
        lo, hi = k * BAND, (k + 1) * BAND
        tile = factor_band(jnp.concatenate([work[lo:hi, lo:hi], eye_b], axis=1))
        inv = jnp.where(rb >= cb, tile[:, BAND:], 0.0)
        full = jnp.dot(inv, work[lo:hi, lo:], precision=HIGHEST, preferred_element_type=F32)
        if hi < PANEL:
            panel = full[:, BAND : PANEL - lo]
            work[hi:, hi:] = work[hi:, hi:] - lax.dot_general(
                panel, full[:, BAND:], (((0,), (0,)), ((), ())), precision=HIGHEST, preferred_element_type=F32
            )
        work[lo:hi, lo:] = full


def factor_first_kernel(scale, keep_ref, near_ref, far_ref, out_ref, work):
    half = PANEL // 2
    lead = (keep_ref[...] + near_ref[...] + far_ref[...]) * scale
    ri = lax.broadcasted_iota(jnp.int32, (PANEL, PANEL), 0)
    ci = lax.broadcasted_iota(jnp.int32, (PANEL, PANEL), 1)
    eye = (ri == ci).astype(F32)
    work[:, PANEL:] = eye
    work[:half, :half] = lead[:half, :] + 0.5 * eye[:half, :half]
    work[:half, half:PANEL] = lead[half:PANEL, :].T
    work[half:, :half] = lead[half:PANEL, :]
    work[half:, half:PANEL] = lead[PANEL:, :] + 0.5 * eye[:half, :half]
    eliminate(work, 0, CUT)
    out_ref[...] = work[...]


def factor_last_kernel(in_ref, out_ref, inverse_ref, norms_ref, work):
    work[...] = in_ref[...]
    eliminate(work, CUT, PANEL // BAND)
    ri = lax.broadcasted_iota(jnp.int32, (PANEL, PANEL), 0)
    ci = lax.broadcasted_iota(jnp.int32, (PANEL, PANEL), 1)
    upper = jnp.where(ci >= ri, work[:, :PANEL], 0.0)
    inverse = jnp.where(ri >= ci, work[:, PANEL:], 0.0)
    out_ref[...] = upper
    inverse_ref[...] = inverse
    norms_ref[:8, :] = jnp.broadcast_to(jnp.sum(inverse * inverse, axis=0, keepdims=True), (8, PANEL))
    norms_ref[8:, :] = jnp.broadcast_to(jnp.sum(upper * upper, axis=0, keepdims=True), (8, PANEL))


def factor_first(keep, near, far, scale):
    spec = pl.BlockSpec(far.shape, lambda i: (0, 0))
    shape = (PANEL, 2 * PANEL)
    return pl.pallas_call(
        functools.partial(factor_first_kernel, scale),
        grid=(1,),
        in_specs=[spec, spec, spec],
        out_specs=pl.BlockSpec(shape, lambda i: (0, 0)),
        out_shape=jax.ShapeDtypeStruct(shape, F32),
        scratch_shapes=[pltpu.VMEM(shape, F32)],
        compiler_params=params(),
        cost_estimate=cost(10_000_000_000, 1 << 20),
        name="factor_first",
    )(keep, near, far)


def factor_last(state, columns):
    square = pl.BlockSpec((PANEL, PANEL), lambda i: (0, 0))
    return pl.pallas_call(
        factor_last_kernel,
        grid=(1,),
        in_specs=[pl.BlockSpec(state.shape, lambda i: (0, 0))],
        out_specs=(square, square, pl.BlockSpec((16, PANEL), lambda i: (0, 0))),
        out_shape=(
            jax.ShapeDtypeStruct((PANEL, columns), F32),
            jax.ShapeDtypeStruct((PANEL, PANEL), F32),
            jax.ShapeDtypeStruct((16, PANEL), F32),
        ),
        scratch_shapes=[pltpu.VMEM(state.shape, F32)],
        cost_estimate=cost(10_000_000_000, 1 << 20),
        name="factor_last",
    )(state)


def couple_kernel(scale, inverse_ref, keep_ref, near_ref, far_ref, whole_ref, out_ref):
    gram = (keep_ref[...] + near_ref[...].astype(F32) + far_ref[...].astype(F32)) * scale
    out_ref[...] = jnp.dot(inverse_ref[...], gram, precision=HIGHEST, preferred_element_type=F32)


def couple(inverse, keep, near, far, whole, start, scale):
    rows, width = far.shape
    block = start // PIECE
    spec = pl.BlockSpec((rows, PIECE), lambda i: (0, i))
    return pl.pallas_call(
        functools.partial(couple_kernel, scale),
        grid=(width // PIECE,),
        in_specs=[pl.BlockSpec(inverse.shape, lambda i: (0, 0)), spec, spec, spec, pl.BlockSpec(memory_space=pltpu.HBM)],
        out_specs=pl.BlockSpec((rows, PIECE), lambda i: (0, block + i)),
        out_shape=jax.ShapeDtypeStruct(whole.shape, F32),
        input_output_aliases={4: 0},
        cost_estimate=cost(12 * PANEL * rows * width, 20 * rows * width),
        name="couple",
    )(inverse, keep, near, far, whole)


ROUNDING = 0.6 * 2.0**-8
LIMIT = 0.004


def judge_kernel(scale, *refs):
    norms_refs, squares_refs, out_ref = refs[:NZ], refs[NZ : 2 * NZ], refs[-1]
    worst = jnp.zeros((8, 1), F32)
    for owner in range(NZ):
        terms = []
        for sender in range(NZ):
            apart = owner ^ sender
            place = relative_owner(apart) * PANEL
            terms.append(squares_refs[sender][:, place : place + PANEL] * float(apart))
        total = (terms[0] + terms[1]) + (terms[2] + terms[3])
        error = jnp.sum(norms_refs[owner][:8, :] * total, axis=1, keepdims=True) * (ROUNDING * scale) ** 2
        size = jnp.sum(norms_refs[owner][8:, :], axis=1, keepdims=True) * LIMIT**2
        worst = jnp.maximum(worst, jnp.where(error <= size, 0.0, 1.0))
    out_ref[0] = jnp.max(worst).astype(jnp.int32)


def judge(norms, squares, scale):
    vmem = pl.BlockSpec(memory_space=pltpu.VMEM)
    return pl.pallas_call(
        functools.partial(judge_kernel, scale),
        in_specs=[vmem] * (2 * NZ),
        out_specs=pl.BlockSpec(memory_space=pltpu.SMEM),
        out_shape=jax.ShapeDtypeStruct((1,), jnp.int32),
        name="judge",
    )(*norms, *squares)


def per_device(flux_rows, row_signs, sample_rows, sample_owner):
    wide, blk = lax.axis_size("wide"), lax.axis_size("blk")
    nx = blk // NZ
    rows, columns = flux_rows.shape
    scale = 1.0 / sample_rows.shape[0]
    me_w, me_b = lax.axis_index("wide"), lax.axis_index("blk")
    me_x, me_z = me_b & (nx - 1), me_b >> (nx.bit_length() - 1)
    had = hadamard_pair()
    signs = row_signs.reshape(1, rows)
    levels = wide.bit_length() - 1

    def at(z, x):
        return z * nx + x

    def z_route(mask):
        return [(at(z, x), at(z ^ mask, x)) for z in range(NZ) for x in range(nx)]

    def x_shift(s):
        return [(at(z, x), at(z, (x + s) % nx)) for z in range(NZ) for x in range(nx)]

    def level_sign(level):
        return jnp.where((me_w >> level) & 1 == 1, -1.0, 1.0).astype(F32)

    def last_level(own, start, whole):
        partner = lax.ppermute(own, "wide", [(w, w ^ (wide // 2)) for w in range(wide)])
        own, whole = join_last(own, partner, level_sign(levels - 1), start, columns, whole)
        pieces = [own]
        for s in range(1, nx):
            pieces.append(lax.ppermute(own, "blk", x_shift(s)))
        return pieces, whole

    def cut(mixed):
        for level in range(levels - 1):
            partner = lax.ppermute(mixed, "wide", [(w, w ^ (1 << level)) for w in range(wide)])
            halves = []
            for half in range(PANEL // PIECE if level == levels - 2 else 1):
                part = slice(half * PIECE, (half + 1) * PIECE) if level == levels - 2 else slice(None)
                own = mixed[:, part].astype(F32)
                other = partner[:, part].astype(F32)
                halves.append(((other + own * level_sign(level)) * SQRT_HALF).astype(BF16))
            mixed = halves[0]
        return halves

    blocks = [(start, PANEL) for start in range(0, columns, PANEL)]
    mixed = [*mix_columns(signs, had, flux_rows, blocks[:1])]
    counts = count_samples(sample_rows, sample_owner, nx, rows, me_z, me_x)
    owner_counts = [counts[0]]
    for s in range(1, nx):
        owner_counts.append(lax.ppermute(counts[s], "blk", x_shift(s)))
    mixed += mix_columns(signs, had, flux_rows, blocks[1:])
    moved = [half for block in mixed for half in cut(block)]
    pieces, whole = [], None
    for tag, piece in enumerate(moved):
        piece, whole = last_level(piece, tag * PIECE, whole)
        pieces.append(piece)

    weights, grams, precise, starts = [], [], [], []
    squares = jnp.zeros((8, NZ * PANEL), F32)
    done = 0
    for i, count in enumerate(GROUPS):
        sources = [[piece[p] for piece in pieces[done : done + count]] for p in range(nx)]
        if i == 0:
            for p in range(nx):
                weights.append(weigh(owner_counts[p], *sources[p]))
        if i == 0:
            keep, send = partial_grams(weights, sources, None)
        else:
            keep, exact, send, squares = partial_grams(weights, sources, squares)
            precise.append((keep, exact))
            starts.append(done * PIECE)
        near = lax.ppermute(send, "blk", z_route(1))
        onward = far_sum(keep, near)
        far = lax.ppermute(onward, "blk", z_route(2))
        grams.append((keep, near, far))
        done += count
    state = factor_first(*grams[0], scale)
    sketch, inverse, norms = factor_last(state, columns)
    line_norms, line_squares = [norms], [squares]
    for mask in range(1, NZ):
        line_norms.append(lax.ppermute(norms, "blk", z_route(mask)))
        line_squares.append(lax.ppermute(squares, "blk", z_route(mask)))
    redo = judge(line_norms, line_squares, scale)[0] != 0
    for i, start in enumerate(starts[:-1]):
        sketch = couple(inverse, *grams[i + 1], sketch, start, scale)

    def rounded(sketch, inverse, last, precise):
        return couple(inverse, *last, sketch, starts[-1], scale)

    def exact(sketch, inverse, last, precise):
        for (keep, send), start in zip(precise, starts):
            near = lax.ppermute(send, "blk", z_route(1))
            far = lax.ppermute(far_sum(keep, near), "blk", z_route(2))
            sketch = couple(inverse, keep, near, far, sketch, start, scale)
        return sketch

    sketch = lax.cond(redo, exact, rounded, sketch, inverse, grams[-1], precise)
    return whole, sketch


def solution(mesh):
    placed = (
        P(("wide", "blk"), None),
        P(("wide", "blk")),
        P(("wide", "blk")),
        P(("wide", "blk"), None),
    )

    return jax.shard_map(
        per_device,
        mesh=mesh,
        in_specs=placed,
        out_specs=(P(("wide", "blk"), None), P(("wide", "blk"), None)),
        check_vma=False,
    )
```

profile of v0, /device:TPU:0, one launch (start us, length us, event | category | flops | bytes accessed | tf_op | source)
XLA Modules:
  0.0 201.8 jit_solution(16923923311500409832)
XLA Ops:
  0.6 2.7 %mix.3 = bf16[1024,256]{1,0:T(8,128)(2,1)} custom-call(s32[1,1024]{1,0:T(1,128)} %bitcast.9, bf16[256,256]{1,0:T(8,128)(2,1)} %constant.24.clone.had_ref, f32[1024,1024]{1,0:T(8,128)} %x_ref.3), custom_call_target="tpu_custom_call" | custom-call | flops 402653184 | bytes 1572864 | tf_op jit(solution)/shard_map/mix/pallas_call | solution.py:68
  3.9 4.9 %mix.2 = (bf16[1024,256]{1,0:T(8,128)(2,1)}, bf16[1024,256]{1,0:T(8,128)(2,1)}, bf16[1024,256]{1,0:T(8,128)(2,1)}) custom-call(s32[1,1024]{1,0:T(1,128)} %bitcast.10, bf16[256,256]{1,0:T(8,128)(2,1)} %constant.24.clone.had_ref, f32[1024,1024]{1,0:T(8,128)} %x_ref.3), custom_call_target="tpu_custom_call" | custom-call | flops 1207959552 | bytes 4718592 | tf_op jit(solution)/shard_map/mix/pallas_call | solution.py:68
  9.3 1.7 counts.1
  11.1 2.6 %collective-permute-start.18 = (f32[4,1024]{1,0:T(4,128)S(1)}, f32[4,1024]{1,0:T(4,128)S(1)}, u32[]{:S(2)}, u32[]{:S(2)}) collective-permute-start(f32[4,1024]{1,0:T(4,128)S(1)} %get-tuple-element.102), channel_id=1, source_target_pairs={{0,1},{1,0},{2,3},{3,2},{4,5},{5,4},{6,7},{7,6},{8,9},{9,8},{10,11... | collective-permute-start | bytes 49160 | tf_op jit(solution)/shard_map/ppermute | solution.py:476
  14.0 1.6 collective-permute-start.17
  16.9 1.4 multiply_convert_fusion.4
  18.3 1.6 collective-permute-start.11
  21.7 1.5 collective-permute-start.13
  25.1 3.8 %collective-permute-done.16.other_ref = bf16[1024,128]{1,0:T(8,128)(2,1)S(1)} collective-permute-done((bf16[1024,128]{1,0:T(8,128)(2,1)S(1)}, bf16[1024,128]{1,0:T(8,128)(2,1)S(1)}, u32[]{:S(2)}, u32[]{:S(2)}) %collective-permute-start.16) | collective-permute-done | bytes 262176 | tf_op jit(solution)/shard_map/ppermute | solution.py:452
  29.6 1.5 collective-permute-start.7
  31.1 3.4 %collective-permute-done.11.other_ref = bf16[1024,128]{1,0:T(8,128)(2,1)S(1)} collective-permute-done((bf16[1024,128]{1,0:T(8,128)(2,1)S(1)}, bf16[1024,128]{1,0:T(8,128)(2,1)S(1)}, u32[]{:S(2)}, u32[]{:S(2)}) %collective-permute-start.11) | collective-permute-done | bytes 262176 | tf_op jit(solution)/shard_map/ppermute | solution.py:452
  34.5 1.5 collective-permute-start.10
  38.5 1.7 collective-permute-done.14.other_ref
  40.5 5.3 %collective-permute-done.13.other_ref = bf16[1024,128]{1,0:T(8,128)(2,1)} collective-permute-done((bf16[1024,128]{1,0:T(8,128)(2,1)S(1)}, bf16[1024,128]{1,0:T(8,128)(2,1)}, u32[]{:S(2)}, u32[]{:S(2)}) %collective-permute-start.13) | collective-permute-done | bytes 262176 | tf_op jit(solution)/shard_map/ppermute | solution.py:452
  46.1 1.7 join.10
  47.8 1.7 join.11
  52.0 5.0 %collective-permute-done.7.other_ref = bf16[1024,128]{1,0:T(8,128)(2,1)S(1)} collective-permute-done((bf16[1024,128]{1,0:T(8,128)(2,1)S(1)}, bf16[1024,128]{1,0:T(8,128)(2,1)S(1)}, u32[]{:S(2)}, u32[]{:S(2)}) %collective-permute-start.7) | collective-permute-done | bytes 262176 | tf_op jit(solution)/shard_map/ppermute | solution.py:452
  57.3 4.7 %collective-permute-done.10.other_ref = bf16[1024,128]{1,0:T(8,128)(2,1)S(1)} collective-permute-done((bf16[1024,128]{1,0:T(8,128)(2,1)S(1)}, bf16[1024,128]{1,0:T(8,128)(2,1)S(1)}, u32[]{:S(2)}, u32[]{:S(2)}) %collective-permute-start.10) | collective-permute-done | bytes 262176 | tf_op jit(solution)/shard_map/ppermute | solution.py:452
  65.8 1.8 collective-permute-start.26
  69.0 3.8 %grams.4 = (f32[768,128]{1,0:T(8,128)S(1)}, f32[768,128]{1,0:T(8,128)S(1)}) custom-call(bf16[1024,1024]{1,0:T(8,128)(2,1)S(1)} %get-tuple-element.100.refs_0_, bf16[1024,1024]{1,0:T(8,128)(2,1)S(1)} %get-tuple-element.101.refs_1_, bf16[1024,128]{1,0:T(8,128)(2,1)S(1)} %get-tuple-element.98.left_ref.refs_2_, ...), custom_call_target="tpu_custom_call" | custom-call | flops 2147483648 | bytes 9437184 | tf_op jit(solution)/shard_map/grams/pallas_call | solution.py:245
  72.8 1.8 collective-permute-start.27
  74.6 1.6 collective-permute-start.21
  76.1 7.2 %grams.5 = (f32[512,384]{1,0:T(8,128)S(1)}, f32[512,384]{1,0:T(8,128)}, bf16[512,384]{1,0:T(8,128)(2,1)S(1)}, f32[8,1024]{1,0:T(8,128)S(1)}) custom-call(bf16[1024,1024]{1,0:T(8,128)(2,1)S(1)} %get-tuple-element.100.refs_0_, bf16[1024,1024]{1,0:T(8,128)(2,1)S(1)} %get-tuple-element.101.refs_1_, bf16[1024,128]{1,0:T(8,128)(2,1)S(1)} %get-tuple-element.111.refs_2_, ...), custom_call_target="tpu_custom_call" | custom-call | flops 3221225472 | bytes 9961472 | tf_op jit(solution)/shard_map/grams/pallas_call | solution.py:245
  83.8 2.8 %collective-permute-done.27.refs_6_ = bf16[1024,128]{1,0:T(8,128)(2,1)S(1)} collective-permute-done((bf16[1024,128]{1,0:T(8,128)(2,1)S(1)}, bf16[1024,128]{1,0:T(8,128)(2,1)S(1)}, u32[]{:S(2)}, u32[]{:S(2)}) %collective-permute-start.27) | collective-permute-done | bytes 262176 | tf_op jit(solution)/shard_map/ppermute | solution.py:456
  86.7 4.8 %grams.6 = (f32[512,256]{1,0:T(8,128)S(1)}, f32[512,256]{1,0:T(8,128)}, bf16[512,256]{1,0:T(8,128)(2,1)S(1)}, f32[8,1024]{1,0:T(8,128)S(1)}) custom-call(bf16[1024,1024]{1,0:T(8,128)(2,1)S(1)} %get-tuple-element.100.refs_0_, bf16[1024,1024]{1,0:T(8,128)(2,1)S(1)} %get-tuple-element.101.refs_1_, bf16[1024,128]{1,0:T(8,128)(2,1)S(1)} %get-tuple-element.109.refs_2_, ...), custom_call_target="tpu_custom_call" | custom-call | flops 2147483648 | bytes 9437184 | tf_op jit(solution)/shard_map/grams/pallas_call | solution.py:245
  91.4 1.6 collective-permute-start.37
  93.0 2.7 %collective-permute-start.22 = (f32[384,128]{1,0:T(8,128)S(1)}, f32[384,128]{1,0:T(8,128)S(1)}, u32[]{:S(2)}, u32[]{:S(2)}) collective-permute-start(f32[384,128]{1,0:T(8,128)S(1)} %add.52), channel_id=1, source_target_pairs={{0,4},{1,5},{2,6},{3,7},{4,0},{5,1},{6,2},{7,3},{8,12},{9,13},{10,... | collective-permute-start | bytes 589832 | tf_op jit(solution)/shard_map/ppermute | solution.py:500
  95.7 4.6 %grams.7 = (f32[512,128]{1,0:T(8,128)S(1)}, f32[512,128]{1,0:T(8,128)}, bf16[512,128]{1,0:T(8,128)(2,1)S(1)}, f32[8,1024]{1,0:T(8,128)S(1)}) custom-call(bf16[1024,1024]{1,0:T(8,128)(2,1)S(1)} %get-tuple-element.100.refs_0_, bf16[1024,1024]{1,0:T(8,128)(2,1)S(1)} %get-tuple-element.101.refs_1_, bf16[1024,128]{1,0:T(8,128)(2,1)S(1)} %get-tuple-element.108.refs_2_, ...), custom_call_target="tpu_custom_call" | custom-call | flops 1073741824 | bytes 8912896 | tf_op jit(solution)/shard_map/grams/pallas_call | solution.py:245
  102.1 3.5 %collective-permute-done.35.near_ref = bf16[512,128]{1,0:T(8,128)(2,1)S(1)} collective-permute-done((bf16[512,128]{1,0:T(8,128)(2,1)S(1)}, bf16[512,128]{1,0:T(8,128)(2,1)S(1)}, u32[]{:S(2)}, u32[]{:S(2)}) %collective-permute-start.35) | collective-permute-done | bytes 131104 | tf_op jit(solution)/shard_map/ppermute | solution.py:498
  105.6 2.8 %collective-permute-start.33 = (f32[8,1024]{1,0:T(8,128)S(1)}, f32[8,1024]{1,0:T(8,128)}, u32[]{:S(2)}, u32[]{:S(2)}) collective-permute-start(f32[8,1024]{1,0:T(8,128)S(1)} %get-tuple-element.116.refs_4_), channel_id=1, source_target_pairs={{0,4},{1,5},{2,6},{3,7},{4,0},{5,1},{6,2},{7,3},{8,12},{9,13},{10,... | collective-permute-start | bytes 98312 | tf_op jit(solution)/shard_map/ppermute | solution.py:508
  108.6 2.9 %collective-permute-start.38 = (bf16[256,256]{1,0:T(8,128)(2,1)S(1)}, bf16[256,256]{1,0:T(8,128)(2,1)}, u32[]{:S(2)}, u32[]{:S(2)}) collective-permute-start(bf16[256,256]{1,0:T(8,128)(2,1)S(1)} %add.54), channel_id=1, source_target_pairs={{0,4},{1,5},{2,6},{3,7},{4,0},{5,1},{6,2},{7,3},{8,12},{9,13},{10,... | collective-permute-start | bytes 393224 | tf_op jit(solution)/shard_map/ppermute | solution.py:500
  111.8 5.0 %factor_first.1.in_ref = f32[256,512]{1,0:T(8,128)S(1)} custom-call(f32[768,128]{1,0:T(8,128)S(1)} %get-tuple-element.105.keep_ref, f32[768,128]{1,0:T(8,128)S(1)} %collective-permute-done.21.near_ref, f32[384,128]{1,0:T(8,128)S(1)} %collective-permute-done.22.far_ref), custom_call_target="tpu_custom_call" | custom-call | flops 10000000000 | bytes 1048576 | tf_op jit(solution)/shard_map/factor_first/pallas_call | solution.py:345
  117.6 6.0 %factor_last.1 = (f32[256,1024]{1,0:T(8,128)S(1)}, f32[256,256]{1,0:T(8,128)S(1)}, f32[16,256]{1,0:T(8,128)}) custom-call(f32[256,512]{1,0:T(8,128)} %copy-done.10), custom_call_target="tpu_custom_call" | custom-call | flops 10000000000 | bytes 1048576 | tf_op jit(solution)/shard_map/factor_last/pallas_call | solution.py:360
  123.6 3.6 %collective-permute-done.40.far_ref = bf16[256,384]{1,0:T(8,128)(2,1)} collective-permute-done((bf16[256,384]{1,0:T(8,128)(2,1)S(1)}, bf16[256,384]{1,0:T(8,128)(2,1)}, u32[]{:S(2)}, u32[]{:S(2)}) %collective-permute-start.40) | collective-permute-done | bytes 196640 | tf_op jit(solution)/shard_map/ppermute | solution.py:500
  127.2 2.6 %couple.10.whole_ref = f32[256,1024]{1,0:T(8,128)S(1)} custom-call(f32[256,256]{1,0:T(8,128)S(1)} %get-tuple-element.117.inverse_ref, f32[512,384]{1,0:T(8,128)S(1)} %get-tuple-element.122.keep_ref, bf16[512,384]{1,0:T(8,128)(2,1)} %copy-done.2, bf16[256,384]{1,0:T(8,128)(2,1)} %collective-permute-done.40.far_ref, ...), custom_call_target="tpu_custom_call", output_to_operand_aliasing={{}: (4, {})} | custom-call | flops 301989888 | bytes 1966080 | tf_op jit(solution)/shard_map/couple/pallas_call | solution.py:385
  129.9 2.3 %collective-permute-start.25 = (f32[16,256]{1,0:T(8,128)S(1)}, f32[16,256]{1,0:T(8,128)S(1)}, u32[]{:S(2)}, u32[]{:S(2)}) collective-permute-start(f32[16,256]{1,0:T(8,128)S(1)} %copy-done.30), channel_id=1, source_target_pairs={{0,6},{1,7},{2,4},{3,5},{4,2},{5,3},{6,0},{7,1},{8,14},{9,15},{10,... | collective-permute-start | bytes 49160 | tf_op jit(solution)/shard_map/ppermute | solution.py:507
  134.3 1.7 couple.11
  138.0 1.5 judge.1
  140.2 60.7 %conditional.1 = (f32[256,1024]{1,0:T(8,128)S(1)}) conditional(s32[]{:T(128)} %bitcast.6, (f32[256,256]{1,0:T(8,128)S(1)}, f32[512,128]{1,0:T(8,128)S(1)}, bf16[512,128]{1,0:T(8,128)(2,1)S(1)}, bf16[256,128]{1,0:T(8,128)(2,1)S(1)}, f32[256,1024]{1,0:T(8,128)S(1)}) %tuple.24, (f32[512,128]{1,0:T(8,128)}, f32[512,128]{1,0:T(8,128)S(1)}, ...), branch_computations={%region_0.1_spmd, %region_1.2_spmd} | conditional | flops 604176384 | bytes 34603564 | solution.py:523
  143.0 22.8 %collective-permute-done.4.near_ref = f32[512,384]{1,0:T(8,128)S(1)} collective-permute-done((f32[512,384]{1,0:T(8,128)}, f32[512,384]{1,0:T(8,128)S(1)}, u32[]{:S(2)}, u32[]{:S(2)}) %collective-permute-start.4) | collective-permute-done | bytes 786464 | tf_op jit(solution)/shard_map/cond/branch_1_fun/ppermute | solution.py:518
  166.1 2.4 %collective-permute-start = (f32[512,128]{1,0:T(8,128)}, f32[512,128]{1,0:T(8,128)S(1)}, u32[]{:S(2)}, u32[]{:S(2)}) collective-permute-start(f32[512,128]{1,0:T(8,128)} %get-tuple-element.36), channel_id=1, source_target_pairs={{0,2},{1,3},{2,0},{3,1},{4,6},{5,7},{6,4},{7,5},{8,10},{9,11},{10,... | collective-permute-start | bytes 786440 | tf_op jit(solution)/shard_map/cond/branch_1_fun/ppermute | solution.py:518
  168.5 12.4 %collective-permute-done.2.near_ref = f32[512,256]{1,0:T(8,128)S(1)} collective-permute-done((f32[512,256]{1,0:T(8,128)}, f32[512,256]{1,0:T(8,128)S(1)}, u32[]{:S(2)}, u32[]{:S(2)}) %collective-permute-start.2) | collective-permute-done | bytes 524320 | tf_op jit(solution)/shard_map/cond/branch_1_fun/ppermute | solution.py:518
  181.5 4.2 %collective-permute-done.near_ref = f32[512,128]{1,0:T(8,128)S(1)} collective-permute-done((f32[512,128]{1,0:T(8,128)}, f32[512,128]{1,0:T(8,128)S(1)}, u32[]{:S(2)}, u32[]{:S(2)}) %collective-permute-start) | collective-permute-done | bytes 262176 | tf_op jit(solution)/shard_map/cond/branch_1_fun/ppermute | solution.py:518
  185.7 2.8 %collective-permute-start.1 = (f32[256,128]{1,0:T(8,128)S(1)}, f32[256,128]{1,0:T(8,128)S(1)}, u32[]{:S(2)}, u32[]{:S(2)}) collective-permute-start(f32[256,128]{1,0:T(8,128)S(1)} %add.49), channel_id=1, source_target_pairs={{0,4},{1,5},{2,6},{3,7},{4,0},{5,1},{6,2},{7,3},{8,12},{9,13},{10,... | collective-permute-start | bytes 393224 | tf_op jit(solution)/shard_map/cond/branch_1_fun/ppermute | solution.py:519
  189.3 2.9 %couple.7.whole_ref = f32[256,1024]{1,0:T(8,128)S(1)} custom-call(f32[256,256]{1,0:T(8,128)S(1)} %get-tuple-element.34.inverse_ref, f32[512,384]{1,0:T(8,128)} %copy-done.12, f32[512,384]{1,0:T(8,128)} %copy-done, f32[256,384]{1,0:T(8,128)} %copy-done.26, f32[256,1024]{1,0:T(8,128)S(1)} %get-tuple-element.41.whole_ref), custom_call_target="tpu_custom_call", output_to_operand_aliasing={{}: (4, {})} | custom-call | flops 301989888 | bytes 1966080 | tf_op jit(solution)/shard_map/cond/branch_1_fun/couple/pallas_call | solution.py:385
  192.2 4.8 %collective-permute-done.3.far_ref = f32[256,256]{1,0:T(8,128)} collective-permute-done((f32[256,256]{1,0:T(8,128)S(1)}, f32[256,256]{1,0:T(8,128)}, u32[]{:S(2)}, u32[]{:S(2)}) %collective-permute-start.3) | collective-permute-done | bytes 262176 | tf_op jit(solution)/shard_map/cond/branch_1_fun/ppermute | solution.py:519
  197.0 1.9 couple.8.whole_ref
  199.5 1.3 couple.9
  (141 shorter events, 31.9 us)
Async XLA Ops:
  3.4 10.4 %collective-permute-start.15 = (bf16[1024,256]{1,0:T(8,128)(2,1)}, bf16[1024,256]{1,0:T(8,128)(2,1)S(1)}, u32[]{:S(2)}, u32[]{:S(2)}) collective-permute-start(bf16[1024,256]{1,0:T(8,128)(2,1)} %mix.3), channel_id=1, source_target_pairs={{0,8},{8,0},{16,24},{24,16},{1,9},{9,1},{17,25},{25,17},{2,10},{10... | collective-permute-start | bytes 1572872 | tf_op jit(solution)/shard_map/ppermute | solution.py:461
  8.7 6.9 %collective-permute-start.9 = (bf16[1024,256]{1,0:T(8,128)(2,1)}, bf16[1024,256]{1,0:T(8,128)(2,1)S(1)}, u32[]{:S(2)}, u32[]{:S(2)}) collective-permute-start(bf16[1024,256]{1,0:T(8,128)(2,1)} %get-tuple-element.87), channel_id=1, source_target_pairs={{0,8},{8,0},{16,24},{24,16},{1,9},{9,1},{17,25},{25,17},{2,10},{10... | collective-permute-start | bytes 1572872 | tf_op jit(solution)/shard_map/ppermute | solution.py:461
  8.9 9.4 %collective-permute-start.12 = (bf16[1024,256]{1,0:T(8,128)(2,1)}, bf16[1024,256]{1,0:T(8,128)(2,1)}, u32[]{:S(2)}, u32[]{:S(2)}) collective-permute-start(bf16[1024,256]{1,0:T(8,128)(2,1)} %get-tuple-element.88), channel_id=1, source_target_pairs={{0,8},{8,0},{16,24},{24,16},{1,9},{9,1},{17,25},{25,17},{2,10},{10... | collective-permute-start | bytes 1572872 | tf_op jit(solution)/shard_map/ppermute | solution.py:461
  11.1 10.1 %collective-permute-start.18 = (f32[4,1024]{1,0:T(4,128)S(1)}, f32[4,1024]{1,0:T(4,128)S(1)}, u32[]{:S(2)}, u32[]{:S(2)}) collective-permute-start(f32[4,1024]{1,0:T(4,128)S(1)} %get-tuple-element.102), channel_id=1, source_target_pairs={{0,1},{1,0},{2,3},{3,2},{4,5},{5,4},{6,7},{7,6},{8,9},{9,8},{10,11... | collective-permute-start | bytes 49160 | tf_op jit(solution)/shard_map/ppermute | solution.py:476
  13.6 8.1 %collective-permute-start.6 = (bf16[1024,256]{1,0:T(8,128)(2,1)}, bf16[1024,256]{1,0:T(8,128)(2,1)}, u32[]{:S(2)}, u32[]{:S(2)}) collective-permute-start(bf16[1024,256]{1,0:T(8,128)(2,1)} %get-tuple-element.86), channel_id=1, source_target_pairs={{0,8},{8,0},{16,24},{24,16},{1,9},{9,1},{17,25},{25,17},{2,10},{10... | collective-permute-start | bytes 1572872 | tf_op jit(solution)/shard_map/ppermute | solution.py:461
  14.0 10.5 %collective-permute-start.17 = (bf16[1024,128]{1,0:T(8,128)(2,1)S(1)}, bf16[1024,128]{1,0:T(8,128)(2,1)S(1)}, u32[]{:S(2)}, u32[]{:S(2)}) collective-permute-start(bf16[1024,128]{1,0:T(8,128)(2,1)S(1)} %get-tuple-element.128.own_ref), channel_id=1, source_target_pairs={{0,16},{8,24},{16,0},{24,8},{1,17},{9,25},{17,1},{25,9},{2,18},{10... | collective-permute-start | bytes 786440 | tf_op jit(solution)/shard_map/ppermute | solution.py:452
  16.4 12.5 %collective-permute-start.16 = (bf16[1024,128]{1,0:T(8,128)(2,1)S(1)}, bf16[1024,128]{1,0:T(8,128)(2,1)S(1)}, u32[]{:S(2)}, u32[]{:S(2)}) collective-permute-start(bf16[1024,128]{1,0:T(8,128)(2,1)S(1)} %get-tuple-element.129.own_ref), channel_id=1, source_target_pairs={{0,16},{8,24},{16,0},{24,8},{1,17},{9,25},{17,1},{25,9},{2,18},{10... | collective-permute-start | bytes 786440 | tf_op jit(solution)/shard_map/ppermute | solution.py:452
  18.3 16.2 %collective-permute-start.11 = (bf16[1024,128]{1,0:T(8,128)(2,1)S(1)}, bf16[1024,128]{1,0:T(8,128)(2,1)S(1)}, u32[]{:S(2)}, u32[]{:S(2)}) collective-permute-start(bf16[1024,128]{1,0:T(8,128)(2,1)S(1)} %get-tuple-element.132.own_ref), channel_id=1, source_target_pairs={{0,16},{8,24},{16,0},{24,8},{1,17},{9,25},{17,1},{25,9},{2,18},{10... | collective-permute-start | bytes 786440 | tf_op jit(solution)/shard_map/ppermute | solution.py:452
  21.2 19.1 %collective-permute-start.14 = (bf16[1024,128]{1,0:T(8,128)(2,1)S(1)}, bf16[1024,128]{1,0:T(8,128)(2,1)}, u32[]{:S(2)}, u32[]{:S(2)}) collective-permute-start(bf16[1024,128]{1,0:T(8,128)(2,1)S(1)} %get-tuple-element.130.own_ref), channel_id=1, source_target_pairs={{0,16},{8,24},{16,0},{24,8},{1,17},{9,25},{17,1},{25,9},{2,18},{10... | collective-permute-start | bytes 786440 | tf_op jit(solution)/shard_map/ppermute | solution.py:452
  21.7 24.1 %collective-permute-start.13 = (bf16[1024,128]{1,0:T(8,128)(2,1)S(1)}, bf16[1024,128]{1,0:T(8,128)(2,1)}, u32[]{:S(2)}, u32[]{:S(2)}) collective-permute-start(bf16[1024,128]{1,0:T(8,128)(2,1)S(1)} %get-tuple-element.131.own_ref), channel_id=1, source_target_pairs={{0,16},{8,24},{16,0},{24,8},{1,17},{9,25},{17,1},{25,9},{2,18},{10... | collective-permute-start | bytes 786440 | tf_op jit(solution)/shard_map/ppermute | solution.py:452
  24.5 26.8 %collective-permute-start.8 = (bf16[1024,128]{1,0:T(8,128)(2,1)S(1)}, bf16[1024,128]{1,0:T(8,128)(2,1)S(1)}, u32[]{:S(2)}, u32[]{:S(2)}) collective-permute-start(bf16[1024,128]{1,0:T(8,128)(2,1)S(1)} %get-tuple-element.134.own_ref), channel_id=1, source_target_pairs={{0,16},{8,24},{16,0},{24,8},{1,17},{9,25},{17,1},{25,9},{2,18},{10... | collective-permute-start | bytes 786440 | tf_op jit(solution)/shard_map/ppermute | solution.py:452
  29.6 27.4 %collective-permute-start.7 = (bf16[1024,128]{1,0:T(8,128)(2,1)S(1)}, bf16[1024,128]{1,0:T(8,128)(2,1)S(1)}, u32[]{:S(2)}, u32[]{:S(2)}) collective-permute-start(bf16[1024,128]{1,0:T(8,128)(2,1)S(1)} %get-tuple-element.135.own_ref), channel_id=1, source_target_pairs={{0,16},{8,24},{16,0},{24,8},{1,17},{9,25},{17,1},{25,9},{2,18},{10... | collective-permute-start | bytes 786440 | tf_op jit(solution)/shard_map/ppermute | solution.py:452
  34.5 27.5 %collective-permute-start.10 = (bf16[1024,128]{1,0:T(8,128)(2,1)S(1)}, bf16[1024,128]{1,0:T(8,128)(2,1)S(1)}, u32[]{:S(2)}, u32[]{:S(2)}) collective-permute-start(bf16[1024,128]{1,0:T(8,128)(2,1)S(1)} %get-tuple-element.133.own_ref), channel_id=1, source_target_pairs={{0,16},{8,24},{16,0},{24,8},{1,17},{9,25},{17,1},{25,9},{2,18},{10... | collective-permute-start | bytes 786440 | tf_op jit(solution)/shard_map/ppermute | solution.py:452
  40.2 25.5 %collective-permute-start.20 = (bf16[1024,128]{1,0:T(8,128)(2,1)S(1)}, bf16[1024,128]{1,0:T(8,128)(2,1)S(1)}, u32[]{:S(2)}, u32[]{:S(2)}) collective-permute-start(bf16[1024,128]{1,0:T(8,128)(2,1)S(1)} %get-tuple-element.99.right_ref.refs_3_), channel_id=1, source_target_pairs={{0,1},{1,0},{2,3},{3,2},{4,5},{5,4},{6,7},{7,6},{8,9},{9,8},{10,11... | collective-permute-start | bytes 786440 | tf_op jit(solution)/shard_map/ppermute | solution.py:456
  45.8 21.7 %collective-permute-start.19 = (bf16[1024,128]{1,0:T(8,128)(2,1)S(1)}, bf16[1024,128]{1,0:T(8,128)(2,1)S(1)}, u32[]{:S(2)}, u32[]{:S(2)}) collective-permute-start(bf16[1024,128]{1,0:T(8,128)(2,1)S(1)} %get-tuple-element.98.left_ref.refs_2_), channel_id=1, source_target_pairs={{0,1},{1,0},{2,3},{3,2},{4,5},{5,4},{6,7},{7,6},{8,9},{9,8},{10,11... | collective-permute-start | bytes 786440 | tf_op jit(solution)/shard_map/ppermute | solution.py:456
  51.3 21.4 %collective-permute-start.31 = (bf16[1024,128]{1,0:T(8,128)(2,1)S(1)}, bf16[1024,128]{1,0:T(8,128)(2,1)S(1)}, u32[]{:S(2)}, u32[]{:S(2)}) collective-permute-start(bf16[1024,128]{1,0:T(8,128)(2,1)S(1)} %get-tuple-element.113.refs_4_), channel_id=1, source_target_pairs={{0,1},{1,0},{2,3},{3,2},{4,5},{5,4},{6,7},{7,6},{8,9},{9,8},{10,11... | collective-permute-start | bytes 786440 | tf_op jit(solution)/shard_map/ppermute | solution.py:456
  57.0 17.6 %collective-permute-start.30 = (bf16[1024,128]{1,0:T(8,128)(2,1)S(1)}, bf16[1024,128]{1,0:T(8,128)(2,1)S(1)}, u32[]{:S(2)}, u32[]{:S(2)}) collective-permute-start(bf16[1024,128]{1,0:T(8,128)(2,1)S(1)} %get-tuple-element.112.refs_3_), channel_id=1, source_target_pairs={{0,1},{1,0},{2,3},{3,2},{4,5},{5,4},{6,7},{7,6},{8,9},{9,8},{10,11... | collective-permute-start | bytes 786440 | tf_op jit(solution)/shard_map/ppermute | solution.py:456
  62.0 14.2 %collective-permute-start.29 = (bf16[1024,128]{1,0:T(8,128)(2,1)S(1)}, bf16[1024,128]{1,0:T(8,128)(2,1)S(1)}, u32[]{:S(2)}, u32[]{:S(2)}) collective-permute-start(bf16[1024,128]{1,0:T(8,128)(2,1)S(1)} %get-tuple-element.111.refs_2_), channel_id=1, source_target_pairs={{0,1},{1,0},{2,3},{3,2},{4,5},{5,4},{6,7},{7,6},{8,9},{9,8},{10,11... | collective-permute-start | bytes 786440 | tf_op jit(solution)/shard_map/ppermute | solution.py:456
  65.8 30.0 %collective-permute-start.26 = (bf16[1024,128]{1,0:T(8,128)(2,1)S(1)}, bf16[1024,128]{1,0:T(8,128)(2,1)S(1)}, u32[]{:S(2)}, u32[]{:S(2)}) collective-permute-start(bf16[1024,128]{1,0:T(8,128)(2,1)S(1)} %get-tuple-element.108.refs_2_), channel_id=1, source_target_pairs={{0,1},{1,0},{2,3},{3,2},{4,5},{5,4},{6,7},{7,6},{8,9},{9,8},{10,11... | collective-permute-start | bytes 786440 | tf_op jit(solution)/shard_map/ppermute | solution.py:456
  67.5 16.3 %collective-permute-start.28 = (bf16[1024,128]{1,0:T(8,128)(2,1)S(1)}, bf16[1024,128]{1,0:T(8,128)(2,1)S(1)}, u32[]{:S(2)}, u32[]{:S(2)}) collective-permute-start(bf16[1024,128]{1,0:T(8,128)(2,1)S(1)} %get-tuple-element.110.refs_3_), channel_id=1, source_target_pairs={{0,1},{1,0},{2,3},{3,2},{4,5},{5,4},{6,7},{7,6},{8,9},{9,8},{10,11... | collective-permute-start | bytes 786440 | tf_op jit(solution)/shard_map/ppermute | solution.py:456
  72.8 13.9 %collective-permute-start.27 = (bf16[1024,128]{1,0:T(8,128)(2,1)S(1)}, bf16[1024,128]{1,0:T(8,128)(2,1)S(1)}, u32[]{:S(2)}, u32[]{:S(2)}) collective-permute-start(bf16[1024,128]{1,0:T(8,128)(2,1)S(1)} %get-tuple-element.109.refs_2_), channel_id=1, source_target_pairs={{0,1},{1,0},{2,3},{3,2},{4,5},{5,4},{6,7},{7,6},{8,9},{9,8},{10,11... | collective-permute-start | bytes 786440 | tf_op jit(solution)/shard_map/ppermute | solution.py:456
  74.6 18.5 %collective-permute-start.21 = (f32[768,128]{1,0:T(8,128)S(1)}, f32[768,128]{1,0:T(8,128)S(1)}, u32[]{:S(2)}, u32[]{:S(2)}) collective-permute-start(f32[768,128]{1,0:T(8,128)S(1)} %get-tuple-element.106), channel_id=1, source_target_pairs={{0,2},{1,3},{2,0},{3,1},{4,6},{5,7},{6,4},{7,5},{8,10},{9,11},{10,... | collective-permute-start | bytes 1179656 | tf_op jit(solution)/shard_map/ppermute | solution.py:498
  83.4 25.2 %collective-permute-start.39 = (bf16[512,384]{1,0:T(8,128)(2,1)S(1)}, bf16[512,384]{1,0:T(8,128)(2,1)S(1)}, u32[]{:S(2)}, u32[]{:S(2)}) collective-permute-start(bf16[512,384]{1,0:T(8,128)(2,1)S(1)} %get-tuple-element.123), channel_id=1, source_target_pairs={{0,2},{1,3},{2,0},{3,1},{4,6},{5,7},{6,4},{7,5},{8,10},{9,11},{10,... | collective-permute-start | bytes 1179656 | tf_op jit(solution)/shard_map/ppermute | solution.py:498
  91.4 20.1 %copy-start.13 = (f32[512,256]{1,0:T(8,128)}, f32[512,256]{1,0:T(8,128)S(1)}, u32[]{:S(2)}) copy-start(f32[512,256]{1,0:T(8,128)S(1)} %get-tuple-element.120.keep_ref) | copy-start | bytes 1572868
  91.4 17.0 %collective-permute-start.37 = (bf16[512,256]{1,0:T(8,128)(2,1)S(1)}, bf16[512,256]{1,0:T(8,128)(2,1)S(1)}, u32[]{:S(2)}, u32[]{:S(2)}) collective-permute-start(bf16[512,256]{1,0:T(8,128)(2,1)S(1)} %get-tuple-element.121), channel_id=1, source_target_pairs={{0,2},{1,3},{2,0},{3,1},{4,6},{5,7},{6,4},{7,5},{8,10},{9,11},{10,... | collective-permute-start | bytes 786440 | tf_op jit(solution)/shard_map/ppermute | solution.py:498
  93.0 18.5 %collective-permute-start.22 = (f32[384,128]{1,0:T(8,128)S(1)}, f32[384,128]{1,0:T(8,128)S(1)}, u32[]{:S(2)}, u32[]{:S(2)}) collective-permute-start(f32[384,128]{1,0:T(8,128)S(1)} %add.52), channel_id=1, source_target_pairs={{0,4},{1,5},{2,6},{3,7},{4,0},{5,1},{6,2},{7,3},{8,12},{9,13},{10,... | collective-permute-start | bytes 589832 | tf_op jit(solution)/shard_map/ppermute | solution.py:500
  100.3 26.9 %copy-start.7 = (f32[8,1024]{1,0:T(8,128)}, f32[8,1024]{1,0:T(8,128)S(1)}, u32[]{:S(2)}) copy-start(f32[8,1024]{1,0:T(8,128)S(1)} %get-tuple-element.116.refs_4_) | copy-start | bytes 98308
  100.3 5.3 %collective-permute-start.35 = (bf16[512,128]{1,0:T(8,128)(2,1)S(1)}, bf16[512,128]{1,0:T(8,128)(2,1)S(1)}, u32[]{:S(2)}, u32[]{:S(2)}) collective-permute-start(bf16[512,128]{1,0:T(8,128)(2,1)S(1)} %get-tuple-element.119), channel_id=1, source_target_pairs={{0,2},{1,3},{2,0},{3,1},{4,6},{5,7},{6,4},{7,5},{8,10},{9,11},{10,... | collective-permute-start | bytes 393224 | tf_op jit(solution)/shard_map/ppermute | solution.py:498
  100.7 29.1 %collective-permute-start.34 = (f32[8,1024]{1,0:T(8,128)S(1)}, f32[8,1024]{1,0:T(8,128)S(1)}, u32[]{:S(2)}, u32[]{:S(2)}) collective-permute-start(f32[8,1024]{1,0:T(8,128)S(1)} %get-tuple-element.116.refs_4_), channel_id=1, source_target_pairs={{0,6},{1,7},{2,4},{3,5},{4,2},{5,3},{6,0},{7,1},{8,14},{9,15},{10,... | collective-permute-start | bytes 98312 | tf_op jit(solution)/shard_map/ppermute | solution.py:508
  105.6 30.5 %collective-permute-start.33 = (f32[8,1024]{1,0:T(8,128)S(1)}, f32[8,1024]{1,0:T(8,128)}, u32[]{:S(2)}, u32[]{:S(2)}) collective-permute-start(f32[8,1024]{1,0:T(8,128)S(1)} %get-tuple-element.116.refs_4_), channel_id=1, source_target_pairs={{0,4},{1,5},{2,6},{3,7},{4,0},{5,1},{6,2},{7,3},{8,12},{9,13},{10,... | collective-permute-start | bytes 98312 | tf_op jit(solution)/shard_map/ppermute | solution.py:508
  108.4 23.7 %collective-permute-start.36 = (bf16[256,128]{1,0:T(8,128)(2,1)S(1)}, bf16[256,128]{1,0:T(8,128)(2,1)S(1)}, u32[]{:S(2)}, u32[]{:S(2)}) collective-permute-start(bf16[256,128]{1,0:T(8,128)(2,1)S(1)} %add.53), channel_id=1, source_target_pairs={{0,4},{1,5},{2,6},{3,7},{4,0},{5,1},{6,2},{7,3},{8,12},{9,13},{10,... | collective-permute-start | bytes 196616 | tf_op jit(solution)/shard_map/ppermute | solution.py:500
  108.6 24.8 %collective-permute-start.38 = (bf16[256,256]{1,0:T(8,128)(2,1)S(1)}, bf16[256,256]{1,0:T(8,128)(2,1)}, u32[]{:S(2)}, u32[]{:S(2)}) collective-permute-start(bf16[256,256]{1,0:T(8,128)(2,1)S(1)} %add.54), channel_id=1, source_target_pairs={{0,4},{1,5},{2,6},{3,7},{4,0},{5,1},{6,2},{7,3},{8,12},{9,13},{10,... | collective-permute-start | bytes 393224 | tf_op jit(solution)/shard_map/ppermute | solution.py:500
  111.6 15.6 %collective-permute-start.40 = (bf16[256,384]{1,0:T(8,128)(2,1)S(1)}, bf16[256,384]{1,0:T(8,128)(2,1)}, u32[]{:S(2)}, u32[]{:S(2)}) collective-permute-start(bf16[256,384]{1,0:T(8,128)(2,1)S(1)} %add.55), channel_id=1, source_target_pairs={{0,4},{1,5},{2,6},{3,7},{4,0},{5,1},{6,2},{7,3},{8,12},{9,13},{10,... | collective-permute-start | bytes 589832 | tf_op jit(solution)/shard_map/ppermute | solution.py:500
  127.2 8.8 %collective-permute-start.32 = (f32[8,1024]{1,0:T(8,128)S(1)}, f32[8,1024]{1,0:T(8,128)S(1)}, u32[]{:S(2)}, u32[]{:S(2)}) collective-permute-start(f32[8,1024]{1,0:T(8,128)S(1)} %get-tuple-element.116.refs_4_), channel_id=1, source_target_pairs={{0,2},{1,3},{2,0},{3,1},{4,6},{5,7},{6,4},{7,5},{8,10},{9,11},{10,... | collective-permute-start | bytes 98312 | tf_op jit(solution)/shard_map/ppermute | solution.py:508
  129.9 6.2 %collective-permute-start.25 = (f32[16,256]{1,0:T(8,128)S(1)}, f32[16,256]{1,0:T(8,128)S(1)}, u32[]{:S(2)}, u32[]{:S(2)}) collective-permute-start(f32[16,256]{1,0:T(8,128)S(1)} %copy-done.30), channel_id=1, source_target_pairs={{0,6},{1,7},{2,4},{3,5},{4,2},{5,3},{6,0},{7,1},{8,14},{9,15},{10,... | collective-permute-start | bytes 49160 | tf_op jit(solution)/shard_map/ppermute | solution.py:507
  132.2 4.6 %collective-permute-start.24 = (f32[16,256]{1,0:T(8,128)S(1)}, f32[16,256]{1,0:T(8,128)S(1)}, u32[]{:S(2)}, u32[]{:S(2)}) collective-permute-start(f32[16,256]{1,0:T(8,128)S(1)} %copy-done.30), channel_id=1, source_target_pairs={{0,4},{1,5},{2,6},{3,7},{4,0},{5,1},{6,2},{7,3},{8,12},{9,13},{10,... | collective-permute-start | bytes 49160 | tf_op jit(solution)/shard_map/ppermute | solution.py:507
  133.4 3.7 %collective-permute-start.23 = (f32[16,256]{1,0:T(8,128)S(1)}, f32[16,256]{1,0:T(8,128)S(1)}, u32[]{:S(2)}, u32[]{:S(2)}) collective-permute-start(f32[16,256]{1,0:T(8,128)S(1)} %copy-done.30), channel_id=1, source_target_pairs={{0,2},{1,3},{2,0},{3,1},{4,6},{5,7},{6,4},{7,5},{8,10},{9,11},{10,... | collective-permute-start | bytes 49160 | tf_op jit(solution)/shard_map/ppermute | solution.py:507
  141.0 25.1 %copy-start.12 = (f32[512,384]{1,0:T(8,128)}, f32[512,384]{1,0:T(8,128)S(1)}, u32[]{:S(2)}) copy-start(f32[512,384]{1,0:T(8,128)S(1)} %get-tuple-element.39.keep_ref) | copy-start | bytes 2359300 | tf_op jit(solution)/shard_map/cond
  141.0 39.9 %copy-start.16 = (f32[512,256]{1,0:T(8,128)S(1)}, f32[512,256]{1,0:T(8,128)}, u32[]{:S(2)}) copy-start(f32[512,256]{1,0:T(8,128)} %copy-done.15) | copy-start | bytes 1572868 | tf_op jit(solution)/shard_map/cond
  141.0 24.8 %collective-permute-start.4 = (f32[512,384]{1,0:T(8,128)}, f32[512,384]{1,0:T(8,128)S(1)}, u32[]{:S(2)}, u32[]{:S(2)}) collective-permute-start(f32[512,384]{1,0:T(8,128)} %get-tuple-element.40), channel_id=1, source_target_pairs={{0,2},{1,3},{2,0},{3,1},{4,6},{5,7},{6,4},{7,5},{8,10},{9,11},{10,... | collective-permute-start | bytes 2359304 | tf_op jit(solution)/shard_map/cond/branch_1_fun/ppermute | solution.py:518
  142.1 43.6 %copy-start.18 = (f32[512,128]{1,0:T(8,128)S(1)}, f32[512,128]{1,0:T(8,128)}, u32[]{:S(2)}) copy-start(f32[512,128]{1,0:T(8,128)} %copy-done.17) | copy-start | bytes 786436 | tf_op jit(solution)/shard_map/cond
  142.1 38.8 %collective-permute-start.2 = (f32[512,256]{1,0:T(8,128)}, f32[512,256]{1,0:T(8,128)S(1)}, u32[]{:S(2)}, u32[]{:S(2)}) collective-permute-start(f32[512,256]{1,0:T(8,128)} %get-tuple-element.38), channel_id=1, source_target_pairs={{0,2},{1,3},{2,0},{3,1},{4,6},{5,7},{6,4},{7,5},{8,10},{9,11},{10,... | collective-permute-start | bytes 1572872 | tf_op jit(solution)/shard_map/cond/branch_1_fun/ppermute | solution.py:518
  165.8 23.4 %copy-start = (f32[512,384]{1,0:T(8,128)}, f32[512,384]{1,0:T(8,128)S(1)}, u32[]{:S(2)}) copy-start(f32[512,384]{1,0:T(8,128)S(1)} %collective-permute-done.4.near_ref) | copy-start | bytes 2359300 | tf_op jit(solution)/shard_map/cond
  165.9 22.6 %collective-permute-start.5 = (f32[256,384]{1,0:T(8,128)S(1)}, f32[256,384]{1,0:T(8,128)S(1)}, u32[]{:S(2)}, u32[]{:S(2)}) collective-permute-start(f32[256,384]{1,0:T(8,128)S(1)} %add.51), channel_id=1, source_target_pairs={{0,4},{1,5},{2,6},{3,7},{4,0},{5,1},{6,2},{7,3},{8,12},{9,13},{10,... | collective-permute-start | bytes 1179656 | tf_op jit(solution)/shard_map/cond/branch_1_fun/ppermute | solution.py:519
  166.1 19.5 %collective-permute-start = (f32[512,128]{1,0:T(8,128)}, f32[512,128]{1,0:T(8,128)S(1)}, u32[]{:S(2)}, u32[]{:S(2)}) collective-permute-start(f32[512,128]{1,0:T(8,128)} %get-tuple-element.36), channel_id=1, source_target_pairs={{0,2},{1,3},{2,0},{3,1},{4,6},{5,7},{6,4},{7,5},{8,10},{9,11},{10,... | collective-permute-start | bytes 786440 | tf_op jit(solution)/shard_map/cond/branch_1_fun/ppermute | solution.py:518
  180.9 11.3 %copy-start.1 = (f32[512,256]{1,0:T(8,128)}, f32[512,256]{1,0:T(8,128)S(1)}, u32[]{:S(2)}) copy-start(f32[512,256]{1,0:T(8,128)S(1)} %collective-permute-done.2.near_ref) | copy-start | bytes 1572868 | tf_op jit(solution)/shard_map/cond
  180.9 16.0 %collective-permute-start.3 = (f32[256,256]{1,0:T(8,128)S(1)}, f32[256,256]{1,0:T(8,128)}, u32[]{:S(2)}, u32[]{:S(2)}) collective-permute-start(f32[256,256]{1,0:T(8,128)S(1)} %add.50), channel_id=1, source_target_pairs={{0,4},{1,5},{2,6},{3,7},{4,0},{5,1},{6,2},{7,3},{8,12},{9,13},{10,... | collective-permute-start | bytes 786440 | tf_op jit(solution)/shard_map/cond/branch_1_fun/ppermute | solution.py:519
  185.7 13.1 %collective-permute-start.1 = (f32[256,128]{1,0:T(8,128)S(1)}, f32[256,128]{1,0:T(8,128)S(1)}, u32[]{:S(2)}, u32[]{:S(2)}) collective-permute-start(f32[256,128]{1,0:T(8,128)S(1)} %add.49), channel_id=1, source_target_pairs={{0,4},{1,5},{2,6},{3,7},{4,0},{5,1},{6,2},{7,3},{8,12},{9,13},{10,... | collective-permute-start | bytes 393224 | tf_op jit(solution)/shard_map/cond/branch_1_fun/ppermute | solution.py:519
  (27 other events, 119.9 us)
where the time goes:
time: 203 us; the launch traced here: 202 us
  waiting for transfers between devices  80.1 us (39%)
  Pallas kernels  63.1 us (31%)
  starting transfers between devices  45.4 us (22%)
  local copies, waits for them, and re-layouts  7.34 us (4%)
  other arithmetic  4.15 us (2%)
    ppermute x3, waiting for transfers between devices, exact(): near = lax.ppermute(send, 'blk', z_route(1))  39.3 us
    ppermute x8, waiting for transfers between devices, last_level(): lax.ppermute(own, 'wide', [(w, w ^ wide // 2) for w in range(wide)])  25 us
    pallas_call x4, Pallas kernels, partial_grams(): pl.pallas_call(functools.partial(gram_kernel, parts, packed, each), grid=...  20.4 us
    pallas_call x5, Pallas kernels, couple(): pl.pallas_call(functools.partial(couple_kernel, scale), grid=(width // PI...  10.4 us
    ppermute x8, starting transfers between devices, last_level(): lax.ppermute(own, 'wide', [(w, w ^ wide // 2) for w in range(wide)])  9.39 us
    pallas_call x8, Pallas kernels, join_last(): pl.pallas_call(join_kernel, grid=(rows // tile,), in_specs=specs, out_spe...  7.98 us
    pallas_call x2, Pallas kernels, mix_columns(): pl.pallas_call(mix_kernel, grid=(count,), in_specs=[pl.BlockSpec((1, rows...  7.62 us
    pallas_call x1, Pallas kernels, factor_last(): pl.pallas_call(factor_last_kernel, grid=(1,), in_specs=[pl.BlockSpec(stat...  6.04 us
  transfers between devices with their start and end apart: 41, of which 16 were waited for; matrix products, arithmetic and copies ran while one was open for 2% of the time, Pallas kernels for 28%

commit v1 on v0

--- a/solution.py
+++ b/solution.py
@@ -12,7 +12,6 @@
 HB = 128
 NZ = 4
 PIECE = 128
-GROUPS = (2, 3, 2, 1)
 SQRT_HALF = 0.7071067811865476
 HIGHEST = lax.Precision.HIGHEST
 F32 = jnp.float32
@@ -95,7 +94,7 @@
     operands, specs, alias = [sign.reshape(1), own, other], [pl.BlockSpec(memory_space=pltpu.SMEM), chunk, chunk], {}
     if whole is not None:
         operands.append(whole)
-        specs.append(pl.BlockSpec(memory_space=pltpu.HBM))
+        specs.append(pl.BlockSpec(memory_space=pl.ANY))
         alias = {3: 1}
     return pl.pallas_call(
         join_kernel,
@@ -326,7 +325,7 @@
     out_ref[...] = work[...]
 
 
-def factor_last_kernel(in_ref, out_ref, inverse_ref, norms_ref, work):
+def factor_last_kernel(in_ref, squares_ref, out_ref, inverse_ref, guard_ref, work):
     work[...] = in_ref[...]
     eliminate(work, CUT, PANEL // BAND)
     ri = lax.broadcasted_iota(jnp.int32, (PANEL, PANEL), 0)
@@ -335,8 +334,11 @@
     inverse = jnp.where(ri >= ci, work[:, PANEL:], 0.0)
     out_ref[...] = upper
     inverse_ref[...] = inverse
-    norms_ref[:8, :] = jnp.broadcast_to(jnp.sum(inverse * inverse, axis=0, keepdims=True), (8, PANEL))
-    norms_ref[8:, :] = jnp.broadcast_to(jnp.sum(upper * upper, axis=0, keepdims=True), (8, PANEL))
+    guard_ref[:, : NZ * PANEL] = squares_ref[...]
+    for place, part in enumerate((inverse, upper)):
+        start = (NZ + place) * PANEL
+        norms = jnp.sum(part * part, axis=0, keepdims=True)
+        guard_ref[:, start : start + PANEL] = jnp.broadcast_to(norms, (8, PANEL))
 
 
 def factor_first(keep, near, far, scale):
@@ -355,22 +357,26 @@
     )(keep, near, far)
 
 
-def factor_last(state, columns):
-    square = pl.BlockSpec((PANEL, PANEL), lambda i: (0, 0))
+def factor_last(state, squares, columns):
+    def resident(shape):
+        return pl.BlockSpec(shape, lambda i: (0, 0))
+
+    square, guard = (PANEL, PANEL), (8, (NZ + 2) * PANEL)
     return pl.pallas_call(
         factor_last_kernel,
         grid=(1,),
-        in_specs=[pl.BlockSpec(state.shape, lambda i: (0, 0))],
-        out_specs=(square, square, pl.BlockSpec((16, PANEL), lambda i: (0, 0))),
+        in_specs=[resident(state.shape), resident(squares.shape)],
+        out_specs=(resident(square), resident(square), resident(guard)),
         out_shape=(
             jax.ShapeDtypeStruct((PANEL, columns), F32),
-            jax.ShapeDtypeStruct((PANEL, PANEL), F32),
-            jax.ShapeDtypeStruct((16, PANEL), F32),
+            jax.ShapeDtypeStruct(square, F32),
+            jax.ShapeDtypeStruct(guard, F32),
         ),
         scratch_shapes=[pltpu.VMEM(state.shape, F32)],
+        compiler_params=params(),
         cost_estimate=cost(10_000_000_000, 1 << 20),
         name="factor_last",
-    )(state)
+    )(state, squares)
 
 
 def couple_kernel(scale, inverse_ref, keep_ref, near_ref, far_ref, whole_ref, out_ref):
@@ -380,15 +386,16 @@
 
 def couple(inverse, keep, near, far, whole, start, scale):
     rows, width = far.shape
-    block = start // PIECE
-    spec = pl.BlockSpec((rows, PIECE), lambda i: (0, i))
+    block = start // width
+    spec = pl.BlockSpec((rows, width), lambda i: (0, 0))
     return pl.pallas_call(
         functools.partial(couple_kernel, scale),
-        grid=(width // PIECE,),
-        in_specs=[pl.BlockSpec(inverse.shape, lambda i: (0, 0)), spec, spec, spec, pl.BlockSpec(memory_space=pltpu.HBM)],
-        out_specs=pl.BlockSpec((rows, PIECE), lambda i: (0, block + i)),
+        grid=(1,),
+        in_specs=[pl.BlockSpec(inverse.shape, lambda i: (0, 0)), spec, spec, spec, pl.BlockSpec(memory_space=pl.ANY)],
+        out_specs=pl.BlockSpec((rows, width), lambda i: (0, block)),
         out_shape=jax.ShapeDtypeStruct(whole.shape, F32),
         input_output_aliases={4: 0},
+        compiler_params=params(),
         cost_estimate=cost(12 * PANEL * rows * width, 20 * rows * width),
         name="couple",
     )(inverse, keep, near, far, whole)
@@ -399,30 +406,33 @@
 
 
 def judge_kernel(scale, *refs):
-    norms_refs, squares_refs, out_ref = refs[:NZ], refs[NZ : 2 * NZ], refs[-1]
+    *guards, out_ref = refs
     worst = jnp.zeros((8, 1), F32)
     for owner in range(NZ):
         terms = []
         for sender in range(NZ):
             apart = owner ^ sender
             place = relative_owner(apart) * PANEL
-            terms.append(squares_refs[sender][:, place : place + PANEL] * float(apart))
+            terms.append(guards[sender][:, place : place + PANEL] * float(apart))
         total = (terms[0] + terms[1]) + (terms[2] + terms[3])
-        error = jnp.sum(norms_refs[owner][:8, :] * total, axis=1, keepdims=True) * (ROUNDING * scale) ** 2
-        size = jnp.sum(norms_refs[owner][8:, :], axis=1, keepdims=True) * LIMIT**2
+        inverse_norms = guards[owner][:, NZ * PANEL : (NZ + 1) * PANEL]
+        upper_norms = guards[owner][:, (NZ + 1) * PANEL :]
+        error = jnp.sum(inverse_norms * total, axis=1, keepdims=True) * (ROUNDING * scale) ** 2
+        size = jnp.sum(upper_norms, axis=1, keepdims=True) * LIMIT**2
         worst = jnp.maximum(worst, jnp.where(error <= size, 0.0, 1.0))
     out_ref[0] = jnp.max(worst).astype(jnp.int32)
 
 
-def judge(norms, squares, scale):
-    vmem = pl.BlockSpec(memory_space=pltpu.VMEM)
+def judge(guards, scale):
+    spec = pl.BlockSpec(guards[0].shape, lambda i: (0, 0))
     return pl.pallas_call(
         functools.partial(judge_kernel, scale),
-        in_specs=[vmem] * (2 * NZ),
+        grid=(1,),
+        in_specs=[spec] * NZ,
         out_specs=pl.BlockSpec(memory_space=pltpu.SMEM),
         out_shape=jax.ShapeDtypeStruct((1,), jnp.int32),
         name="judge",
-    )(*norms, *squares)
+    )(*guards)
 
 
 def per_device(flux_rows, row_signs, sample_rows, sample_owner):
@@ -456,17 +466,21 @@
             pieces.append(lax.ppermute(own, "blk", x_shift(s)))
         return pieces, whole
 
-    def cut(mixed):
-        for level in range(levels - 1):
+    def level_up(level, own, partner):
+        total = (partner.astype(F32) + own.astype(F32) * level_sign(level)) * SQRT_HALF
+        return total.astype(BF16)
+
+    def first_levels(mixed, last=levels - 1):
+        for level in range(last):
             partner = lax.ppermute(mixed, "wide", [(w, w ^ (1 << level)) for w in range(wide)])
-            halves = []
-            for half in range(PANEL // PIECE if level == levels - 2 else 1):
-                part = slice(half * PIECE, (half + 1) * PIECE) if level == levels - 2 else slice(None)
-                own = mixed[:, part].astype(F32)
-                other = partner[:, part].astype(F32)
-                halves.append(((other + own * level_sign(level)) * SQRT_HALF).astype(BF16))
-            mixed = halves[0]
-        return halves
+            mixed = level_up(level, mixed, partner)
+        return mixed
+
+    def cut_lead(mixed):
+        mixed = first_levels(mixed, levels - 2)
+        partner = lax.ppermute(mixed, "wide", [(w, w ^ (1 << (levels - 2))) for w in range(wide)])
+        cuts = [slice(start, start + PIECE) for start in range(0, PANEL, PIECE)]
+        return [level_up(levels - 2, mixed[:, cut], partner[:, cut]) for cut in cuts]
 
     blocks = [(start, PANEL) for start in range(0, columns, PANEL)]
     mixed = [*mix_columns(signs, had, flux_rows, blocks[:1])]
@@ -475,49 +489,45 @@
     for s in range(1, nx):
         owner_counts.append(lax.ppermute(counts[s], "blk", x_shift(s)))
     mixed += mix_columns(signs, had, flux_rows, blocks[1:])
-    moved = [half for block in mixed for half in cut(block)]
-    pieces, whole = [], None
-    for tag, piece in enumerate(moved):
-        piece, whole = last_level(piece, tag * PIECE, whole)
+    pieces, whole, place = [], None, 0
+    for piece in cut_lead(mixed[0]) + [first_levels(block) for block in mixed[1:]]:
+        piece, whole = last_level(piece, place, whole)
+        place += piece[0].shape[1]
         pieces.append(piece)
-
-    weights, grams, precise, starts = [], [], [], []
+    groups = [[[pieces[0][p], pieces[1][p]] for p in range(nx)]] + [[[piece[p]] for p in range(nx)] for piece in pieces[2:]]
+
+    weights, grams, precise = [], [], []
     squares = jnp.zeros((8, NZ * PANEL), F32)
-    done = 0
-    for i, count in enumerate(GROUPS):
-        sources = [[piece[p] for piece in pieces[done : done + count]] for p in range(nx)]
+    for i, sources in enumerate(groups):
         if i == 0:
             for p in range(nx):
                 weights.append(weigh(owner_counts[p], *sources[p]))
         if i == 0:
             keep, send = partial_grams(weights, sources, None)
         else:
-            keep, exact, send, squares = partial_grams(weights, sources, squares)
-            precise.append((keep, exact))
-            starts.append(done * PIECE)
+            keep, exact_send, send, squares = partial_grams(weights, sources, squares)
+            precise.append((keep, exact_send))
         near = lax.ppermute(send, "blk", z_route(1))
         onward = far_sum(keep, near)
         far = lax.ppermute(onward, "blk", z_route(2))
         grams.append((keep, near, far))
-        done += count
     state = factor_first(*grams[0], scale)
-    sketch, inverse, norms = factor_last(state, columns)
-    line_norms, line_squares = [norms], [squares]
+    sketch, inverse, guard = factor_last(state, squares, columns)
+    guards = [guard]
     for mask in range(1, NZ):
-        line_norms.append(lax.ppermute(norms, "blk", z_route(mask)))
-        line_squares.append(lax.ppermute(squares, "blk", z_route(mask)))
-    redo = judge(line_norms, line_squares, scale)[0] != 0
-    for i, start in enumerate(starts[:-1]):
-        sketch = couple(inverse, *grams[i + 1], sketch, start, scale)
+        guards.append(lax.ppermute(guard, "blk", z_route(mask)))
+    redo = judge(guards, scale)[0] != 0
+    for i in range(1, len(groups) - 1):
+        sketch = couple(inverse, *grams[i], sketch, i * PANEL, scale)
 
     def rounded(sketch, inverse, last, precise):
-        return couple(inverse, *last, sketch, starts[-1], scale)
+        return couple(inverse, *last, sketch, columns - PANEL, scale)
 
     def exact(sketch, inverse, last, precise):
-        for (keep, send), start in zip(precise, starts):
+        for i, (keep, send) in enumerate(precise):
             near = lax.ppermute(send, "blk", z_route(1))
             far = lax.ppermute(far_sum(keep, near), "blk", z_route(2))
-            sketch = couple(inverse, keep, near, far, sketch, start, scale)
+            sketch = couple(inverse, keep, near, far, sketch, (i + 1) * PANEL, scale)
         return sketch
 
     sketch = lax.cond(redo, exact, rounded, sketch, inverse, grams[-1], precise)

time: 203 us -> 193 us (0.951)
  waiting for transfers between devices: 80.1 us -> 102 us
  Pallas kernels: 63.1 us -> 47.3 us
  starting transfers between devices: 45.4 us -> 37.6 us
  local copies, waits for them, and re-layouts: 7.34 us -> 1.6 us
    ppermute x3, waiting for transfers between devices: 4.79 us -> 16.5 us  [exact(): far = lax.ppermute(far_sum(keep, near), 'blk', z_route(2))]
    pallas_call x7, Pallas kernels: 18 us -> 7.92 us  [the longest x1 4.39 us: factor_last(): pl.pallas_call(factor_last_kernel, grid=(1,), in_specs=[resident(state.sh...]
    ppermute x4, waiting for transfers between devices: 3.49 us -> 11.5 us  [per_device(): near = lax.ppermute(send, 'blk', z_route(1))]
    ppermute x10 -> x7, waiting for transfers between devices: 1.07 us -> 6.97 us  [the longest x3 6.96 us: per_device(): guards.append(lax.ppermute(guard, 'blk', z_route(mask)))]
    ppermute x10 -> x7, starting transfers between devices: 9.78 us -> 5.08 us  [the longest x3 3.91 us: per_device(): guards.append(lax.ppermute(guard, 'blk', z_route(mask)))]
    ppermute x8 -> x5, waiting for transfers between devices: 25 us -> 20.3 us  [last_level(): lax.ppermute(own, 'wide', [(w, w ^ wide // 2) for w in range(wide)])]
    ppermute x8 -> x5, waiting for transfers between devices: 2.84 us -> 6.52 us  [last_level(): pieces.append(lax.ppermute(own, 'blk', x_shift(s)))]
    pallas_call x8 -> x5, Pallas kernels: 7.98 us -> 4.34 us  [join_last(): pl.pallas_call(join_kernel, grid=(rows // tile,), in_specs=specs, out_spe...]
  transfers between devices with their start and end apart: 41 -> 32, of which waited for: 16 -> 15; matrix products, arithmetic and copies ran while one was open for 2% -> 2% of each run, Pallas kernels for 28% -> 22%
where the time goes in v1:
time: 193 us
  waiting for transfers between devices  102 us (53%)
  Pallas kernels  47.3 us (25%)
  starting transfers between devices  37.6 us (19%)
  other arithmetic  2.92 us (2%)
    ppermute x3, waiting for transfers between devices, exact(): near = lax.ppermute(send, 'blk', z_route(1))  37.4 us
    ppermute x5, waiting for transfers between devices, last_level(): lax.ppermute(own, 'wide', [(w, w ^ wide // 2) for w in range(wide)])  20.3 us
    pallas_call x4, Pallas kernels, partial_grams(): pl.pallas_call(functools.partial(gram_kernel, parts, packed, each), grid=...  18.2 us
    ppermute x3, waiting for transfers between devices, exact(): far = lax.ppermute(far_sum(keep, near), 'blk', z_route(2))  16.5 us
    ppermute x4, waiting for transfers between devices, per_device(): near = lax.ppermute(send, 'blk', z_route(1))  11.5 us
    ppermute x4, starting transfers between devices, per_device(): far = lax.ppermute(onward, 'blk', z_route(2))  8.98 us
    pallas_call x2, Pallas kernels, mix_columns(): pl.pallas_call(mix_kernel, grid=(count,), in_specs=[pl.BlockSpec((1, rows...  7.66 us
    ppermute x5, starting transfers between devices, last_level(): lax.ppermute(own, 'wide', [(w, w ^ wide // 2) for w in range(wide)])  7.28 us
  transfers between devices with their start and end apart: 32, of which 15 were waited for; matrix products, arithmetic and copies ran while one was open for 2% of the time, Pallas kernels for 22%

profile of v1, /device:TPU:0, one launch (start us, length us, event | category | flops | bytes accessed | tf_op | source)
XLA Modules:
  0.0 192.7 jit_solution(9837508211828179904)
XLA Ops:
  0.6 4.9 %mix.2 = (bf16[1024,256]{1,0:T(8,128)(2,1)}, bf16[1024,256]{1,0:T(8,128)(2,1)}, bf16[1024,256]{1,0:T(8,128)(2,1)}) custom-call(s32[1,1024]{1,0:T(1,128)} %bitcast.9, bf16[256,256]{1,0:T(8,128)(2,1)} %constant.25.clone.had_ref, f32[1024,1024]{1,0:T(8,128)} %x_ref.3), custom_call_target="tpu_custom_call" | custom-call | flops 1207959552 | bytes 4718592 | tf_op jit(solution)/shard_map/mix/pallas_call | solution.py:67
  6.1 2.8 %mix.3 = bf16[1024,256]{1,0:T(8,128)(2,1)} custom-call(s32[1,1024]{1,0:T(1,128)} %bitcast.10, bf16[256,256]{1,0:T(8,128)(2,1)} %constant.25.clone.had_ref, f32[1024,1024]{1,0:T(8,128)} %x_ref.3), custom_call_target="tpu_custom_call" | custom-call | flops 402653184 | bytes 1572864 | tf_op jit(solution)/shard_map/mix/pallas_call | solution.py:67
  9.5 1.2 multiply_convert_fusion.own_ref
  10.7 3.0 %collective-permute-start.11 = (bf16[1024,256]{1,0:T(8,128)(2,1)S(1)}, bf16[1024,256]{1,0:T(8,128)(2,1)S(1)}, u32[]{:S(2)}, u32[]{:S(2)}) collective-permute-start(bf16[1024,256]{1,0:T(8,128)(2,1)S(1)} %multiply_convert_fusion.own_ref), channel_id=1, source_target_pairs={{0,16},{8,24},{16,0},{24,8},{1,17},{9,25},{17,1},{25,9},{2,18},{10... | collective-permute-start | bytes 1572872 | tf_op jit(solution)/shard_map/ppermute | solution.py:462
  13.7 1.2 multiply_convert_fusion.3
  15.0 2.0 %collective-permute-start.14 = (bf16[1024,128]{1,0:T(8,128)(2,1)S(1)}, bf16[1024,128]{1,0:T(8,128)(2,1)S(1)}, u32[]{:S(2)}, u32[]{:S(2)}) collective-permute-start(bf16[1024,128]{1,0:T(8,128)(2,1)S(1)} %get-tuple-element.116.own_ref), channel_id=1, source_target_pairs={{0,16},{8,24},{16,0},{24,8},{1,17},{9,25},{17,1},{25,9},{2,18},{10... | collective-permute-start | bytes 786440 | tf_op jit(solution)/shard_map/ppermute | solution.py:462
  17.4 20.3 %collective-permute-done.14.other_ref = bf16[1024,128]{1,0:T(8,128)(2,1)S(1)} collective-permute-done((bf16[1024,128]{1,0:T(8,128)(2,1)S(1)}, bf16[1024,128]{1,0:T(8,128)(2,1)S(1)}, u32[]{:S(2)}, u32[]{:S(2)}) %collective-permute-start.14) | collective-permute-done | bytes 262176 | tf_op jit(solution)/shard_map/ppermute | solution.py:462
  38.5 2.0 %collective-permute-start.16 = (bf16[1024,128]{1,0:T(8,128)(2,1)S(1)}, bf16[1024,128]{1,0:T(8,128)(2,1)S(1)}, u32[]{:S(2)}, u32[]{:S(2)}) collective-permute-start(bf16[1024,128]{1,0:T(8,128)(2,1)S(1)} %get-tuple-element.89.left_ref.refs_2_), channel_id=1, source_target_pairs={{0,1},{1,0},{2,3},{3,2},{4,5},{5,4},{6,7},{7,6},{8,9},{9,8},{10,11... | collective-permute-start | bytes 786440 | tf_op jit(solution)/shard_map/ppermute | solution.py:466
  41.5 2.1 %collective-permute-start.7 = (bf16[1024,256]{1,0:T(8,128)(2,1)S(1)}, bf16[1024,256]{1,0:T(8,128)(2,1)S(1)}, u32[]{:S(2)}, u32[]{:S(2)}) collective-permute-start(bf16[1024,256]{1,0:T(8,128)(2,1)S(1)} %multiply_convert_fusion.2.own_ref), channel_id=1, source_target_pairs={{0,16},{8,24},{16,0},{24,8},{1,17},{9,25},{17,1},{25,9},{2,18},{10... | collective-permute-start | bytes 1572872 | tf_op jit(solution)/shard_map/ppermute | solution.py:462
  43.7 1.7 counts.1
  45.4 1.5 collective-permute-start.15
  46.9 1.1 weigh.2
  48.0 0.9 join.7
  49.0 2.6 %collective-permute-done.15.counts_ref = f32[4,1024]{1,0:T(4,128)S(1)} collective-permute-done((f32[4,1024]{1,0:T(4,128)S(1)}, f32[4,1024]{1,0:T(4,128)S(1)}, u32[]{:S(2)}, u32[]{:S(2)}) %collective-permute-start.15) | collective-permute-done | bytes 16416 | tf_op jit(solution)/shard_map/ppermute | solution.py:490
  51.6 1.4 collective-permute-start.22
  53.0 1.1 weigh.3
  54.2 3.8 %grams.4 = (f32[768,128]{1,0:T(8,128)S(1)}, f32[768,128]{1,0:T(8,128)S(1)}) custom-call(bf16[1024,1024]{1,0:T(8,128)(2,1)S(1)} %get-tuple-element.91.refs_0_, bf16[1024,1024]{1,0:T(8,128)(2,1)S(1)} %get-tuple-element.92.refs_1_, bf16[1024,128]{1,0:T(8,128)(2,1)S(1)} %get-tuple-element.89.left_ref.refs_2_, ...), custom_call_target="tpu_custom_call" | custom-call | flops 2147483648 | bytes 9437184 | tf_op jit(solution)/shard_map/grams/pallas_call | solution.py:244
  58.0 1.6 collective-permute-start.18
  61.9 1.5 collective-permute-start.20
  63.5 2.9 %collective-permute-done.18.near_ref = f32[768,128]{1,0:T(8,128)S(1)} collective-permute-done((f32[768,128]{1,0:T(8,128)S(1)}, f32[768,128]{1,0:T(8,128)S(1)}, u32[]{:S(2)}, u32[]{:S(2)}) %collective-permute-start.18) | collective-permute-done | bytes 393248 | tf_op jit(solution)/shard_map/ppermute | solution.py:510
  66.3 3.6 %collective-permute-start.19 = (f32[384,128]{1,0:T(8,128)S(1)}, f32[384,128]{1,0:T(8,128)S(1)}, u32[]{:S(2)}, u32[]{:S(2)}) collective-permute-start(f32[384,128]{1,0:T(8,128)S(1)} %add.37), channel_id=1, source_target_pairs={{0,4},{1,5},{2,6},{3,7},{4,0},{5,1},{6,2},{7,3},{8,12},{9,13},{10,... | collective-permute-start | bytes 589832 | tf_op jit(solution)/shard_map/ppermute | solution.py:512
  69.9 4.8 %grams.5 = (f32[512,256]{1,0:T(8,128)S(1)}, f32[512,256]{1,0:T(8,128)}, bf16[512,256]{1,0:T(8,128)(2,1)S(1)}, f32[8,1024]{1,0:T(8,128)S(1)}) custom-call(bf16[1024,1024]{1,0:T(8,128)(2,1)S(1)} %get-tuple-element.91.refs_0_, bf16[1024,1024]{1,0:T(8,128)(2,1)S(1)} %get-tuple-element.92.refs_1_, bf16[1024,256]{1,0:T(8,128)(2,1)S(1)} %get-tuple-element.100.refs_2_, ...), custom_call_target="tpu_custom_call" | custom-call | flops 2147483648 | bytes 9437184 | tf_op jit(solution)/shard_map/grams/pallas_call | solution.py:244
  74.7 2.9 %collective-permute-done.21.refs_5_ = bf16[1024,256]{1,0:T(8,128)(2,1)S(1)} collective-permute-done((bf16[1024,256]{1,0:T(8,128)(2,1)S(1)}, bf16[1024,256]{1,0:T(8,128)(2,1)S(1)}, u32[]{:S(2)}, u32[]{:S(2)}) %collective-permute-start.21) | collective-permute-done | bytes 524320 | tf_op jit(solution)/shard_map/ppermute | solution.py:466
  77.6 4.8 %grams.6 = (f32[512,256]{1,0:T(8,128)S(1)}, f32[512,256]{1,0:T(8,128)}, bf16[512,256]{1,0:T(8,128)(2,1)S(1)}, f32[8,1024]{1,0:T(8,128)S(1)}) custom-call(bf16[1024,1024]{1,0:T(8,128)(2,1)S(1)} %get-tuple-element.91.refs_0_, bf16[1024,1024]{1,0:T(8,128)(2,1)S(1)} %get-tuple-element.92.refs_1_, bf16[1024,256]{1,0:T(8,128)(2,1)S(1)} %get-tuple-element.99.refs_2_, ...), custom_call_target="tpu_custom_call" | custom-call | flops 2147483648 | bytes 9437184 | tf_op jit(solution)/shard_map/grams/pallas_call | solution.py:244
  82.5 3.6 %collective-permute-done.20.refs_5_ = bf16[1024,256]{1,0:T(8,128)(2,1)S(1)} collective-permute-done((bf16[1024,256]{1,0:T(8,128)(2,1)S(1)}, bf16[1024,256]{1,0:T(8,128)(2,1)S(1)}, u32[]{:S(2)}, u32[]{:S(2)}) %collective-permute-start.20) | collective-permute-done | bytes 524320 | tf_op jit(solution)/shard_map/ppermute | solution.py:466
  86.0 4.8 %grams.7 = (f32[512,256]{1,0:T(8,128)S(1)}, f32[512,256]{1,0:T(8,128)}, bf16[512,256]{1,0:T(8,128)(2,1)S(1)}, f32[8,1024]{1,0:T(8,128)S(1)}) custom-call(bf16[1024,1024]{1,0:T(8,128)(2,1)S(1)} %get-tuple-element.91.refs_0_, bf16[1024,1024]{1,0:T(8,128)(2,1)S(1)} %get-tuple-element.92.refs_1_, bf16[1024,256]{1,0:T(8,128)(2,1)S(1)} %get-tuple-element.98.refs_2_, ...), custom_call_target="tpu_custom_call" | custom-call | flops 2147483648 | bytes 9437184 | tf_op jit(solution)/shard_map/grams/pallas_call | solution.py:244
  91.8 1.1 collective-permute-start.28
  93.8 5.0 %factor_first.1.in_ref = f32[256,512]{1,0:T(8,128)S(1)} custom-call(f32[768,128]{1,0:T(8,128)S(1)} %get-tuple-element.96.keep_ref, f32[768,128]{1,0:T(8,128)S(1)} %collective-permute-done.18.near_ref, f32[384,128]{1,0:T(8,128)S(1)} %collective-permute-done.19.far_ref), custom_call_target="tpu_custom_call" | custom-call | flops 10000000000 | bytes 1048576 | tf_op jit(solution)/shard_map/factor_first/pallas_call | solution.py:347
  98.8 7.4 %collective-permute-done.28.near_ref = bf16[512,256]{1,0:T(8,128)(2,1)S(1)} collective-permute-done((bf16[512,256]{1,0:T(8,128)(2,1)S(1)}, bf16[512,256]{1,0:T(8,128)(2,1)S(1)}, u32[]{:S(2)}, u32[]{:S(2)}) %collective-permute-start.28) | collective-permute-done | bytes 262176 | tf_op jit(solution)/shard_map/ppermute | solution.py:510
  106.2 1.5 collective-permute-start.29
  107.6 1.3 collective-permute-done.30.near_ref
  109.0 3.4 %collective-permute-start.31 = (bf16[256,256]{1,0:T(8,128)(2,1)S(1)}, bf16[256,256]{1,0:T(8,128)(2,1)S(1)}, u32[]{:S(2)}, u32[]{:S(2)}) collective-permute-start(bf16[256,256]{1,0:T(8,128)(2,1)S(1)} %add.40), channel_id=1, source_target_pairs={{0,4},{1,5},{2,6},{3,7},{4,0},{5,1},{6,2},{7,3},{8,12},{9,13},{10,... | collective-permute-start | bytes 393224 | tf_op jit(solution)/shard_map/ppermute | solution.py:512
  112.4 4.4 %factor_last.1 = (f32[256,1024]{1,0:T(8,128)S(1)}, f32[256,256]{1,0:T(8,128)S(1)}, f32[8,1536]{1,0:T(8,128)S(1)}) custom-call(f32[256,512]{1,0:T(8,128)S(1)} %factor_first.1.in_ref, f32[8,1024]{1,0:T(8,128)S(1)} %get-tuple-element.103.squares_ref), custom_call_target="tpu_custom_call" | custom-call | flops 10000000000 | bytes 1048576 | tf_op jit(solution)/shard_map/factor_last/pallas_call | solution.py:365
  117.5 2.5 %collective-permute-start.24 = (f32[8,1536]{1,0:T(8,128)S(1)}, f32[8,1536]{1,0:T(8,128)S(1)}, u32[]{:S(2)}, u32[]{:S(2)}) collective-permute-start(f32[8,1536]{1,0:T(8,128)S(1)} %get-tuple-element.104.refs_0_), channel_id=1, source_target_pairs={{0,4},{1,5},{2,6},{3,7},{4,0},{5,1},{6,2},{7,3},{8,12},{9,13},{10,... | collective-permute-start | bytes 147464 | tf_op jit(solution)/shard_map/ppermute | solution.py:518
  120.0 2.2 %collective-permute-done.23.refs_1_ = f32[8,1536]{1,0:T(8,128)S(1)} collective-permute-done((f32[8,1536]{1,0:T(8,128)S(1)}, f32[8,1536]{1,0:T(8,128)S(1)}, u32[]{:S(2)}, u32[]{:S(2)}) %collective-permute-start.23) | collective-permute-done | bytes 49184 | tf_op jit(solution)/shard_map/ppermute | solution.py:518
  122.2 1.2 collective-permute-start.25
  123.5 2.3 %collective-permute-done.24.refs_2_ = f32[8,1536]{1,0:T(8,128)S(1)} collective-permute-done((f32[8,1536]{1,0:T(8,128)S(1)}, f32[8,1536]{1,0:T(8,128)S(1)}, u32[]{:S(2)}, u32[]{:S(2)}) %collective-permute-start.24) | collective-permute-done | bytes 49184 | tf_op jit(solution)/shard_map/ppermute | solution.py:518
  125.7 2.5 %collective-permute-done.25.refs_3_ = f32[8,1536]{1,0:T(8,128)} collective-permute-done((f32[8,1536]{1,0:T(8,128)S(1)}, f32[8,1536]{1,0:T(8,128)}, u32[]{:S(2)}, u32[]{:S(2)}) %collective-permute-start.25) | collective-permute-done | bytes 49184 | tf_op jit(solution)/shard_map/ppermute | solution.py:518
  128.2 1.5 judge.1
  131.9 59.8 %conditional.1 = (f32[256,1024]{1,0:T(8,128)S(1)}) conditional(s32[]{:T(128)} %bitcast.6, (f32[256,256]{1,0:T(8,128)S(1)}, f32[512,256]{1,0:T(8,128)S(1)}, bf16[512,256]{1,0:T(8,128)(2,1)S(1)}, bf16[256,256]{1,0:T(8,128)(2,1)S(1)}, f32[256,1024]{1,0:T(8,128)S(1)}) %tuple.21, (f32[512,256]{1,0:T(8,128)}, f32[512,256]{1,0:T(8,128)S(1)}, ...), branch_computations={%region_0.1_spmd, %region_1.2_spmd} | conditional | flops 604176384 | bytes 19923248 | solution.py:533
  131.9 2.0 %collective-permute-start.2 = (f32[512,256]{1,0:T(8,128)}, f32[512,256]{1,0:T(8,128)S(1)}, u32[]{:S(2)}, u32[]{:S(2)}) collective-permute-start(f32[512,256]{1,0:T(8,128)} %get-tuple-element.38), channel_id=1, source_target_pairs={{0,2},{1,3},{2,0},{3,1},{4,6},{5,7},{6,4},{7,5},{8,10},{9,11},{10,... | collective-permute-start | bytes 1572872 | tf_op jit(solution)/shard_map/cond/branch_1_fun/ppermute | solution.py:528
  134.0 15.7 %collective-permute-done.4.near_ref = f32[512,256]{1,0:T(8,128)S(1)} collective-permute-done((f32[512,256]{1,0:T(8,128)}, f32[512,256]{1,0:T(8,128)S(1)}, u32[]{:S(2)}, u32[]{:S(2)}) %collective-permute-start.4) | collective-permute-done | bytes 524320 | tf_op jit(solution)/shard_map/cond/branch_1_fun/ppermute | solution.py:528
  149.9 16.1 %collective-permute-done.2.near_ref = f32[512,256]{1,0:T(8,128)S(1)} collective-permute-done((f32[512,256]{1,0:T(8,128)}, f32[512,256]{1,0:T(8,128)S(1)}, u32[]{:S(2)}, u32[]{:S(2)}) %collective-permute-start.2) | collective-permute-done | bytes 524320 | tf_op jit(solution)/shard_map/cond/branch_1_fun/ppermute | solution.py:528
  166.1 5.5 %collective-permute-done.near_ref = f32[512,256]{1,0:T(8,128)S(1)} collective-permute-done((f32[512,256]{1,0:T(8,128)}, f32[512,256]{1,0:T(8,128)S(1)}, u32[]{:S(2)}, u32[]{:S(2)}) %collective-permute-start) | collective-permute-done | bytes 524320 | tf_op jit(solution)/shard_map/cond/branch_1_fun/ppermute | solution.py:528
  171.7 2.4 %collective-permute-start.1 = (f32[256,256]{1,0:T(8,128)S(1)}, f32[256,256]{1,0:T(8,128)S(1)}, u32[]{:S(2)}, u32[]{:S(2)}) collective-permute-start(f32[256,256]{1,0:T(8,128)S(1)} %add.34), channel_id=1, source_target_pairs={{0,4},{1,5},{2,6},{3,7},{4,0},{5,1},{6,2},{7,3},{8,12},{9,13},{10,... | collective-permute-start | bytes 786440 | tf_op jit(solution)/shard_map/cond/branch_1_fun/ppermute | solution.py:529
  174.5 14.0 %collective-permute-done.3.far_ref = f32[256,256]{1,0:T(8,128)S(1)} collective-permute-done((f32[256,256]{1,0:T(8,128)S(1)}, f32[256,256]{1,0:T(8,128)S(1)}, u32[]{:S(2)}, u32[]{:S(2)}) %collective-permute-start.3) | collective-permute-done | bytes 262176 | tf_op jit(solution)/shard_map/cond/branch_1_fun/ppermute | solution.py:529
  188.8 2.5 %collective-permute-done.1.far_ref = f32[256,256]{1,0:T(8,128)S(1)} collective-permute-done((f32[256,256]{1,0:T(8,128)S(1)}, f32[256,256]{1,0:T(8,128)S(1)}, u32[]{:S(2)}, u32[]{:S(2)}) %collective-permute-start.1) | collective-permute-done | bytes 262176 | tf_op jit(solution)/shard_map/cond/branch_1_fun/ppermute | solution.py:529
  191.8 1.0 copy-done.3
  (82 shorter events, 11.5 us)
Async XLA Ops:
  5.5 3.4 %copy-start.11 = (bf16[1024,256]{1,0:T(8,128)(2,1)S(1)}, bf16[1024,256]{1,0:T(8,128)(2,1)}, u32[]{:S(2)}) copy-start(bf16[1024,256]{1,0:T(8,128)(2,1)} %get-tuple-element.81) | copy-start | bytes 1572868
  5.5 3.8 %copy-start.10 = (bf16[1024,256]{1,0:T(8,128)(2,1)S(1)}, bf16[1024,256]{1,0:T(8,128)(2,1)}, u32[]{:S(2)}) copy-start(bf16[1024,256]{1,0:T(8,128)(2,1)} %get-tuple-element.80) | copy-start | bytes 1572868
  5.5 3.9 %copy-start.12 = (bf16[1024,256]{1,0:T(8,128)(2,1)S(1)}, bf16[1024,256]{1,0:T(8,128)(2,1)}, u32[]{:S(2)}) copy-start(bf16[1024,256]{1,0:T(8,128)(2,1)} %get-tuple-element.82) | copy-start | bytes 1572868
  5.5 3.9 %collective-permute-start.10 = (bf16[1024,256]{1,0:T(8,128)(2,1)}, bf16[1024,256]{1,0:T(8,128)(2,1)}, u32[]{:S(2)}, u32[]{:S(2)}) collective-permute-start(bf16[1024,256]{1,0:T(8,128)(2,1)} %get-tuple-element.82), channel_id=1, source_target_pairs={{0,8},{8,0},{16,24},{24,16},{1,9},{9,1},{17,25},{25,17},{2,10},{10... | collective-permute-start | bytes 1572872 | tf_op jit(solution)/shard_map/ppermute | solution.py:475
  8.8 4.8 %collective-permute-start.12 = (bf16[1024,256]{1,0:T(8,128)(2,1)}, bf16[1024,256]{1,0:T(8,128)(2,1)S(1)}, u32[]{:S(2)}, u32[]{:S(2)}) collective-permute-start(bf16[1024,256]{1,0:T(8,128)(2,1)} %mix.3), channel_id=1, source_target_pairs={{0,8},{8,0},{16,24},{24,16},{1,9},{9,1},{17,25},{25,17},{2,10},{10... | collective-permute-start | bytes 1572872 | tf_op jit(solution)/shard_map/ppermute | solution.py:481
  9.0 8.0 %collective-permute-start.8 = (bf16[1024,256]{1,0:T(8,128)(2,1)S(1)}, bf16[1024,256]{1,0:T(8,128)(2,1)S(1)}, u32[]{:S(2)}, u32[]{:S(2)}) collective-permute-start(bf16[1024,256]{1,0:T(8,128)(2,1)S(1)} %copy-done.11), channel_id=1, source_target_pairs={{0,8},{8,0},{16,24},{24,16},{1,9},{9,1},{17,25},{25,17},{2,10},{10... | collective-permute-start | bytes 1572872 | tf_op jit(solution)/shard_map/ppermute | solution.py:475
  9.4 31.9 %collective-permute-start.6 = (bf16[1024,256]{1,0:T(8,128)(2,1)S(1)}, bf16[1024,256]{1,0:T(8,128)(2,1)S(1)}, u32[]{:S(2)}, u32[]{:S(2)}) collective-permute-start(bf16[1024,256]{1,0:T(8,128)(2,1)S(1)} %copy-done.10), channel_id=1, source_target_pairs={{0,8},{8,0},{16,24},{24,16},{1,9},{9,1},{17,25},{25,17},{2,10},{10... | collective-permute-start | bytes 1572872 | tf_op jit(solution)/shard_map/ppermute | solution.py:475
  10.7 34.7 %collective-permute-start.11 = (bf16[1024,256]{1,0:T(8,128)(2,1)S(1)}, bf16[1024,256]{1,0:T(8,128)(2,1)S(1)}, u32[]{:S(2)}, u32[]{:S(2)}) collective-permute-start(bf16[1024,256]{1,0:T(8,128)(2,1)S(1)} %multiply_convert_fusion.own_ref), channel_id=1, source_target_pairs={{0,16},{8,24},{16,0},{24,8},{1,17},{9,25},{17,1},{25,9},{2,18},{10... | collective-permute-start | bytes 1572872 | tf_op jit(solution)/shard_map/ppermute | solution.py:462
  14.9 25.5 %collective-permute-start.13 = (bf16[1024,128]{1,0:T(8,128)(2,1)S(1)}, bf16[1024,128]{1,0:T(8,128)(2,1)S(1)}, u32[]{:S(2)}, u32[]{:S(2)}) collective-permute-start(bf16[1024,128]{1,0:T(8,128)(2,1)S(1)} %get-tuple-element.117.own_ref), channel_id=1, source_target_pairs={{0,16},{8,24},{16,0},{24,8},{1,17},{9,25},{17,1},{25,9},{2,18},{10... | collective-permute-start | bytes 786440 | tf_op jit(solution)/shard_map/ppermute | solution.py:462
  15.0 22.7 %collective-permute-start.14 = (bf16[1024,128]{1,0:T(8,128)(2,1)S(1)}, bf16[1024,128]{1,0:T(8,128)(2,1)S(1)}, u32[]{:S(2)}, u32[]{:S(2)}) collective-permute-start(bf16[1024,128]{1,0:T(8,128)(2,1)S(1)} %get-tuple-element.116.own_ref), channel_id=1, source_target_pairs={{0,16},{8,24},{16,0},{24,8},{1,17},{9,25},{17,1},{25,9},{2,18},{10... | collective-permute-start | bytes 786440 | tf_op jit(solution)/shard_map/ppermute | solution.py:462
  17.2 42.4 %collective-permute-start.9 = (bf16[1024,256]{1,0:T(8,128)(2,1)S(1)}, bf16[1024,256]{1,0:T(8,128)(2,1)S(1)}, u32[]{:S(2)}, u32[]{:S(2)}) collective-permute-start(bf16[1024,256]{1,0:T(8,128)(2,1)S(1)} %multiply_convert_fusion.1.own_ref), channel_id=1, source_target_pairs={{0,16},{8,24},{16,0},{24,8},{1,17},{9,25},{17,1},{25,9},{2,18},{10... | collective-permute-start | bytes 1572872 | tf_op jit(solution)/shard_map/ppermute | solution.py:462
  38.5 14.6 %collective-permute-start.16 = (bf16[1024,128]{1,0:T(8,128)(2,1)S(1)}, bf16[1024,128]{1,0:T(8,128)(2,1)S(1)}, u32[]{:S(2)}, u32[]{:S(2)}) collective-permute-start(bf16[1024,128]{1,0:T(8,128)(2,1)S(1)} %get-tuple-element.89.left_ref.refs_2_), channel_id=1, source_target_pairs={{0,1},{1,0},{2,3},{3,2},{4,5},{5,4},{6,7},{7,6},{8,9},{9,8},{10,11... | collective-permute-start | bytes 786440 | tf_op jit(solution)/shard_map/ppermute | solution.py:466
  40.5 3.2 %copy-start.1 = (s32[2048]{0:T(1024)S(1)}, s32[2048]{0:T(1024)}, u32[]{:S(2)}) copy-start(s32[2048]{0:T(1024)} %param.9) | copy-start | bytes 24580
  40.5 3.2 %copy-start.2 = (s32[2048,1]{0,1:T(1,128)S(1)}, s32[2048,1]{0,1:T(1,128)}, u32[]{:S(2)}) copy-start(s32[2048,1]{0,1:T(1,128)} %param.10) | copy-start | bytes 24580
  41.3 11.8 %collective-permute-start.17 = (bf16[1024,128]{1,0:T(8,128)(2,1)S(1)}, bf16[1024,128]{1,0:T(8,128)(2,1)S(1)}, u32[]{:S(2)}, u32[]{:S(2)}) collective-permute-start(bf16[1024,128]{1,0:T(8,128)(2,1)S(1)} %get-tuple-element.90.right_ref.refs_3_), channel_id=1, source_target_pairs={{0,1},{1,0},{2,3},{3,2},{4,5},{5,4},{6,7},{7,6},{8,9},{9,8},{10,11... | collective-permute-start | bytes 786440 | tf_op jit(solution)/shard_map/ppermute | solution.py:466
  41.5 19.5 %collective-permute-start.7 = (bf16[1024,256]{1,0:T(8,128)(2,1)S(1)}, bf16[1024,256]{1,0:T(8,128)(2,1)S(1)}, u32[]{:S(2)}, u32[]{:S(2)}) collective-permute-start(bf16[1024,256]{1,0:T(8,128)(2,1)S(1)} %multiply_convert_fusion.2.own_ref), channel_id=1, source_target_pairs={{0,16},{8,24},{16,0},{24,8},{1,17},{9,25},{17,1},{25,9},{2,18},{10... | collective-permute-start | bytes 1572872 | tf_op jit(solution)/shard_map/ppermute | solution.py:462
  45.4 6.2 %collective-permute-start.15 = (f32[4,1024]{1,0:T(4,128)S(1)}, f32[4,1024]{1,0:T(4,128)S(1)}, u32[]{:S(2)}, u32[]{:S(2)}) collective-permute-start(f32[4,1024]{1,0:T(4,128)S(1)} %get-tuple-element.93), channel_id=1, source_target_pairs={{0,1},{1,0},{2,3},{3,2},{4,5},{5,4},{6,7},{7,6},{8,9},{9,8},{10,11... | collective-permute-start | bytes 49160 | tf_op jit(solution)/shard_map/ppermute | solution.py:490
  51.6 18.3 %collective-permute-start.22 = (bf16[1024,256]{1,0:T(8,128)(2,1)S(1)}, bf16[1024,256]{1,0:T(8,128)(2,1)S(1)}, u32[]{:S(2)}, u32[]{:S(2)}) collective-permute-start(bf16[1024,256]{1,0:T(8,128)(2,1)S(1)} %get-tuple-element.100.refs_2_), channel_id=1, source_target_pairs={{0,1},{1,0},{2,3},{3,2},{4,5},{5,4},{6,7},{7,6},{8,9},{9,8},{10,11... | collective-permute-start | bytes 1572872 | tf_op jit(solution)/shard_map/ppermute | solution.py:466
  58.0 8.4 %collective-permute-start.18 = (f32[768,128]{1,0:T(8,128)S(1)}, f32[768,128]{1,0:T(8,128)S(1)}, u32[]{:S(2)}, u32[]{:S(2)}) collective-permute-start(f32[768,128]{1,0:T(8,128)S(1)} %get-tuple-element.97), channel_id=1, source_target_pairs={{0,2},{1,3},{2,0},{3,1},{4,6},{5,7},{6,4},{7,5},{8,10},{9,11},{10,... | collective-permute-start | bytes 1179656 | tf_op jit(solution)/shard_map/ppermute | solution.py:510
  60.5 17.1 %collective-permute-start.21 = (bf16[1024,256]{1,0:T(8,128)(2,1)S(1)}, bf16[1024,256]{1,0:T(8,128)(2,1)S(1)}, u32[]{:S(2)}, u32[]{:S(2)}) collective-permute-start(bf16[1024,256]{1,0:T(8,128)(2,1)S(1)} %get-tuple-element.99.refs_2_), channel_id=1, source_target_pairs={{0,1},{1,0},{2,3},{3,2},{4,5},{5,4},{6,7},{7,6},{8,9},{9,8},{10,11... | collective-permute-start | bytes 1572872 | tf_op jit(solution)/shard_map/ppermute | solution.py:466
  61.9 24.1 %collective-permute-start.20 = (bf16[1024,256]{1,0:T(8,128)(2,1)S(1)}, bf16[1024,256]{1,0:T(8,128)(2,1)S(1)}, u32[]{:S(2)}, u32[]{:S(2)}) collective-permute-start(bf16[1024,256]{1,0:T(8,128)(2,1)S(1)} %get-tuple-element.98.refs_2_), channel_id=1, source_target_pairs={{0,1},{1,0},{2,3},{3,2},{4,5},{5,4},{6,7},{7,6},{8,9},{9,8},{10,11... | collective-permute-start | bytes 1572872 | tf_op jit(solution)/shard_map/ppermute | solution.py:466
  66.3 27.5 %collective-permute-start.19 = (f32[384,128]{1,0:T(8,128)S(1)}, f32[384,128]{1,0:T(8,128)S(1)}, u32[]{:S(2)}, u32[]{:S(2)}) collective-permute-start(f32[384,128]{1,0:T(8,128)S(1)} %add.37), channel_id=1, source_target_pairs={{0,4},{1,5},{2,6},{3,7},{4,0},{5,1},{6,2},{7,3},{8,12},{9,13},{10,... | collective-permute-start | bytes 589832 | tf_op jit(solution)/shard_map/ppermute | solution.py:512
  82.5 23.7 %copy-start.4 = (f32[512,256]{1,0:T(8,128)}, f32[512,256]{1,0:T(8,128)S(1)}, u32[]{:S(2)}) copy-start(f32[512,256]{1,0:T(8,128)S(1)} %get-tuple-element.108.keep_ref) | copy-start | bytes 1572868
  90.8 26.2 %copy-start.6 = (f32[512,256]{1,0:T(8,128)}, f32[512,256]{1,0:T(8,128)S(1)}, u32[]{:S(2)}) copy-start(f32[512,256]{1,0:T(8,128)S(1)} %get-tuple-element.106.keep_ref) | copy-start | bytes 1572868
  90.8 26.2 %collective-permute-start.26 = (bf16[512,256]{1,0:T(8,128)(2,1)S(1)}, bf16[512,256]{1,0:T(8,128)(2,1)S(1)}, u32[]{:S(2)}, u32[]{:S(2)}) collective-permute-start(bf16[512,256]{1,0:T(8,128)(2,1)S(1)} %get-tuple-element.107), channel_id=1, source_target_pairs={{0,2},{1,3},{2,0},{3,1},{4,6},{5,7},{6,4},{7,5},{8,10},{9,11},{10,... | collective-permute-start | bytes 786440 | tf_op jit(solution)/shard_map/ppermute | solution.py:510
  91.8 14.4 %collective-permute-start.28 = (bf16[512,256]{1,0:T(8,128)(2,1)S(1)}, bf16[512,256]{1,0:T(8,128)(2,1)S(1)}, u32[]{:S(2)}, u32[]{:S(2)}) collective-permute-start(bf16[512,256]{1,0:T(8,128)(2,1)S(1)} %get-tuple-element.109), channel_id=1, source_target_pairs={{0,2},{1,3},{2,0},{3,1},{4,6},{5,7},{6,4},{7,5},{8,10},{9,11},{10,... | collective-permute-start | bytes 786440 | tf_op jit(solution)/shard_map/ppermute | solution.py:510
  92.9 16.1 %collective-permute-start.30 = (bf16[512,256]{1,0:T(8,128)(2,1)S(1)}, bf16[512,256]{1,0:T(8,128)(2,1)S(1)}, u32[]{:S(2)}, u32[]{:S(2)}) collective-permute-start(bf16[512,256]{1,0:T(8,128)(2,1)S(1)} %get-tuple-element.111), channel_id=1, source_target_pairs={{0,2},{1,3},{2,0},{3,1},{4,6},{5,7},{6,4},{7,5},{8,10},{9,11},{10,... | collective-permute-start | bytes 786440 | tf_op jit(solution)/shard_map/ppermute | solution.py:510
  106.2 24.7 %collective-permute-start.29 = (bf16[256,256]{1,0:T(8,128)(2,1)S(1)}, bf16[256,256]{1,0:T(8,128)(2,1)S(1)}, u32[]{:S(2)}, u32[]{:S(2)}) collective-permute-start(bf16[256,256]{1,0:T(8,128)(2,1)S(1)} %add.39), channel_id=1, source_target_pairs={{0,4},{1,5},{2,6},{3,7},{4,0},{5,1},{6,2},{7,3},{8,12},{9,13},{10,... | collective-permute-start | bytes 393224 | tf_op jit(solution)/shard_map/ppermute | solution.py:512
  109.0 21.5 %collective-permute-start.31 = (bf16[256,256]{1,0:T(8,128)(2,1)S(1)}, bf16[256,256]{1,0:T(8,128)(2,1)S(1)}, u32[]{:S(2)}, u32[]{:S(2)}) collective-permute-start(bf16[256,256]{1,0:T(8,128)(2,1)S(1)} %add.40), channel_id=1, source_target_pairs={{0,4},{1,5},{2,6},{3,7},{4,0},{5,1},{6,2},{7,3},{8,12},{9,13},{10,... | collective-permute-start | bytes 393224 | tf_op jit(solution)/shard_map/ppermute | solution.py:512
  116.8 11.4 %copy-start = (f32[8,1536]{1,0:T(8,128)}, f32[8,1536]{1,0:T(8,128)S(1)}, u32[]{:S(2)}) copy-start(f32[8,1536]{1,0:T(8,128)S(1)} %get-tuple-element.104.refs_0_) | copy-start | bytes 147460
  116.8 5.4 %collective-permute-start.23 = (f32[8,1536]{1,0:T(8,128)S(1)}, f32[8,1536]{1,0:T(8,128)S(1)}, u32[]{:S(2)}, u32[]{:S(2)}) collective-permute-start(f32[8,1536]{1,0:T(8,128)S(1)} %get-tuple-element.104.refs_0_), channel_id=1, source_target_pairs={{0,2},{1,3},{2,0},{3,1},{4,6},{5,7},{6,4},{7,5},{8,10},{9,11},{10,... | collective-permute-start | bytes 147464 | tf_op jit(solution)/shard_map/ppermute | solution.py:518
  117.0 14.3 %collective-permute-start.27 = (bf16[256,256]{1,0:T(8,128)(2,1)S(1)}, bf16[256,256]{1,0:T(8,128)(2,1)S(1)}, u32[]{:S(2)}, u32[]{:S(2)}) collective-permute-start(bf16[256,256]{1,0:T(8,128)(2,1)S(1)} %add.38), channel_id=1, source_target_pairs={{0,4},{1,5},{2,6},{3,7},{4,0},{5,1},{6,2},{7,3},{8,12},{9,13},{10,... | collective-permute-start | bytes 393224 | tf_op jit(solution)/shard_map/ppermute | solution.py:512
  117.5 8.2 %collective-permute-start.24 = (f32[8,1536]{1,0:T(8,128)S(1)}, f32[8,1536]{1,0:T(8,128)S(1)}, u32[]{:S(2)}, u32[]{:S(2)}) collective-permute-start(f32[8,1536]{1,0:T(8,128)S(1)} %get-tuple-element.104.refs_0_), channel_id=1, source_target_pairs={{0,4},{1,5},{2,6},{3,7},{4,0},{5,1},{6,2},{7,3},{8,12},{9,13},{10,... | collective-permute-start | bytes 147464 | tf_op jit(solution)/shard_map/ppermute | solution.py:518
  122.2 6.0 %copy-start.13 = (f32[8,1536]{1,0:T(8,128)}, f32[8,1536]{1,0:T(8,128)S(1)}, u32[]{:S(2)}) copy-start(f32[8,1536]{1,0:T(8,128)S(1)} %collective-permute-done.23.refs_1_) | copy-start | bytes 147460
  122.2 6.0 %collective-permute-start.25 = (f32[8,1536]{1,0:T(8,128)S(1)}, f32[8,1536]{1,0:T(8,128)}, u32[]{:S(2)}, u32[]{:S(2)}) collective-permute-start(f32[8,1536]{1,0:T(8,128)S(1)} %get-tuple-element.104.refs_0_), channel_id=1, source_target_pairs={{0,6},{1,7},{2,4},{3,5},{4,2},{5,3},{6,0},{7,1},{8,14},{9,15},{10,... | collective-permute-start | bytes 147464 | tf_op jit(solution)/shard_map/ppermute | solution.py:518
  125.7 2.5 %copy-start.14 = (f32[8,1536]{1,0:T(8,128)}, f32[8,1536]{1,0:T(8,128)S(1)}, u32[]{:S(2)}) copy-start(f32[8,1536]{1,0:T(8,128)S(1)} %collective-permute-done.24.refs_2_) | copy-start | bytes 147460
  129.8 1.2 copy-start.5
  130.9 1.0 copy-start.7
  131.9 2.0 %copy-start.8 = (f32[512,256]{1,0:T(8,128)}, f32[512,256]{1,0:T(8,128)S(1)}, u32[]{:S(2)}) copy-start(f32[512,256]{1,0:T(8,128)S(1)} %get-tuple-element.35.keep_ref) | copy-start | bytes 1572868 | tf_op jit(solution)/shard_map/cond
  131.9 17.8 %collective-permute-start.4 = (f32[512,256]{1,0:T(8,128)}, f32[512,256]{1,0:T(8,128)S(1)}, u32[]{:S(2)}, u32[]{:S(2)}) collective-permute-start(f32[512,256]{1,0:T(8,128)} %get-tuple-element.40), channel_id=1, source_target_pairs={{0,2},{1,3},{2,0},{3,1},{4,6},{5,7},{6,4},{7,5},{8,10},{9,11},{10,... | collective-permute-start | bytes 1572872 | tf_op jit(solution)/shard_map/cond/branch_1_fun/ppermute | solution.py:528
  131.9 34.0 %collective-permute-start.2 = (f32[512,256]{1,0:T(8,128)}, f32[512,256]{1,0:T(8,128)S(1)}, u32[]{:S(2)}, u32[]{:S(2)}) collective-permute-start(f32[512,256]{1,0:T(8,128)} %get-tuple-element.38), channel_id=1, source_target_pairs={{0,2},{1,3},{2,0},{3,1},{4,6},{5,7},{6,4},{7,5},{8,10},{9,11},{10,... | collective-permute-start | bytes 1572872 | tf_op jit(solution)/shard_map/cond/branch_1_fun/ppermute | solution.py:528
  134.0 37.7 %copy-start.9 = (f32[512,256]{1,0:T(8,128)S(1)}, f32[512,256]{1,0:T(8,128)}, u32[]{:S(2)}) copy-start(f32[512,256]{1,0:T(8,128)} %copy-done.8) | copy-start | bytes 1572868 | tf_op jit(solution)/shard_map/cond
  134.0 37.7 %collective-permute-start = (f32[512,256]{1,0:T(8,128)}, f32[512,256]{1,0:T(8,128)S(1)}, u32[]{:S(2)}, u32[]{:S(2)}) collective-permute-start(f32[512,256]{1,0:T(8,128)} %get-tuple-element.36), channel_id=1, source_target_pairs={{0,2},{1,3},{2,0},{3,1},{4,6},{5,7},{6,4},{7,5},{8,10},{9,11},{10,... | collective-permute-start | bytes 1572872 | tf_op jit(solution)/shard_map/cond/branch_1_fun/ppermute | solution.py:528
  149.8 24.3 %collective-permute-start.5 = (f32[256,256]{1,0:T(8,128)S(1)}, f32[256,256]{1,0:T(8,128)S(1)}, u32[]{:S(2)}, u32[]{:S(2)}) collective-permute-start(f32[256,256]{1,0:T(8,128)S(1)} %add.36), channel_id=1, source_target_pairs={{0,4},{1,5},{2,6},{3,7},{4,0},{5,1},{6,2},{7,3},{8,12},{9,13},{10,... | collective-permute-start | bytes 786440 | tf_op jit(solution)/shard_map/cond/branch_1_fun/ppermute | solution.py:529
  166.0 22.4 %collective-permute-start.3 = (f32[256,256]{1,0:T(8,128)S(1)}, f32[256,256]{1,0:T(8,128)S(1)}, u32[]{:S(2)}, u32[]{:S(2)}) collective-permute-start(f32[256,256]{1,0:T(8,128)S(1)} %add.35), channel_id=1, source_target_pairs={{0,4},{1,5},{2,6},{3,7},{4,0},{5,1},{6,2},{7,3},{8,12},{9,13},{10,... | collective-permute-start | bytes 786440 | tf_op jit(solution)/shard_map/cond/branch_1_fun/ppermute | solution.py:529
  171.7 19.6 %collective-permute-start.1 = (f32[256,256]{1,0:T(8,128)S(1)}, f32[256,256]{1,0:T(8,128)S(1)}, u32[]{:S(2)}, u32[]{:S(2)}) collective-permute-start(f32[256,256]{1,0:T(8,128)S(1)} %add.34), channel_id=1, source_target_pairs={{0,4},{1,5},{2,6},{3,7},{4,0},{5,1},{6,2},{7,3},{8,12},{9,13},{10,... | collective-permute-start | bytes 786440 | tf_op jit(solution)/shard_map/cond/branch_1_fun/ppermute | solution.py:529
  191.7 1.0 copy-start.3

commit v2 on v1

--- a/solution.py
+++ b/solution.py
@@ -205,11 +205,12 @@
             before_ref, rounded_ref, squares_ref = outs[0], outs[3], outs[4]
             keep_ref[...] = acc[:middle, :]
             send_ref[...] = acc[middle:, :]
-            rounded_ref[...] = acc[middle:, :].astype(BF16)
-            squares = (acc[...] * acc[...]).astype(BF16)
-            ones = jnp.ones((8, squares.shape[1]), BF16)
-            squares_ref[...] = before_ref[...] + lax.dot_general(
-                ones, squares, (((1,), (1,)), ((), ())), preferred_element_type=F32
+            rounded = acc[PANEL:, :].astype(BF16)
+            rounded_ref[...] = rounded[middle - PANEL :, :]
+            ones = jnp.ones((8, rounded.shape[1]), BF16)
+            squares_ref[:, :PANEL] = before_ref[:, :PANEL]
+            squares_ref[:, PANEL:] = before_ref[:, PANEL:] + lax.dot_general(
+                ones, rounded * rounded, (((1,), (1,)), ((), ())), preferred_element_type=F32
             )
 
 
@@ -406,17 +407,22 @@
 
 
 def judge_kernel(scale, *refs):
-    *guards, out_ref = refs
+    *guard_refs, out_ref, guards, sems = refs
+    copies = [pltpu.make_async_copy(ref, guards.at[k], sems.at[k]) for k, ref in enumerate(guard_refs)]
+    for copy in copies:
+        copy.start()
+    for copy in copies:
+        copy.wait()
     worst = jnp.zeros((8, 1), F32)
     for owner in range(NZ):
         terms = []
         for sender in range(NZ):
             apart = owner ^ sender
             place = relative_owner(apart) * PANEL
-            terms.append(guards[sender][:, place : place + PANEL] * float(apart))
+            terms.append(guards[sender, :, place : place + PANEL] * float(apart))
         total = (terms[0] + terms[1]) + (terms[2] + terms[3])
-        inverse_norms = guards[owner][:, NZ * PANEL : (NZ + 1) * PANEL]
-        upper_norms = guards[owner][:, (NZ + 1) * PANEL :]
+        inverse_norms = guards[owner, :, NZ * PANEL : (NZ + 1) * PANEL]
+        upper_norms = guards[owner, :, (NZ + 1) * PANEL :]
         error = jnp.sum(inverse_norms * total, axis=1, keepdims=True) * (ROUNDING * scale) ** 2
         size = jnp.sum(upper_norms, axis=1, keepdims=True) * LIMIT**2
         worst = jnp.maximum(worst, jnp.where(error <= size, 0.0, 1.0))
@@ -424,13 +430,12 @@
 
 
 def judge(guards, scale):
-    spec = pl.BlockSpec(guards[0].shape, lambda i: (0, 0))
     return pl.pallas_call(
         functools.partial(judge_kernel, scale),
-        grid=(1,),
-        in_specs=[spec] * NZ,
+        in_specs=[pl.BlockSpec(memory_space=pltpu.HBM)] * NZ,
         out_specs=pl.BlockSpec(memory_space=pltpu.SMEM),
         out_shape=jax.ShapeDtypeStruct((1,), jnp.int32),
+        scratch_shapes=[pltpu.VMEM((NZ,) + guards[0].shape, F32), pltpu.SemaphoreType.DMA((NZ,))],
         name="judge",
     )(*guards)
 

time: 193 us -> 193 us (level)
  no operation moved by 1% of the time
where the time goes in v2:
time: 193 us
  waiting for transfers between devices  102 us (53%)
  Pallas kernels  47.2 us (24%)
  starting transfers between devices  37.6 us (19%)
  other arithmetic  2.92 us (2%)
    ppermute x3, waiting for transfers between devices, exact(): near = lax.ppermute(send, 'blk', z_route(1))  37.4 us
    ppermute x5, waiting for transfers between devices, last_level(): lax.ppermute(own, 'wide', [(w, w ^ wide // 2) for w in range(wide)])  20.3 us
    pallas_call x4, Pallas kernels, partial_grams(): pl.pallas_call(functools.partial(gram_kernel, parts, packed, each), grid=...  18 us
    ppermute x3, waiting for transfers between devices, exact(): far = lax.ppermute(far_sum(keep, near), 'blk', z_route(2))  16.5 us
    ppermute x4, waiting for transfers between devices, per_device(): near = lax.ppermute(send, 'blk', z_route(1))  11.5 us
    ppermute x4, starting transfers between devices, per_device(): far = lax.ppermute(onward, 'blk', z_route(2))  8.99 us
    pallas_call x2, Pallas kernels, mix_columns(): pl.pallas_call(mix_kernel, grid=(count,), in_specs=[pl.BlockSpec((1, rows...  7.66 us
    ppermute x5, starting transfers between devices, last_level(): lax.ppermute(own, 'wide', [(w, w ^ wide // 2) for w in range(wide)])  7.28 us
  transfers between devices with their start and end apart: 32, of which 15 were waited for; matrix products, arithmetic and copies ran while one was open for 2% of the time, Pallas kernels for 22%

profile of v2, /device:TPU:0, one launch (start us, length us, event | category | flops | bytes accessed | tf_op | source)
XLA Modules:
  0.0 192.7 jit_solution(2548121751852358568)
XLA Ops:
  0.6 4.9 %mix.2 = (bf16[1024,256]{1,0:T(8,128)(2,1)}, bf16[1024,256]{1,0:T(8,128)(2,1)}, bf16[1024,256]{1,0:T(8,128)(2,1)}) custom-call(s32[1,1024]{1,0:T(1,128)} %bitcast.9, bf16[256,256]{1,0:T(8,128)(2,1)} %constant.25.clone.had_ref, f32[1024,1024]{1,0:T(8,128)} %x_ref.3), custom_call_target="tpu_custom_call" | custom-call | flops 1207959552 | bytes 4718592 | tf_op jit(solution)/shard_map/mix/pallas_call | solution.py:67
  6.1 2.8 %mix.3 = bf16[1024,256]{1,0:T(8,128)(2,1)} custom-call(s32[1,1024]{1,0:T(1,128)} %bitcast.10, bf16[256,256]{1,0:T(8,128)(2,1)} %constant.25.clone.had_ref, f32[1024,1024]{1,0:T(8,128)} %x_ref.3), custom_call_target="tpu_custom_call" | custom-call | flops 402653184 | bytes 1572864 | tf_op jit(solution)/shard_map/mix/pallas_call | solution.py:67
  9.5 1.2 multiply_convert_fusion.own_ref
  10.7 3.0 %collective-permute-start.11 = (bf16[1024,256]{1,0:T(8,128)(2,1)S(1)}, bf16[1024,256]{1,0:T(8,128)(2,1)S(1)}, u32[]{:S(2)}, u32[]{:S(2)}) collective-permute-start(bf16[1024,256]{1,0:T(8,128)(2,1)S(1)} %multiply_convert_fusion.own_ref), channel_id=1, source_target_pairs={{0,16},{8,24},{16,0},{24,8},{1,17},{9,25},{17,1},{25,9},{2,18},{10... | collective-permute-start | bytes 1572872 | tf_op jit(solution)/shard_map/ppermute | solution.py:467
  13.7 1.2 multiply_convert_fusion.3
  15.0 2.0 %collective-permute-start.14 = (bf16[1024,128]{1,0:T(8,128)(2,1)S(1)}, bf16[1024,128]{1,0:T(8,128)(2,1)S(1)}, u32[]{:S(2)}, u32[]{:S(2)}) collective-permute-start(bf16[1024,128]{1,0:T(8,128)(2,1)S(1)} %get-tuple-element.116.own_ref), channel_id=1, source_target_pairs={{0,16},{8,24},{16,0},{24,8},{1,17},{9,25},{17,1},{25,9},{2,18},{10... | collective-permute-start | bytes 786440 | tf_op jit(solution)/shard_map/ppermute | solution.py:467
  17.4 20.3 %collective-permute-done.14.other_ref = bf16[1024,128]{1,0:T(8,128)(2,1)S(1)} collective-permute-done((bf16[1024,128]{1,0:T(8,128)(2,1)S(1)}, bf16[1024,128]{1,0:T(8,128)(2,1)S(1)}, u32[]{:S(2)}, u32[]{:S(2)}) %collective-permute-start.14) | collective-permute-done | bytes 262176 | tf_op jit(solution)/shard_map/ppermute | solution.py:467
  38.5 2.0 %collective-permute-start.16 = (bf16[1024,128]{1,0:T(8,128)(2,1)S(1)}, bf16[1024,128]{1,0:T(8,128)(2,1)S(1)}, u32[]{:S(2)}, u32[]{:S(2)}) collective-permute-start(bf16[1024,128]{1,0:T(8,128)(2,1)S(1)} %get-tuple-element.89.left_ref.refs_2_), channel_id=1, source_target_pairs={{0,1},{1,0},{2,3},{3,2},{4,5},{5,4},{6,7},{7,6},{8,9},{9,8},{10,11... | collective-permute-start | bytes 786440 | tf_op jit(solution)/shard_map/ppermute | solution.py:471
  41.5 2.1 %collective-permute-start.7 = (bf16[1024,256]{1,0:T(8,128)(2,1)S(1)}, bf16[1024,256]{1,0:T(8,128)(2,1)S(1)}, u32[]{:S(2)}, u32[]{:S(2)}) collective-permute-start(bf16[1024,256]{1,0:T(8,128)(2,1)S(1)} %multiply_convert_fusion.2.own_ref), channel_id=1, source_target_pairs={{0,16},{8,24},{16,0},{24,8},{1,17},{9,25},{17,1},{25,9},{2,18},{10... | collective-permute-start | bytes 1572872 | tf_op jit(solution)/shard_map/ppermute | solution.py:467
  43.7 1.7 counts.1
  45.4 1.5 collective-permute-start.15
  46.9 1.1 weigh.2
  48.0 0.9 join.7
  49.0 2.6 %collective-permute-done.15.counts_ref = f32[4,1024]{1,0:T(4,128)S(1)} collective-permute-done((f32[4,1024]{1,0:T(4,128)S(1)}, f32[4,1024]{1,0:T(4,128)S(1)}, u32[]{:S(2)}, u32[]{:S(2)}) %collective-permute-start.15) | collective-permute-done | bytes 16416 | tf_op jit(solution)/shard_map/ppermute | solution.py:495
  51.6 1.4 collective-permute-start.22
  53.0 1.1 weigh.3
  54.2 3.8 %grams.4 = (f32[768,128]{1,0:T(8,128)S(1)}, f32[768,128]{1,0:T(8,128)S(1)}) custom-call(bf16[1024,1024]{1,0:T(8,128)(2,1)S(1)} %get-tuple-element.91.refs_0_, bf16[1024,1024]{1,0:T(8,128)(2,1)S(1)} %get-tuple-element.92.refs_1_, bf16[1024,128]{1,0:T(8,128)(2,1)S(1)} %get-tuple-element.89.left_ref.refs_2_, ...), custom_call_target="tpu_custom_call" | custom-call | flops 2147483648 | bytes 9437184 | tf_op jit(solution)/shard_map/grams/pallas_call | solution.py:245
  58.0 1.6 collective-permute-start.18
  61.9 1.5 collective-permute-start.20
  63.5 2.9 %collective-permute-done.18.near_ref = f32[768,128]{1,0:T(8,128)S(1)} collective-permute-done((f32[768,128]{1,0:T(8,128)S(1)}, f32[768,128]{1,0:T(8,128)S(1)}, u32[]{:S(2)}, u32[]{:S(2)}) %collective-permute-start.18) | collective-permute-done | bytes 393248 | tf_op jit(solution)/shard_map/ppermute | solution.py:515
  66.3 3.6 %collective-permute-start.19 = (f32[384,128]{1,0:T(8,128)S(1)}, f32[384,128]{1,0:T(8,128)S(1)}, u32[]{:S(2)}, u32[]{:S(2)}) collective-permute-start(f32[384,128]{1,0:T(8,128)S(1)} %add.37), channel_id=1, source_target_pairs={{0,4},{1,5},{2,6},{3,7},{4,0},{5,1},{6,2},{7,3},{8,12},{9,13},{10,... | collective-permute-start | bytes 589832 | tf_op jit(solution)/shard_map/ppermute | solution.py:517
  69.9 4.7 %grams.5 = (f32[512,256]{1,0:T(8,128)S(1)}, f32[512,256]{1,0:T(8,128)}, bf16[512,256]{1,0:T(8,128)(2,1)S(1)}, f32[8,1024]{1,0:T(8,128)S(1)}) custom-call(bf16[1024,1024]{1,0:T(8,128)(2,1)S(1)} %get-tuple-element.91.refs_0_, bf16[1024,1024]{1,0:T(8,128)(2,1)S(1)} %get-tuple-element.92.refs_1_, bf16[1024,256]{1,0:T(8,128)(2,1)S(1)} %get-tuple-element.100.refs_2_, ...), custom_call_target="tpu_custom_call" | custom-call | flops 2147483648 | bytes 9437184 | tf_op jit(solution)/shard_map/grams/pallas_call | solution.py:245
  74.7 3.0 %collective-permute-done.21.refs_5_ = bf16[1024,256]{1,0:T(8,128)(2,1)S(1)} collective-permute-done((bf16[1024,256]{1,0:T(8,128)(2,1)S(1)}, bf16[1024,256]{1,0:T(8,128)(2,1)S(1)}, u32[]{:S(2)}, u32[]{:S(2)}) %collective-permute-start.21) | collective-permute-done | bytes 524320 | tf_op jit(solution)/shard_map/ppermute | solution.py:471
  77.6 4.8 %grams.6 = (f32[512,256]{1,0:T(8,128)S(1)}, f32[512,256]{1,0:T(8,128)}, bf16[512,256]{1,0:T(8,128)(2,1)S(1)}, f32[8,1024]{1,0:T(8,128)S(1)}) custom-call(bf16[1024,1024]{1,0:T(8,128)(2,1)S(1)} %get-tuple-element.91.refs_0_, bf16[1024,1024]{1,0:T(8,128)(2,1)S(1)} %get-tuple-element.92.refs_1_, bf16[1024,256]{1,0:T(8,128)(2,1)S(1)} %get-tuple-element.99.refs_2_, ...), custom_call_target="tpu_custom_call" | custom-call | flops 2147483648 | bytes 9437184 | tf_op jit(solution)/shard_map/grams/pallas_call | solution.py:245
  82.4 3.6 %collective-permute-done.20.refs_5_ = bf16[1024,256]{1,0:T(8,128)(2,1)S(1)} collective-permute-done((bf16[1024,256]{1,0:T(8,128)(2,1)S(1)}, bf16[1024,256]{1,0:T(8,128)(2,1)S(1)}, u32[]{:S(2)}, u32[]{:S(2)}) %collective-permute-start.20) | collective-permute-done | bytes 524320 | tf_op jit(solution)/shard_map/ppermute | solution.py:471
  86.0 4.8 %grams.7 = (f32[512,256]{1,0:T(8,128)S(1)}, f32[512,256]{1,0:T(8,128)}, bf16[512,256]{1,0:T(8,128)(2,1)S(1)}, f32[8,1024]{1,0:T(8,128)S(1)}) custom-call(bf16[1024,1024]{1,0:T(8,128)(2,1)S(1)} %get-tuple-element.91.refs_0_, bf16[1024,1024]{1,0:T(8,128)(2,1)S(1)} %get-tuple-element.92.refs_1_, bf16[1024,256]{1,0:T(8,128)(2,1)S(1)} %get-tuple-element.98.refs_2_, ...), custom_call_target="tpu_custom_call" | custom-call | flops 2147483648 | bytes 9437184 | tf_op jit(solution)/shard_map/grams/pallas_call | solution.py:245
  91.7 1.1 collective-permute-start.28
  93.7 5.0 %factor_first.1.in_ref = f32[256,512]{1,0:T(8,128)S(1)} custom-call(f32[768,128]{1,0:T(8,128)S(1)} %get-tuple-element.96.keep_ref, f32[768,128]{1,0:T(8,128)S(1)} %collective-permute-done.18.near_ref, f32[384,128]{1,0:T(8,128)S(1)} %collective-permute-done.19.far_ref), custom_call_target="tpu_custom_call" | custom-call | flops 10000000000 | bytes 1048576 | tf_op jit(solution)/shard_map/factor_first/pallas_call | solution.py:348
  98.7 7.4 %collective-permute-done.28.near_ref = bf16[512,256]{1,0:T(8,128)(2,1)S(1)} collective-permute-done((bf16[512,256]{1,0:T(8,128)(2,1)S(1)}, bf16[512,256]{1,0:T(8,128)(2,1)S(1)}, u32[]{:S(2)}, u32[]{:S(2)}) %collective-permute-start.28) | collective-permute-done | bytes 262176 | tf_op jit(solution)/shard_map/ppermute | solution.py:515
  106.1 1.5 collective-permute-start.29
  107.6 1.3 collective-permute-done.30.near_ref
  108.9 3.4 %collective-permute-start.31 = (bf16[256,256]{1,0:T(8,128)(2,1)S(1)}, bf16[256,256]{1,0:T(8,128)(2,1)S(1)}, u32[]{:S(2)}, u32[]{:S(2)}) collective-permute-start(bf16[256,256]{1,0:T(8,128)(2,1)S(1)} %add.40), channel_id=1, source_target_pairs={{0,4},{1,5},{2,6},{3,7},{4,0},{5,1},{6,2},{7,3},{8,12},{9,13},{10,... | collective-permute-start | bytes 393224 | tf_op jit(solution)/shard_map/ppermute | solution.py:517
  112.3 4.4 %factor_last.1 = (f32[256,1024]{1,0:T(8,128)S(1)}, f32[256,256]{1,0:T(8,128)S(1)}, f32[8,1536]{1,0:T(8,128)S(1)}) custom-call(f32[256,512]{1,0:T(8,128)S(1)} %factor_first.1.in_ref, f32[8,1024]{1,0:T(8,128)S(1)} %get-tuple-element.103.squares_ref), custom_call_target="tpu_custom_call" | custom-call | flops 10000000000 | bytes 1048576 | tf_op jit(solution)/shard_map/factor_last/pallas_call | solution.py:366
  117.5 2.5 %collective-permute-start.24 = (f32[8,1536]{1,0:T(8,128)S(1)}, f32[8,1536]{1,0:T(8,128)S(1)}, u32[]{:S(2)}, u32[]{:S(2)}) collective-permute-start(f32[8,1536]{1,0:T(8,128)S(1)} %get-tuple-element.104.refs_0_), channel_id=1, source_target_pairs={{0,4},{1,5},{2,6},{3,7},{4,0},{5,1},{6,2},{7,3},{8,12},{9,13},{10,... | collective-permute-start | bytes 147464 | tf_op jit(solution)/shard_map/ppermute | solution.py:523
  120.0 2.2 %collective-permute-done.23.refs_1_ = f32[8,1536]{1,0:T(8,128)S(1)} collective-permute-done((f32[8,1536]{1,0:T(8,128)S(1)}, f32[8,1536]{1,0:T(8,128)S(1)}, u32[]{:S(2)}, u32[]{:S(2)}) %collective-permute-start.23) | collective-permute-done | bytes 49184 | tf_op jit(solution)/shard_map/ppermute | solution.py:523
  122.2 1.2 collective-permute-start.25
  123.4 2.3 %collective-permute-done.24.refs_2_ = f32[8,1536]{1,0:T(8,128)S(1)} collective-permute-done((f32[8,1536]{1,0:T(8,128)S(1)}, f32[8,1536]{1,0:T(8,128)S(1)}, u32[]{:S(2)}, u32[]{:S(2)}) %collective-permute-start.24) | collective-permute-done | bytes 49184 | tf_op jit(solution)/shard_map/ppermute | solution.py:523
  125.7 2.5 %collective-permute-done.25.refs_3_ = f32[8,1536]{1,0:T(8,128)} collective-permute-done((f32[8,1536]{1,0:T(8,128)S(1)}, f32[8,1536]{1,0:T(8,128)}, u32[]{:S(2)}, u32[]{:S(2)}) %collective-permute-start.25) | collective-permute-done | bytes 49184 | tf_op jit(solution)/shard_map/ppermute | solution.py:523
  128.2 1.6 judge.1
  131.9 59.8 %conditional.1 = (f32[256,1024]{1,0:T(8,128)S(1)}) conditional(s32[]{:T(128)} %bitcast.6, (f32[256,256]{1,0:T(8,128)S(1)}, f32[512,256]{1,0:T(8,128)S(1)}, bf16[512,256]{1,0:T(8,128)(2,1)S(1)}, bf16[256,256]{1,0:T(8,128)(2,1)S(1)}, f32[256,1024]{1,0:T(8,128)S(1)}) %tuple.21, (f32[512,256]{1,0:T(8,128)}, f32[512,256]{1,0:T(8,128)S(1)}, ...), branch_computations={%region_0.1_spmd, %region_1.2_spmd} | conditional | flops 604176384 | bytes 19923248 | solution.py:538
  131.9 2.0 %collective-permute-start.2 = (f32[512,256]{1,0:T(8,128)}, f32[512,256]{1,0:T(8,128)S(1)}, u32[]{:S(2)}, u32[]{:S(2)}) collective-permute-start(f32[512,256]{1,0:T(8,128)} %get-tuple-element.38), channel_id=1, source_target_pairs={{0,2},{1,3},{2,0},{3,1},{4,6},{5,7},{6,4},{7,5},{8,10},{9,11},{10,... | collective-permute-start | bytes 1572872 | tf_op jit(solution)/shard_map/cond/branch_1_fun/ppermute | solution.py:533
  134.0 15.7 %collective-permute-done.4.near_ref = f32[512,256]{1,0:T(8,128)S(1)} collective-permute-done((f32[512,256]{1,0:T(8,128)}, f32[512,256]{1,0:T(8,128)S(1)}, u32[]{:S(2)}, u32[]{:S(2)}) %collective-permute-start.4) | collective-permute-done | bytes 524320 | tf_op jit(solution)/shard_map/cond/branch_1_fun/ppermute | solution.py:533
  149.9 16.1 %collective-permute-done.2.near_ref = f32[512,256]{1,0:T(8,128)S(1)} collective-permute-done((f32[512,256]{1,0:T(8,128)}, f32[512,256]{1,0:T(8,128)S(1)}, u32[]{:S(2)}, u32[]{:S(2)}) %collective-permute-start.2) | collective-permute-done | bytes 524320 | tf_op jit(solution)/shard_map/cond/branch_1_fun/ppermute | solution.py:533
  166.1 5.5 %collective-permute-done.near_ref = f32[512,256]{1,0:T(8,128)S(1)} collective-permute-done((f32[512,256]{1,0:T(8,128)}, f32[512,256]{1,0:T(8,128)S(1)}, u32[]{:S(2)}, u32[]{:S(2)}) %collective-permute-start) | collective-permute-done | bytes 524320 | tf_op jit(solution)/shard_map/cond/branch_1_fun/ppermute | solution.py:533
  171.7 2.4 %collective-permute-start.1 = (f32[256,256]{1,0:T(8,128)S(1)}, f32[256,256]{1,0:T(8,128)S(1)}, u32[]{:S(2)}, u32[]{:S(2)}) collective-permute-start(f32[256,256]{1,0:T(8,128)S(1)} %add.34), channel_id=1, source_target_pairs={{0,4},{1,5},{2,6},{3,7},{4,0},{5,1},{6,2},{7,3},{8,12},{9,13},{10,... | collective-permute-start | bytes 786440 | tf_op jit(solution)/shard_map/cond/branch_1_fun/ppermute | solution.py:534
  174.5 14.0 %collective-permute-done.3.far_ref = f32[256,256]{1,0:T(8,128)S(1)} collective-permute-done((f32[256,256]{1,0:T(8,128)S(1)}, f32[256,256]{1,0:T(8,128)S(1)}, u32[]{:S(2)}, u32[]{:S(2)}) %collective-permute-start.3) | collective-permute-done | bytes 262176 | tf_op jit(solution)/shard_map/cond/branch_1_fun/ppermute | solution.py:534
  188.8 2.5 %collective-permute-done.1.far_ref = f32[256,256]{1,0:T(8,128)S(1)} collective-permute-done((f32[256,256]{1,0:T(8,128)S(1)}, f32[256,256]{1,0:T(8,128)S(1)}, u32[]{:S(2)}, u32[]{:S(2)}) %collective-permute-start.1) | collective-permute-done | bytes 262176 | tf_op jit(solution)/shard_map/cond/branch_1_fun/ppermute | solution.py:534
  191.8 1.0 copy-done.3
  (82 shorter events, 11.5 us)
Async XLA Ops:
  5.5 3.4 %copy-start.11 = (bf16[1024,256]{1,0:T(8,128)(2,1)S(1)}, bf16[1024,256]{1,0:T(8,128)(2,1)}, u32[]{:S(2)}) copy-start(bf16[1024,256]{1,0:T(8,128)(2,1)} %get-tuple-element.81) | copy-start | bytes 1572868
  5.5 3.8 %copy-start.10 = (bf16[1024,256]{1,0:T(8,128)(2,1)S(1)}, bf16[1024,256]{1,0:T(8,128)(2,1)}, u32[]{:S(2)}) copy-start(bf16[1024,256]{1,0:T(8,128)(2,1)} %get-tuple-element.80) | copy-start | bytes 1572868
  5.5 3.9 %copy-start.12 = (bf16[1024,256]{1,0:T(8,128)(2,1)S(1)}, bf16[1024,256]{1,0:T(8,128)(2,1)}, u32[]{:S(2)}) copy-start(bf16[1024,256]{1,0:T(8,128)(2,1)} %get-tuple-element.82) | copy-start | bytes 1572868
  5.5 3.9 %collective-permute-start.10 = (bf16[1024,256]{1,0:T(8,128)(2,1)}, bf16[1024,256]{1,0:T(8,128)(2,1)}, u32[]{:S(2)}, u32[]{:S(2)}) collective-permute-start(bf16[1024,256]{1,0:T(8,128)(2,1)} %get-tuple-element.82), channel_id=1, source_target_pairs={{0,8},{8,0},{16,24},{24,16},{1,9},{9,1},{17,25},{25,17},{2,10},{10... | collective-permute-start | bytes 1572872 | tf_op jit(solution)/shard_map/ppermute | solution.py:480
  8.8 4.8 %collective-permute-start.12 = (bf16[1024,256]{1,0:T(8,128)(2,1)}, bf16[1024,256]{1,0:T(8,128)(2,1)S(1)}, u32[]{:S(2)}, u32[]{:S(2)}) collective-permute-start(bf16[1024,256]{1,0:T(8,128)(2,1)} %mix.3), channel_id=1, source_target_pairs={{0,8},{8,0},{16,24},{24,16},{1,9},{9,1},{17,25},{25,17},{2,10},{10... | collective-permute-start | bytes 1572872 | tf_op jit(solution)/shard_map/ppermute | solution.py:486
  9.0 8.0 %collective-permute-start.8 = (bf16[1024,256]{1,0:T(8,128)(2,1)S(1)}, bf16[1024,256]{1,0:T(8,128)(2,1)S(1)}, u32[]{:S(2)}, u32[]{:S(2)}) collective-permute-start(bf16[1024,256]{1,0:T(8,128)(2,1)S(1)} %copy-done.11), channel_id=1, source_target_pairs={{0,8},{8,0},{16,24},{24,16},{1,9},{9,1},{17,25},{25,17},{2,10},{10... | collective-permute-start | bytes 1572872 | tf_op jit(solution)/shard_map/ppermute | solution.py:480
  9.4 31.9 %collective-permute-start.6 = (bf16[1024,256]{1,0:T(8,128)(2,1)S(1)}, bf16[1024,256]{1,0:T(8,128)(2,1)S(1)}, u32[]{:S(2)}, u32[]{:S(2)}) collective-permute-start(bf16[1024,256]{1,0:T(8,128)(2,1)S(1)} %copy-done.10), channel_id=1, source_target_pairs={{0,8},{8,0},{16,24},{24,16},{1,9},{9,1},{17,25},{25,17},{2,10},{10... | collective-permute-start | bytes 1572872 | tf_op jit(solution)/shard_map/ppermute | solution.py:480
  10.7 34.7 %collective-permute-start.11 = (bf16[1024,256]{1,0:T(8,128)(2,1)S(1)}, bf16[1024,256]{1,0:T(8,128)(2,1)S(1)}, u32[]{:S(2)}, u32[]{:S(2)}) collective-permute-start(bf16[1024,256]{1,0:T(8,128)(2,1)S(1)} %multiply_convert_fusion.own_ref), channel_id=1, source_target_pairs={{0,16},{8,24},{16,0},{24,8},{1,17},{9,25},{17,1},{25,9},{2,18},{10... | collective-permute-start | bytes 1572872 | tf_op jit(solution)/shard_map/ppermute | solution.py:467
  14.9 25.5 %collective-permute-start.13 = (bf16[1024,128]{1,0:T(8,128)(2,1)S(1)}, bf16[1024,128]{1,0:T(8,128)(2,1)S(1)}, u32[]{:S(2)}, u32[]{:S(2)}) collective-permute-start(bf16[1024,128]{1,0:T(8,128)(2,1)S(1)} %get-tuple-element.117.own_ref), channel_id=1, source_target_pairs={{0,16},{8,24},{16,0},{24,8},{1,17},{9,25},{17,1},{25,9},{2,18},{10... | collective-permute-start | bytes 786440 | tf_op jit(solution)/shard_map/ppermute | solution.py:467
  15.0 22.7 %collective-permute-start.14 = (bf16[1024,128]{1,0:T(8,128)(2,1)S(1)}, bf16[1024,128]{1,0:T(8,128)(2,1)S(1)}, u32[]{:S(2)}, u32[]{:S(2)}) collective-permute-start(bf16[1024,128]{1,0:T(8,128)(2,1)S(1)} %get-tuple-element.116.own_ref), channel_id=1, source_target_pairs={{0,16},{8,24},{16,0},{24,8},{1,17},{9,25},{17,1},{25,9},{2,18},{10... | collective-permute-start | bytes 786440 | tf_op jit(solution)/shard_map/ppermute | solution.py:467
  17.2 42.4 %collective-permute-start.9 = (bf16[1024,256]{1,0:T(8,128)(2,1)S(1)}, bf16[1024,256]{1,0:T(8,128)(2,1)S(1)}, u32[]{:S(2)}, u32[]{:S(2)}) collective-permute-start(bf16[1024,256]{1,0:T(8,128)(2,1)S(1)} %multiply_convert_fusion.1.own_ref), channel_id=1, source_target_pairs={{0,16},{8,24},{16,0},{24,8},{1,17},{9,25},{17,1},{25,9},{2,18},{10... | collective-permute-start | bytes 1572872 | tf_op jit(solution)/shard_map/ppermute | solution.py:467
  38.5 14.6 %collective-permute-start.16 = (bf16[1024,128]{1,0:T(8,128)(2,1)S(1)}, bf16[1024,128]{1,0:T(8,128)(2,1)S(1)}, u32[]{:S(2)}, u32[]{:S(2)}) collective-permute-start(bf16[1024,128]{1,0:T(8,128)(2,1)S(1)} %get-tuple-element.89.left_ref.refs_2_), channel_id=1, source_target_pairs={{0,1},{1,0},{2,3},{3,2},{4,5},{5,4},{6,7},{7,6},{8,9},{9,8},{10,11... | collective-permute-start | bytes 786440 | tf_op jit(solution)/shard_map/ppermute | solution.py:471
  40.5 3.2 %copy-start.1 = (s32[2048]{0:T(1024)S(1)}, s32[2048]{0:T(1024)}, u32[]{:S(2)}) copy-start(s32[2048]{0:T(1024)} %param.9) | copy-start | bytes 24580
  40.5 3.2 %copy-start.2 = (s32[2048,1]{0,1:T(1,128)S(1)}, s32[2048,1]{0,1:T(1,128)}, u32[]{:S(2)}) copy-start(s32[2048,1]{0,1:T(1,128)} %param.10) | copy-start | bytes 24580
  41.3 11.8 %collective-permute-start.17 = (bf16[1024,128]{1,0:T(8,128)(2,1)S(1)}, bf16[1024,128]{1,0:T(8,128)(2,1)S(1)}, u32[]{:S(2)}, u32[]{:S(2)}) collective-permute-start(bf16[1024,128]{1,0:T(8,128)(2,1)S(1)} %get-tuple-element.90.right_ref.refs_3_), channel_id=1, source_target_pairs={{0,1},{1,0},{2,3},{3,2},{4,5},{5,4},{6,7},{7,6},{8,9},{9,8},{10,11... | collective-permute-start | bytes 786440 | tf_op jit(solution)/shard_map/ppermute | solution.py:471
  41.5 19.5 %collective-permute-start.7 = (bf16[1024,256]{1,0:T(8,128)(2,1)S(1)}, bf16[1024,256]{1,0:T(8,128)(2,1)S(1)}, u32[]{:S(2)}, u32[]{:S(2)}) collective-permute-start(bf16[1024,256]{1,0:T(8,128)(2,1)S(1)} %multiply_convert_fusion.2.own_ref), channel_id=1, source_target_pairs={{0,16},{8,24},{16,0},{24,8},{1,17},{9,25},{17,1},{25,9},{2,18},{10... | collective-permute-start | bytes 1572872 | tf_op jit(solution)/shard_map/ppermute | solution.py:467
  45.4 6.2 %collective-permute-start.15 = (f32[4,1024]{1,0:T(4,128)S(1)}, f32[4,1024]{1,0:T(4,128)S(1)}, u32[]{:S(2)}, u32[]{:S(2)}) collective-permute-start(f32[4,1024]{1,0:T(4,128)S(1)} %get-tuple-element.93), channel_id=1, source_target_pairs={{0,1},{1,0},{2,3},{3,2},{4,5},{5,4},{6,7},{7,6},{8,9},{9,8},{10,11... | collective-permute-start | bytes 49160 | tf_op jit(solution)/shard_map/ppermute | solution.py:495
  51.6 18.3 %collective-permute-start.22 = (bf16[1024,256]{1,0:T(8,128)(2,1)S(1)}, bf16[1024,256]{1,0:T(8,128)(2,1)S(1)}, u32[]{:S(2)}, u32[]{:S(2)}) collective-permute-start(bf16[1024,256]{1,0:T(8,128)(2,1)S(1)} %get-tuple-element.100.refs_2_), channel_id=1, source_target_pairs={{0,1},{1,0},{2,3},{3,2},{4,5},{5,4},{6,7},{7,6},{8,9},{9,8},{10,11... | collective-permute-start | bytes 1572872 | tf_op jit(solution)/shard_map/ppermute | solution.py:471
  58.0 8.4 %collective-permute-start.18 = (f32[768,128]{1,0:T(8,128)S(1)}, f32[768,128]{1,0:T(8,128)S(1)}, u32[]{:S(2)}, u32[]{:S(2)}) collective-permute-start(f32[768,128]{1,0:T(8,128)S(1)} %get-tuple-element.97), channel_id=1, source_target_pairs={{0,2},{1,3},{2,0},{3,1},{4,6},{5,7},{6,4},{7,5},{8,10},{9,11},{10,... | collective-permute-start | bytes 1179656 | tf_op jit(solution)/shard_map/ppermute | solution.py:515
  60.5 17.1 %collective-permute-start.21 = (bf16[1024,256]{1,0:T(8,128)(2,1)S(1)}, bf16[1024,256]{1,0:T(8,128)(2,1)S(1)}, u32[]{:S(2)}, u32[]{:S(2)}) collective-permute-start(bf16[1024,256]{1,0:T(8,128)(2,1)S(1)} %get-tuple-element.99.refs_2_), channel_id=1, source_target_pairs={{0,1},{1,0},{2,3},{3,2},{4,5},{5,4},{6,7},{7,6},{8,9},{9,8},{10,11... | collective-permute-start | bytes 1572872 | tf_op jit(solution)/shard_map/ppermute | solution.py:471
  61.9 24.1 %collective-permute-start.20 = (bf16[1024,256]{1,0:T(8,128)(2,1)S(1)}, bf16[1024,256]{1,0:T(8,128)(2,1)S(1)}, u32[]{:S(2)}, u32[]{:S(2)}) collective-permute-start(bf16[1024,256]{1,0:T(8,128)(2,1)S(1)} %get-tuple-element.98.refs_2_), channel_id=1, source_target_pairs={{0,1},{1,0},{2,3},{3,2},{4,5},{5,4},{6,7},{7,6},{8,9},{9,8},{10,11... | collective-permute-start | bytes 1572872 | tf_op jit(solution)/shard_map/ppermute | solution.py:471
  66.3 27.4 %collective-permute-start.19 = (f32[384,128]{1,0:T(8,128)S(1)}, f32[384,128]{1,0:T(8,128)S(1)}, u32[]{:S(2)}, u32[]{:S(2)}) collective-permute-start(f32[384,128]{1,0:T(8,128)S(1)} %add.37), channel_id=1, source_target_pairs={{0,4},{1,5},{2,6},{3,7},{4,0},{5,1},{6,2},{7,3},{8,12},{9,13},{10,... | collective-permute-start | bytes 589832 | tf_op jit(solution)/shard_map/ppermute | solution.py:517
  82.4 23.7 %copy-start.4 = (f32[512,256]{1,0:T(8,128)}, f32[512,256]{1,0:T(8,128)S(1)}, u32[]{:S(2)}) copy-start(f32[512,256]{1,0:T(8,128)S(1)} %get-tuple-element.108.keep_ref) | copy-start | bytes 1572868
  90.8 26.2 %copy-start.6 = (f32[512,256]{1,0:T(8,128)}, f32[512,256]{1,0:T(8,128)S(1)}, u32[]{:S(2)}) copy-start(f32[512,256]{1,0:T(8,128)S(1)} %get-tuple-element.106.keep_ref) | copy-start | bytes 1572868
  90.8 26.2 %collective-permute-start.26 = (bf16[512,256]{1,0:T(8,128)(2,1)S(1)}, bf16[512,256]{1,0:T(8,128)(2,1)S(1)}, u32[]{:S(2)}, u32[]{:S(2)}) collective-permute-start(bf16[512,256]{1,0:T(8,128)(2,1)S(1)} %get-tuple-element.107), channel_id=1, source_target_pairs={{0,2},{1,3},{2,0},{3,1},{4,6},{5,7},{6,4},{7,5},{8,10},{9,11},{10,... | collective-permute-start | bytes 786440 | tf_op jit(solution)/shard_map/ppermute | solution.py:515
  91.7 14.4 %collective-permute-start.28 = (bf16[512,256]{1,0:T(8,128)(2,1)S(1)}, bf16[512,256]{1,0:T(8,128)(2,1)S(1)}, u32[]{:S(2)}, u32[]{:S(2)}) collective-permute-start(bf16[512,256]{1,0:T(8,128)(2,1)S(1)} %get-tuple-element.109), channel_id=1, source_target_pairs={{0,2},{1,3},{2,0},{3,1},{4,6},{5,7},{6,4},{7,5},{8,10},{9,11},{10,... | collective-permute-start | bytes 786440 | tf_op jit(solution)/shard_map/ppermute | solution.py:515
  92.8 16.1 %collective-permute-start.30 = (bf16[512,256]{1,0:T(8,128)(2,1)S(1)}, bf16[512,256]{1,0:T(8,128)(2,1)S(1)}, u32[]{:S(2)}, u32[]{:S(2)}) collective-permute-start(bf16[512,256]{1,0:T(8,128)(2,1)S(1)} %get-tuple-element.111), channel_id=1, source_target_pairs={{0,2},{1,3},{2,0},{3,1},{4,6},{5,7},{6,4},{7,5},{8,10},{9,11},{10,... | collective-permute-start | bytes 786440 | tf_op jit(solution)/shard_map/ppermute | solution.py:515
  106.1 24.8 %collective-permute-start.29 = (bf16[256,256]{1,0:T(8,128)(2,1)S(1)}, bf16[256,256]{1,0:T(8,128)(2,1)S(1)}, u32[]{:S(2)}, u32[]{:S(2)}) collective-permute-start(bf16[256,256]{1,0:T(8,128)(2,1)S(1)} %add.39), channel_id=1, source_target_pairs={{0,4},{1,5},{2,6},{3,7},{4,0},{5,1},{6,2},{7,3},{8,12},{9,13},{10,... | collective-permute-start | bytes 393224 | tf_op jit(solution)/shard_map/ppermute | solution.py:517
  108.9 21.5 %collective-permute-start.31 = (bf16[256,256]{1,0:T(8,128)(2,1)S(1)}, bf16[256,256]{1,0:T(8,128)(2,1)S(1)}, u32[]{:S(2)}, u32[]{:S(2)}) collective-permute-start(bf16[256,256]{1,0:T(8,128)(2,1)S(1)} %add.40), channel_id=1, source_target_pairs={{0,4},{1,5},{2,6},{3,7},{4,0},{5,1},{6,2},{7,3},{8,12},{9,13},{10,... | collective-permute-start | bytes 393224 | tf_op jit(solution)/shard_map/ppermute | solution.py:517
  116.7 11.4 %copy-start = (f32[8,1536]{1,0:T(8,128)}, f32[8,1536]{1,0:T(8,128)S(1)}, u32[]{:S(2)}) copy-start(f32[8,1536]{1,0:T(8,128)S(1)} %get-tuple-element.104.refs_0_) | copy-start | bytes 147460
  116.8 5.4 %collective-permute-start.23 = (f32[8,1536]{1,0:T(8,128)S(1)}, f32[8,1536]{1,0:T(8,128)S(1)}, u32[]{:S(2)}, u32[]{:S(2)}) collective-permute-start(f32[8,1536]{1,0:T(8,128)S(1)} %get-tuple-element.104.refs_0_), channel_id=1, source_target_pairs={{0,2},{1,3},{2,0},{3,1},{4,6},{5,7},{6,4},{7,5},{8,10},{9,11},{10,... | collective-permute-start | bytes 147464 | tf_op jit(solution)/shard_map/ppermute | solution.py:523
  117.0 14.4 %collective-permute-start.27 = (bf16[256,256]{1,0:T(8,128)(2,1)S(1)}, bf16[256,256]{1,0:T(8,128)(2,1)S(1)}, u32[]{:S(2)}, u32[]{:S(2)}) collective-permute-start(bf16[256,256]{1,0:T(8,128)(2,1)S(1)} %add.38), channel_id=1, source_target_pairs={{0,4},{1,5},{2,6},{3,7},{4,0},{5,1},{6,2},{7,3},{8,12},{9,13},{10,... | collective-permute-start | bytes 393224 | tf_op jit(solution)/shard_map/ppermute | solution.py:517
  117.5 8.2 %collective-permute-start.24 = (f32[8,1536]{1,0:T(8,128)S(1)}, f32[8,1536]{1,0:T(8,128)S(1)}, u32[]{:S(2)}, u32[]{:S(2)}) collective-permute-start(f32[8,1536]{1,0:T(8,128)S(1)} %get-tuple-element.104.refs_0_), channel_id=1, source_target_pairs={{0,4},{1,5},{2,6},{3,7},{4,0},{5,1},{6,2},{7,3},{8,12},{9,13},{10,... | collective-permute-start | bytes 147464 | tf_op jit(solution)/shard_map/ppermute | solution.py:523
  122.2 6.0 %copy-start.13 = (f32[8,1536]{1,0:T(8,128)}, f32[8,1536]{1,0:T(8,128)S(1)}, u32[]{:S(2)}) copy-start(f32[8,1536]{1,0:T(8,128)S(1)} %collective-permute-done.23.refs_1_) | copy-start | bytes 147460
  122.2 6.0 %collective-permute-start.25 = (f32[8,1536]{1,0:T(8,128)S(1)}, f32[8,1536]{1,0:T(8,128)}, u32[]{:S(2)}, u32[]{:S(2)}) collective-permute-start(f32[8,1536]{1,0:T(8,128)S(1)} %get-tuple-element.104.refs_0_), channel_id=1, source_target_pairs={{0,6},{1,7},{2,4},{3,5},{4,2},{5,3},{6,0},{7,1},{8,14},{9,15},{10,... | collective-permute-start | bytes 147464 | tf_op jit(solution)/shard_map/ppermute | solution.py:523
  125.7 2.5 %copy-start.14 = (f32[8,1536]{1,0:T(8,128)}, f32[8,1536]{1,0:T(8,128)S(1)}, u32[]{:S(2)}) copy-start(f32[8,1536]{1,0:T(8,128)S(1)} %collective-permute-done.24.refs_2_) | copy-start | bytes 147460
  129.8 1.2 copy-start.5
  130.9 1.0 copy-start.7
  131.9 2.0 %copy-start.8 = (f32[512,256]{1,0:T(8,128)}, f32[512,256]{1,0:T(8,128)S(1)}, u32[]{:S(2)}) copy-start(f32[512,256]{1,0:T(8,128)S(1)} %get-tuple-element.35.keep_ref) | copy-start | bytes 1572868 | tf_op jit(solution)/shard_map/cond
  131.9 17.8 %collective-permute-start.4 = (f32[512,256]{1,0:T(8,128)}, f32[512,256]{1,0:T(8,128)S(1)}, u32[]{:S(2)}, u32[]{:S(2)}) collective-permute-start(f32[512,256]{1,0:T(8,128)} %get-tuple-element.40), channel_id=1, source_target_pairs={{0,2},{1,3},{2,0},{3,1},{4,6},{5,7},{6,4},{7,5},{8,10},{9,11},{10,... | collective-permute-start | bytes 1572872 | tf_op jit(solution)/shard_map/cond/branch_1_fun/ppermute | solution.py:533
  131.9 34.0 %collective-permute-start.2 = (f32[512,256]{1,0:T(8,128)}, f32[512,256]{1,0:T(8,128)S(1)}, u32[]{:S(2)}, u32[]{:S(2)}) collective-permute-start(f32[512,256]{1,0:T(8,128)} %get-tuple-element.38), channel_id=1, source_target_pairs={{0,2},{1,3},{2,0},{3,1},{4,6},{5,7},{6,4},{7,5},{8,10},{9,11},{10,... | collective-permute-start | bytes 1572872 | tf_op jit(solution)/shard_map/cond/branch_1_fun/ppermute | solution.py:533
  134.0 37.7 %copy-start.9 = (f32[512,256]{1,0:T(8,128)S(1)}, f32[512,256]{1,0:T(8,128)}, u32[]{:S(2)}) copy-start(f32[512,256]{1,0:T(8,128)} %copy-done.8) | copy-start | bytes 1572868 | tf_op jit(solution)/shard_map/cond
  134.0 37.7 %collective-permute-start = (f32[512,256]{1,0:T(8,128)}, f32[512,256]{1,0:T(8,128)S(1)}, u32[]{:S(2)}, u32[]{:S(2)}) collective-permute-start(f32[512,256]{1,0:T(8,128)} %get-tuple-element.36), channel_id=1, source_target_pairs={{0,2},{1,3},{2,0},{3,1},{4,6},{5,7},{6,4},{7,5},{8,10},{9,11},{10,... | collective-permute-start | bytes 1572872 | tf_op jit(solution)/shard_map/cond/branch_1_fun/ppermute | solution.py:533
  149.8 24.3 %collective-permute-start.5 = (f32[256,256]{1,0:T(8,128)S(1)}, f32[256,256]{1,0:T(8,128)S(1)}, u32[]{:S(2)}, u32[]{:S(2)}) collective-permute-start(f32[256,256]{1,0:T(8,128)S(1)} %add.36), channel_id=1, source_target_pairs={{0,4},{1,5},{2,6},{3,7},{4,0},{5,1},{6,2},{7,3},{8,12},{9,13},{10,... | collective-permute-start | bytes 786440 | tf_op jit(solution)/shard_map/cond/branch_1_fun/ppermute | solution.py:534
  166.0 22.4 %collective-permute-start.3 = (f32[256,256]{1,0:T(8,128)S(1)}, f32[256,256]{1,0:T(8,128)S(1)}, u32[]{:S(2)}, u32[]{:S(2)}) collective-permute-start(f32[256,256]{1,0:T(8,128)S(1)} %add.35), channel_id=1, source_target_pairs={{0,4},{1,5},{2,6},{3,7},{4,0},{5,1},{6,2},{7,3},{8,12},{9,13},{10,... | collective-permute-start | bytes 786440 | tf_op jit(solution)/shard_map/cond/branch_1_fun/ppermute | solution.py:534
  171.7 19.6 %collective-permute-start.1 = (f32[256,256]{1,0:T(8,128)S(1)}, f32[256,256]{1,0:T(8,128)S(1)}, u32[]{:S(2)}, u32[]{:S(2)}) collective-permute-start(f32[256,256]{1,0:T(8,128)S(1)} %add.34), channel_id=1, source_target_pairs={{0,4},{1,5},{2,6},{3,7},{4,0},{5,1},{6,2},{7,3},{8,12},{9,13},{10,... | collective-permute-start | bytes 786440 | tf_op jit(solution)/shard_map/cond/branch_1_fun/ppermute | solution.py:534
  191.7 1.0 copy-start.3

commit v3 on v2

--- a/solution.py
+++ b/solution.py
@@ -255,23 +255,29 @@
     )(*operands)
 
 
-def add_kernel(keep_ref, near_ref, out_ref):
-    out_ref[...] = (keep_ref[...] + near_ref[...].astype(F32)).astype(out_ref.dtype)
-
-
-def far_sum(keep, near):
+def add_kernel(*refs):
+    *in_refs, out_ref = refs
+    rows = in_refs[0].shape[0]
+    for k in range(len(in_refs) // 2):
+        total = in_refs[2 * k][...] + in_refs[2 * k + 1][...].astype(F32)
+        out_ref[k * rows : (k + 1) * rows, :] = total.astype(out_ref.dtype)
+
+
+def far_sums(*pairs):
+    keep, near = pairs[0]
     rows, width = keep.shape[0] // 2, keep.shape[1]
     spec = pl.BlockSpec((rows, width), lambda i: (1, 0))
+    shape = (len(pairs) * rows, width)
     return pl.pallas_call(
         add_kernel,
         grid=(1,),
-        in_specs=[spec, spec],
-        out_specs=pl.BlockSpec((rows, width), lambda i: (0, 0)),
-        out_shape=jax.ShapeDtypeStruct((rows, width), near.dtype),
-        compiler_params=params(),
-        cost_estimate=cost(rows * width, 12 * rows * width),
+        in_specs=[spec] * (2 * len(pairs)),
+        out_specs=pl.BlockSpec(shape, lambda i: (0, 0)),
+        out_shape=jax.ShapeDtypeStruct(shape, near.dtype),
+        compiler_params=params(),
+        cost_estimate=cost(len(pairs) * rows * width, 12 * len(pairs) * rows * width),
         name="add",
-    )(keep, near)
+    )(*[operand for pair in pairs for operand in pair])
 
 
 BAND = 64
@@ -385,14 +391,15 @@
     out_ref[...] = jnp.dot(inverse_ref[...], gram, precision=HIGHEST, preferred_element_type=F32)
 
 
-def couple(inverse, keep, near, far, whole, start, scale):
-    rows, width = far.shape
+def couple(inverse, keep, near, far, place, whole, start, scale):
+    width = far.shape[1]
+    rows = PANEL
     block = start // width
     spec = pl.BlockSpec((rows, width), lambda i: (0, 0))
     return pl.pallas_call(
         functools.partial(couple_kernel, scale),
         grid=(1,),
-        in_specs=[pl.BlockSpec(inverse.shape, lambda i: (0, 0)), spec, spec, spec, pl.BlockSpec(memory_space=pl.ANY)],
+        in_specs=[pl.BlockSpec(inverse.shape, lambda i: (0, 0)), spec, spec, pl.BlockSpec((rows, width), lambda i: (place, 0)), pl.BlockSpec(memory_space=pl.ANY)],
         out_specs=pl.BlockSpec((rows, width), lambda i: (0, block)),
         out_shape=jax.ShapeDtypeStruct(whole.shape, F32),
         input_output_aliases={4: 0},
@@ -513,10 +520,16 @@
             keep, exact_send, send, squares = partial_grams(weights, sources, squares)
             precise.append((keep, exact_send))
         near = lax.ppermute(send, "blk", z_route(1))
-        onward = far_sum(keep, near)
-        far = lax.ppermute(onward, "blk", z_route(2))
-        grams.append((keep, near, far))
-    state = factor_first(*grams[0], scale)
+        grams.append((keep, near))
+    last = len(groups) - 1
+    far = {}
+    for members in ((0,), tuple(range(1, last)), (last,)):
+        onward = far_sums(*[grams[i] for i in members])
+        onward = lax.ppermute(onward, "blk", z_route(2))
+        for place, i in enumerate(members):
+            far[i] = (onward, place)
+    grams = [pair + far[i] for i, pair in enumerate(grams)]
+    state = factor_first(*grams[0][:3], scale)
     sketch, inverse, guard = factor_last(state, squares, columns)
     guards = [guard]
     for mask in range(1, NZ):
@@ -526,16 +539,16 @@
         sketch = couple(inverse, *grams[i], sketch, i * PANEL, scale)
 
     def rounded(sketch, inverse, last, precise):
-        return couple(inverse, *last, sketch, columns - PANEL, scale)
+        return couple(inverse, *last, 0, sketch, columns - PANEL, scale)
 
     def exact(sketch, inverse, last, precise):
         for i, (keep, send) in enumerate(precise):
             near = lax.ppermute(send, "blk", z_route(1))
-            far = lax.ppermute(far_sum(keep, near), "blk", z_route(2))
-            sketch = couple(inverse, keep, near, far, sketch, (i + 1) * PANEL, scale)
+            far = lax.ppermute(far_sums((keep, near)), "blk", z_route(2))
+            sketch = couple(inverse, keep, near, far, 0, sketch, (i + 1) * PANEL, scale)
         return sketch
 
-    sketch = lax.cond(redo, exact, rounded, sketch, inverse, grams[-1], precise)
+    sketch = lax.cond(redo, exact, rounded, sketch, inverse, grams[-1][:3], precise)
     return whole, sketch
 
 

time: 193 us -> 191 us (0.990)
  starting transfers between devices: 37.6 us -> 35.3 us
    ppermute x3, waiting for transfers between devices: 6.97 us -> 3.36 us  [per_device(): guards.append(lax.ppermute(guard, 'blk', z_route(mask)))]
    ppermute x7 -> x6, starting transfers between devices: 11.6 us -> 8.13 us  [the longest x3 6.15 us: per_device(): onward = lax.ppermute(onward, 'blk', z_route(2))]
    ppermute x4, waiting for transfers between devices: 11.5 us -> 14.6 us  [per_device(): near = lax.ppermute(send, 'blk', z_route(1))]
    ppermute x7 -> x6, waiting for transfers between devices: 16.5 us -> 16.7 us  [the longest x3 16.6 us: exact(): far = lax.ppermute(far_sums((keep, near)), 'blk', z_route(2))]
  transfers between devices with their start and end apart: 32 -> 31, of which waited for: 15 -> 16; matrix products, arithmetic and copies ran while one was open for 2% -> 2% of each run, Pallas kernels for 22% -> 22%
where the time goes in v3:
time: 191 us; the launch traced here: 190 us
  waiting for transfers between devices  101 us (53%)
  Pallas kernels  48.1 us (25%)
  starting transfers between devices  35.3 us (18%)
  other arithmetic  2.92 us (2%)
    ppermute x3, waiting for transfers between devices, exact(): near = lax.ppermute(send, 'blk', z_route(1))  36.6 us
    ppermute x5, waiting for transfers between devices, last_level(): lax.ppermute(own, 'wide', [(w, w ^ wide // 2) for w in range(wide)])  20.3 us
    pallas_call x4, Pallas kernels, partial_grams(): pl.pallas_call(functools.partial(gram_kernel, parts, packed, each), grid=...  18 us
    ppermute x3, waiting for transfers between devices, exact(): far = lax.ppermute(far_sums((keep, near)), 'blk', z_route(2))  16.6 us
    ppermute x4, waiting for transfers between devices, per_device(): near = lax.ppermute(send, 'blk', z_route(1))  14.6 us
    pallas_call x2, Pallas kernels, mix_columns(): pl.pallas_call(mix_kernel, grid=(count,), in_specs=[pl.BlockSpec((1, rows...  7.65 us
    ppermute x5, starting transfers between devices, last_level(): lax.ppermute(own, 'wide', [(w, w ^ wide // 2) for w in range(wide)])  7.27 us
    ppermute x5, waiting for transfers between devices, last_level(): pieces.append(lax.ppermute(own, 'blk', x_shift(s)))  6.56 us
  transfers between devices with their start and end apart: 31, of which 16 were waited for; matrix products, arithmetic and copies ran while one was open for 2% of the time, Pallas kernels for 22%

profile of v3, /device:TPU:0, one launch (start us, length us, event | category | flops | bytes accessed | tf_op | source)
XLA Modules:
  0.0 190.3 jit_solution(4121929591939852554)
XLA Ops:
  0.6 4.9 %mix.2 = (bf16[1024,256]{1,0:T(8,128)(2,1)}, bf16[1024,256]{1,0:T(8,128)(2,1)}, bf16[1024,256]{1,0:T(8,128)(2,1)}) custom-call(s32[1,1024]{1,0:T(1,128)} %bitcast.9, bf16[256,256]{1,0:T(8,128)(2,1)} %constant.25.clone.had_ref, f32[1024,1024]{1,0:T(8,128)} %x_ref.3), custom_call_target="tpu_custom_call" | custom-call | flops 1207959552 | bytes 4718592 | tf_op jit(solution)/shard_map/mix/pallas_call | solution.py:67
  6.1 2.7 %mix.3 = bf16[1024,256]{1,0:T(8,128)(2,1)} custom-call(s32[1,1024]{1,0:T(1,128)} %bitcast.10, bf16[256,256]{1,0:T(8,128)(2,1)} %constant.25.clone.had_ref, f32[1024,1024]{1,0:T(8,128)} %x_ref.3), custom_call_target="tpu_custom_call" | custom-call | flops 402653184 | bytes 1572864 | tf_op jit(solution)/shard_map/mix/pallas_call | solution.py:67
  9.5 1.2 multiply_convert_fusion.own_ref
  10.7 3.0 %collective-permute-start.11 = (bf16[1024,256]{1,0:T(8,128)(2,1)S(1)}, bf16[1024,256]{1,0:T(8,128)(2,1)S(1)}, u32[]{:S(2)}, u32[]{:S(2)}) collective-permute-start(bf16[1024,256]{1,0:T(8,128)(2,1)S(1)} %multiply_convert_fusion.own_ref), channel_id=1, source_target_pairs={{0,16},{8,24},{16,0},{24,8},{1,17},{9,25},{17,1},{25,9},{2,18},{10... | collective-permute-start | bytes 1572872 | tf_op jit(solution)/shard_map/ppermute | solution.py:474
  13.7 1.2 multiply_convert_fusion.3
  15.0 2.0 %collective-permute-start.14 = (bf16[1024,128]{1,0:T(8,128)(2,1)S(1)}, bf16[1024,128]{1,0:T(8,128)(2,1)S(1)}, u32[]{:S(2)}, u32[]{:S(2)}) collective-permute-start(bf16[1024,128]{1,0:T(8,128)(2,1)S(1)} %get-tuple-element.116.own_ref), channel_id=1, source_target_pairs={{0,16},{8,24},{16,0},{24,8},{1,17},{9,25},{17,1},{25,9},{2,18},{10... | collective-permute-start | bytes 786440 | tf_op jit(solution)/shard_map/ppermute | solution.py:474
  17.3 20.3 %collective-permute-done.14.other_ref = bf16[1024,128]{1,0:T(8,128)(2,1)S(1)} collective-permute-done((bf16[1024,128]{1,0:T(8,128)(2,1)S(1)}, bf16[1024,128]{1,0:T(8,128)(2,1)S(1)}, u32[]{:S(2)}, u32[]{:S(2)}) %collective-permute-start.14) | collective-permute-done | bytes 262176 | tf_op jit(solution)/shard_map/ppermute | solution.py:474
  38.5 2.0 %collective-permute-start.16 = (bf16[1024,128]{1,0:T(8,128)(2,1)S(1)}, bf16[1024,128]{1,0:T(8,128)(2,1)S(1)}, u32[]{:S(2)}, u32[]{:S(2)}) collective-permute-start(bf16[1024,128]{1,0:T(8,128)(2,1)S(1)} %get-tuple-element.89.left_ref.refs_2_), channel_id=1, source_target_pairs={{0,1},{1,0},{2,3},{3,2},{4,5},{5,4},{6,7},{7,6},{8,9},{9,8},{10,11... | collective-permute-start | bytes 786440 | tf_op jit(solution)/shard_map/ppermute | solution.py:478
  41.5 2.1 %collective-permute-start.7 = (bf16[1024,256]{1,0:T(8,128)(2,1)S(1)}, bf16[1024,256]{1,0:T(8,128)(2,1)S(1)}, u32[]{:S(2)}, u32[]{:S(2)}) collective-permute-start(bf16[1024,256]{1,0:T(8,128)(2,1)S(1)} %multiply_convert_fusion.2.own_ref), channel_id=1, source_target_pairs={{0,16},{8,24},{16,0},{24,8},{1,17},{9,25},{17,1},{25,9},{2,18},{10... | collective-permute-start | bytes 1572872 | tf_op jit(solution)/shard_map/ppermute | solution.py:474
  43.7 1.7 counts.1
  45.4 1.5 collective-permute-start.15
  46.9 1.1 weigh.2
  48.0 0.9 join.7
  49.0 2.6 %collective-permute-done.15.counts_ref = f32[4,1024]{1,0:T(4,128)S(1)} collective-permute-done((f32[4,1024]{1,0:T(4,128)S(1)}, f32[4,1024]{1,0:T(4,128)S(1)}, u32[]{:S(2)}, u32[]{:S(2)}) %collective-permute-start.15) | collective-permute-done | bytes 16416 | tf_op jit(solution)/shard_map/ppermute | solution.py:502
  51.6 1.4 collective-permute-start.22
  53.0 1.1 weigh.3
  54.2 3.8 %grams.4 = (f32[768,128]{1,0:T(8,128)S(1)}, f32[768,128]{1,0:T(8,128)S(1)}) custom-call(bf16[1024,1024]{1,0:T(8,128)(2,1)S(1)} %get-tuple-element.91.refs_0_, bf16[1024,1024]{1,0:T(8,128)(2,1)S(1)} %get-tuple-element.92.refs_1_, bf16[1024,128]{1,0:T(8,128)(2,1)S(1)} %get-tuple-element.89.left_ref.refs_2_, ...), custom_call_target="tpu_custom_call" | custom-call | flops 2147483648 | bytes 9437184 | tf_op jit(solution)/shard_map/grams/pallas_call | solution.py:245
  57.9 1.7 collective-permute-start.18
  61.9 1.5 collective-permute-start.20
  63.4 2.8 %collective-permute-done.18.refs_1_.near_ref = f32[768,128]{1,0:T(8,128)S(1)} collective-permute-done((f32[768,128]{1,0:T(8,128)S(1)}, f32[768,128]{1,0:T(8,128)S(1)}, u32[]{:S(2)}, u32[]{:S(2)}) %collective-permute-start.18) | collective-permute-done | bytes 393248 | tf_op jit(solution)/shard_map/ppermute | solution.py:522
  66.3 3.6 %collective-permute-start.19 = (f32[384,128]{1,0:T(8,128)S(1)}, f32[384,128]{1,0:T(8,128)S(1)}, u32[]{:S(2)}, u32[]{:S(2)}) collective-permute-start(f32[384,128]{1,0:T(8,128)S(1)} %add.36), channel_id=1, source_target_pairs={{0,4},{1,5},{2,6},{3,7},{4,0},{5,1},{6,2},{7,3},{8,12},{9,13},{10,... | collective-permute-start | bytes 589832 | tf_op jit(solution)/shard_map/ppermute | solution.py:528
  69.9 4.7 %grams.5 = (f32[512,256]{1,0:T(8,128)S(1)}, f32[512,256]{1,0:T(8,128)}, bf16[512,256]{1,0:T(8,128)(2,1)S(1)}, f32[8,1024]{1,0:T(8,128)S(1)}) custom-call(bf16[1024,1024]{1,0:T(8,128)(2,1)S(1)} %get-tuple-element.91.refs_0_, bf16[1024,1024]{1,0:T(8,128)(2,1)S(1)} %get-tuple-element.92.refs_1_, bf16[1024,256]{1,0:T(8,128)(2,1)S(1)} %get-tuple-element.100.refs_2_, ...), custom_call_target="tpu_custom_call" | custom-call | flops 2147483648 | bytes 9437184 | tf_op jit(solution)/shard_map/grams/pallas_call | solution.py:245
  74.7 3.0 %collective-permute-done.21.refs_5_ = bf16[1024,256]{1,0:T(8,128)(2,1)S(1)} collective-permute-done((bf16[1024,256]{1,0:T(8,128)(2,1)S(1)}, bf16[1024,256]{1,0:T(8,128)(2,1)S(1)}, u32[]{:S(2)}, u32[]{:S(2)}) %collective-permute-start.21) | collective-permute-done | bytes 524320 | tf_op jit(solution)/shard_map/ppermute | solution.py:478
  77.6 4.8 %grams.6 = (f32[512,256]{1,0:T(8,128)S(1)}, f32[512,256]{1,0:T(8,128)}, bf16[512,256]{1,0:T(8,128)(2,1)S(1)}, f32[8,1024]{1,0:T(8,128)S(1)}) custom-call(bf16[1024,1024]{1,0:T(8,128)(2,1)S(1)} %get-tuple-element.91.refs_0_, bf16[1024,1024]{1,0:T(8,128)(2,1)S(1)} %get-tuple-element.92.refs_1_, bf16[1024,256]{1,0:T(8,128)(2,1)S(1)} %get-tuple-element.99.refs_2_, ...), custom_call_target="tpu_custom_call" | custom-call | flops 2147483648 | bytes 9437184 | tf_op jit(solution)/shard_map/grams/pallas_call | solution.py:245
  82.4 3.6 %collective-permute-done.20.refs_5_ = bf16[1024,256]{1,0:T(8,128)(2,1)S(1)} collective-permute-done((bf16[1024,256]{1,0:T(8,128)(2,1)S(1)}, bf16[1024,256]{1,0:T(8,128)(2,1)S(1)}, u32[]{:S(2)}, u32[]{:S(2)}) %collective-permute-start.20) | collective-permute-done | bytes 524320 | tf_op jit(solution)/shard_map/ppermute | solution.py:478
  86.0 4.7 %grams.7 = (f32[512,256]{1,0:T(8,128)S(1)}, f32[512,256]{1,0:T(8,128)}, bf16[512,256]{1,0:T(8,128)(2,1)S(1)}, f32[8,1024]{1,0:T(8,128)S(1)}) custom-call(bf16[1024,1024]{1,0:T(8,128)(2,1)S(1)} %get-tuple-element.91.refs_0_, bf16[1024,1024]{1,0:T(8,128)(2,1)S(1)} %get-tuple-element.92.refs_1_, bf16[1024,256]{1,0:T(8,128)(2,1)S(1)} %get-tuple-element.98.refs_2_, ...), custom_call_target="tpu_custom_call" | custom-call | flops 2147483648 | bytes 9437184 | tf_op jit(solution)/shard_map/grams/pallas_call | solution.py:245
  90.7 0.9 collective-permute-start.26
  91.7 1.1 collective-permute-start.28
  93.7 5.0 %factor_first.1.in_ref = f32[256,512]{1,0:T(8,128)S(1)} custom-call(f32[768,128]{1,0:T(8,128)S(1)} %get-tuple-element.96.refs_0_.keep_ref, f32[768,128]{1,0:T(8,128)S(1)} %collective-permute-done.18.refs_1_.near_ref, f32[384,128]{1,0:T(8,128)S(1)} %collective-permute-done.19.far_ref), custom_call_target="tpu_custom_call" | custom-call | flops 10000000000 | bytes 1048576 | tf_op jit(solution)/shard_map/factor_first/pallas_call | solution.py:354
  98.7 2.6 %collective-permute-done.26.refs_1_ = bf16[512,256]{1,0:T(8,128)(2,1)S(1)} collective-permute-done((bf16[512,256]{1,0:T(8,128)(2,1)S(1)}, bf16[512,256]{1,0:T(8,128)(2,1)S(1)}, u32[]{:S(2)}, u32[]{:S(2)}) %collective-permute-start.26) | collective-permute-done | bytes 262176 | tf_op jit(solution)/shard_map/ppermute | solution.py:522
  101.4 1.1 collective-permute-start.27
  102.5 3.7 %collective-permute-done.28.refs_3_.near_ref = bf16[512,256]{1,0:T(8,128)(2,1)S(1)} collective-permute-done((bf16[512,256]{1,0:T(8,128)(2,1)S(1)}, bf16[512,256]{1,0:T(8,128)(2,1)S(1)}, u32[]{:S(2)}, u32[]{:S(2)}) %collective-permute-start.28) | collective-permute-done | bytes 262176 | tf_op jit(solution)/shard_map/ppermute | solution.py:522
  106.2 5.5 %collective-permute-done.29.refs_1_.near_ref = bf16[512,256]{1,0:T(8,128)(2,1)S(1)} collective-permute-done((bf16[512,256]{1,0:T(8,128)(2,1)S(1)}, bf16[512,256]{1,0:T(8,128)(2,1)S(1)}, u32[]{:S(2)}, u32[]{:S(2)}) %collective-permute-start.29) | collective-permute-done | bytes 262176 | tf_op jit(solution)/shard_map/ppermute | solution.py:522
  111.7 1.4 collective-permute-start.30
  113.1 4.4 %factor_last.1 = (f32[256,1024]{1,0:T(8,128)S(1)}, f32[256,256]{1,0:T(8,128)S(1)}, f32[8,1536]{1,0:T(8,128)S(1)}) custom-call(f32[256,512]{1,0:T(8,128)S(1)} %factor_first.1.in_ref, f32[8,1024]{1,0:T(8,128)S(1)} %get-tuple-element.103.squares_ref), custom_call_target="tpu_custom_call" | custom-call | flops 10000000000 | bytes 1048576 | tf_op jit(solution)/shard_map/factor_last/pallas_call | solution.py:372
  119.2 2.7 %collective-permute-start.25 = (f32[8,1536]{1,0:T(8,128)S(1)}, f32[8,1536]{1,0:T(8,128)}, u32[]{:S(2)}, u32[]{:S(2)}) collective-permute-start(f32[8,1536]{1,0:T(8,128)S(1)} %get-tuple-element.104.refs_0_), channel_id=1, source_target_pairs={{0,6},{1,7},{2,4},{3,5},{4,2},{5,3},{6,0},{7,1},{8,14},{9,15},{10,... | collective-permute-start | bytes 147464 | tf_op jit(solution)/shard_map/ppermute | solution.py:536
  122.0 1.8 collective-permute-done.23.refs_1_
  124.3 1.0 collective-permute-done.25.refs_3_
  125.3 1.6 judge.1
  127.6 1.4 couple.10.whole_ref
  130.0 59.3 %conditional.1 = (f32[256,1024]{1,0:T(8,128)S(1)}) conditional(s32[]{:T(128)} %bitcast.6, (f32[256,256]{1,0:T(8,128)S(1)}, f32[512,256]{1,0:T(8,128)S(1)}, bf16[512,256]{1,0:T(8,128)(2,1)S(1)}, bf16[256,256]{1,0:T(8,128)(2,1)S(1)}, f32[256,1024]{1,0:T(8,128)S(1)}) %tuple.14, (f32[512,256]{1,0:T(8,128)}, f32[512,256]{1,0:T(8,128)S(1)}, ...), branch_computations={%region_0.1_spmd, %region_1.2_spmd} | conditional | flops 604176384 | bytes 15728888 | solution.py:551
  130.7 1.3 collective-permute-start.2
  132.8 15.1 %collective-permute-done.4.refs_1_.near_ref = f32[512,256]{1,0:T(8,128)S(1)} collective-permute-done((f32[512,256]{1,0:T(8,128)}, f32[512,256]{1,0:T(8,128)S(1)}, u32[]{:S(2)}, u32[]{:S(2)}) %collective-permute-start.4) | collective-permute-done | bytes 524320 | tf_op jit(solution)/shard_map/cond/branch_1_fun/ppermute | solution.py:546
  148.8 15.9 %collective-permute-done.2.refs_1_.near_ref = f32[512,256]{1,0:T(8,128)S(1)} collective-permute-done((f32[512,256]{1,0:T(8,128)}, f32[512,256]{1,0:T(8,128)S(1)}, u32[]{:S(2)}, u32[]{:S(2)}) %collective-permute-start.2) | collective-permute-done | bytes 524320 | tf_op jit(solution)/shard_map/cond/branch_1_fun/ppermute | solution.py:546
  165.6 5.6 %collective-permute-done.refs_1_.near_ref = f32[512,256]{1,0:T(8,128)S(1)} collective-permute-done((f32[512,256]{1,0:T(8,128)}, f32[512,256]{1,0:T(8,128)S(1)}, u32[]{:S(2)}, u32[]{:S(2)}) %collective-permute-start) | collective-permute-done | bytes 524320 | tf_op jit(solution)/shard_map/cond/branch_1_fun/ppermute | solution.py:546
  171.9 14.2 %collective-permute-done.3.far_ref = f32[256,256]{1,0:T(8,128)S(1)} collective-permute-done((f32[256,256]{1,0:T(8,128)S(1)}, f32[256,256]{1,0:T(8,128)S(1)}, u32[]{:S(2)}, u32[]{:S(2)}) %collective-permute-start.3) | collective-permute-done | bytes 262176 | tf_op jit(solution)/shard_map/cond/branch_1_fun/ppermute | solution.py:547
  186.5 2.5 %collective-permute-done.1.far_ref = f32[256,256]{1,0:T(8,128)S(1)} collective-permute-done((f32[256,256]{1,0:T(8,128)S(1)}, f32[256,256]{1,0:T(8,128)S(1)}, u32[]{:S(2)}, u32[]{:S(2)}) %collective-permute-start.1) | collective-permute-done | bytes 262176 | tf_op jit(solution)/shard_map/cond/branch_1_fun/ppermute | solution.py:547
  189.3 1.0 copy-done.3
  (75 shorter events, 14.9 us)
Async XLA Ops:
  5.5 3.4 %copy-start.9 = (bf16[1024,256]{1,0:T(8,128)(2,1)S(1)}, bf16[1024,256]{1,0:T(8,128)(2,1)}, u32[]{:S(2)}) copy-start(bf16[1024,256]{1,0:T(8,128)(2,1)} %get-tuple-element.81) | copy-start | bytes 1572868
  5.5 3.8 %copy-start.8 = (bf16[1024,256]{1,0:T(8,128)(2,1)S(1)}, bf16[1024,256]{1,0:T(8,128)(2,1)}, u32[]{:S(2)}) copy-start(bf16[1024,256]{1,0:T(8,128)(2,1)} %get-tuple-element.80) | copy-start | bytes 1572868
  5.5 3.9 %copy-start.10 = (bf16[1024,256]{1,0:T(8,128)(2,1)S(1)}, bf16[1024,256]{1,0:T(8,128)(2,1)}, u32[]{:S(2)}) copy-start(bf16[1024,256]{1,0:T(8,128)(2,1)} %get-tuple-element.82) | copy-start | bytes 1572868
  5.5 3.9 %collective-permute-start.10 = (bf16[1024,256]{1,0:T(8,128)(2,1)}, bf16[1024,256]{1,0:T(8,128)(2,1)}, u32[]{:S(2)}, u32[]{:S(2)}) collective-permute-start(bf16[1024,256]{1,0:T(8,128)(2,1)} %get-tuple-element.82), channel_id=1, source_target_pairs={{0,8},{8,0},{16,24},{24,16},{1,9},{9,1},{17,25},{25,17},{2,10},{10... | collective-permute-start | bytes 1572872 | tf_op jit(solution)/shard_map/ppermute | solution.py:487
  8.8 4.8 %collective-permute-start.12 = (bf16[1024,256]{1,0:T(8,128)(2,1)}, bf16[1024,256]{1,0:T(8,128)(2,1)S(1)}, u32[]{:S(2)}, u32[]{:S(2)}) collective-permute-start(bf16[1024,256]{1,0:T(8,128)(2,1)} %mix.3), channel_id=1, source_target_pairs={{0,8},{8,0},{16,24},{24,16},{1,9},{9,1},{17,25},{25,17},{2,10},{10... | collective-permute-start | bytes 1572872 | tf_op jit(solution)/shard_map/ppermute | solution.py:493
  9.0 8.0 %collective-permute-start.8 = (bf16[1024,256]{1,0:T(8,128)(2,1)S(1)}, bf16[1024,256]{1,0:T(8,128)(2,1)S(1)}, u32[]{:S(2)}, u32[]{:S(2)}) collective-permute-start(bf16[1024,256]{1,0:T(8,128)(2,1)S(1)} %copy-done.9), channel_id=1, source_target_pairs={{0,8},{8,0},{16,24},{24,16},{1,9},{9,1},{17,25},{25,17},{2,10},{10... | collective-permute-start | bytes 1572872 | tf_op jit(solution)/shard_map/ppermute | solution.py:487
  9.4 31.9 %collective-permute-start.6 = (bf16[1024,256]{1,0:T(8,128)(2,1)S(1)}, bf16[1024,256]{1,0:T(8,128)(2,1)S(1)}, u32[]{:S(2)}, u32[]{:S(2)}) collective-permute-start(bf16[1024,256]{1,0:T(8,128)(2,1)S(1)} %copy-done.8), channel_id=1, source_target_pairs={{0,8},{8,0},{16,24},{24,16},{1,9},{9,1},{17,25},{25,17},{2,10},{10... | collective-permute-start | bytes 1572872 | tf_op jit(solution)/shard_map/ppermute | solution.py:487
  10.7 34.7 %collective-permute-start.11 = (bf16[1024,256]{1,0:T(8,128)(2,1)S(1)}, bf16[1024,256]{1,0:T(8,128)(2,1)S(1)}, u32[]{:S(2)}, u32[]{:S(2)}) collective-permute-start(bf16[1024,256]{1,0:T(8,128)(2,1)S(1)} %multiply_convert_fusion.own_ref), channel_id=1, source_target_pairs={{0,16},{8,24},{16,0},{24,8},{1,17},{9,25},{17,1},{25,9},{2,18},{10... | collective-permute-start | bytes 1572872 | tf_op jit(solution)/shard_map/ppermute | solution.py:474
  14.9 25.5 %collective-permute-start.13 = (bf16[1024,128]{1,0:T(8,128)(2,1)S(1)}, bf16[1024,128]{1,0:T(8,128)(2,1)S(1)}, u32[]{:S(2)}, u32[]{:S(2)}) collective-permute-start(bf16[1024,128]{1,0:T(8,128)(2,1)S(1)} %get-tuple-element.117.own_ref), channel_id=1, source_target_pairs={{0,16},{8,24},{16,0},{24,8},{1,17},{9,25},{17,1},{25,9},{2,18},{10... | collective-permute-start | bytes 786440 | tf_op jit(solution)/shard_map/ppermute | solution.py:474
  15.0 22.7 %collective-permute-start.14 = (bf16[1024,128]{1,0:T(8,128)(2,1)S(1)}, bf16[1024,128]{1,0:T(8,128)(2,1)S(1)}, u32[]{:S(2)}, u32[]{:S(2)}) collective-permute-start(bf16[1024,128]{1,0:T(8,128)(2,1)S(1)} %get-tuple-element.116.own_ref), channel_id=1, source_target_pairs={{0,16},{8,24},{16,0},{24,8},{1,17},{9,25},{17,1},{25,9},{2,18},{10... | collective-permute-start | bytes 786440 | tf_op jit(solution)/shard_map/ppermute | solution.py:474
  17.2 42.4 %collective-permute-start.9 = (bf16[1024,256]{1,0:T(8,128)(2,1)S(1)}, bf16[1024,256]{1,0:T(8,128)(2,1)S(1)}, u32[]{:S(2)}, u32[]{:S(2)}) collective-permute-start(bf16[1024,256]{1,0:T(8,128)(2,1)S(1)} %multiply_convert_fusion.1.own_ref), channel_id=1, source_target_pairs={{0,16},{8,24},{16,0},{24,8},{1,17},{9,25},{17,1},{25,9},{2,18},{10... | collective-permute-start | bytes 1572872 | tf_op jit(solution)/shard_map/ppermute | solution.py:474
  38.5 14.6 %collective-permute-start.16 = (bf16[1024,128]{1,0:T(8,128)(2,1)S(1)}, bf16[1024,128]{1,0:T(8,128)(2,1)S(1)}, u32[]{:S(2)}, u32[]{:S(2)}) collective-permute-start(bf16[1024,128]{1,0:T(8,128)(2,1)S(1)} %get-tuple-element.89.left_ref.refs_2_), channel_id=1, source_target_pairs={{0,1},{1,0},{2,3},{3,2},{4,5},{5,4},{6,7},{7,6},{8,9},{9,8},{10,11... | collective-permute-start | bytes 786440 | tf_op jit(solution)/shard_map/ppermute | solution.py:478
  40.5 3.2 %copy-start.1 = (s32[2048]{0:T(1024)S(1)}, s32[2048]{0:T(1024)}, u32[]{:S(2)}) copy-start(s32[2048]{0:T(1024)} %param.9) | copy-start | bytes 24580
  40.5 3.2 %copy-start.2 = (s32[2048,1]{0,1:T(1,128)S(1)}, s32[2048,1]{0,1:T(1,128)}, u32[]{:S(2)}) copy-start(s32[2048,1]{0,1:T(1,128)} %param.10) | copy-start | bytes 24580
  41.3 11.8 %collective-permute-start.17 = (bf16[1024,128]{1,0:T(8,128)(2,1)S(1)}, bf16[1024,128]{1,0:T(8,128)(2,1)S(1)}, u32[]{:S(2)}, u32[]{:S(2)}) collective-permute-start(bf16[1024,128]{1,0:T(8,128)(2,1)S(1)} %get-tuple-element.90.right_ref.refs_3_), channel_id=1, source_target_pairs={{0,1},{1,0},{2,3},{3,2},{4,5},{5,4},{6,7},{7,6},{8,9},{9,8},{10,11... | collective-permute-start | bytes 786440 | tf_op jit(solution)/shard_map/ppermute | solution.py:478
  41.5 19.5 %collective-permute-start.7 = (bf16[1024,256]{1,0:T(8,128)(2,1)S(1)}, bf16[1024,256]{1,0:T(8,128)(2,1)S(1)}, u32[]{:S(2)}, u32[]{:S(2)}) collective-permute-start(bf16[1024,256]{1,0:T(8,128)(2,1)S(1)} %multiply_convert_fusion.2.own_ref), channel_id=1, source_target_pairs={{0,16},{8,24},{16,0},{24,8},{1,17},{9,25},{17,1},{25,9},{2,18},{10... | collective-permute-start | bytes 1572872 | tf_op jit(solution)/shard_map/ppermute | solution.py:474
  45.4 6.2 %collective-permute-start.15 = (f32[4,1024]{1,0:T(4,128)S(1)}, f32[4,1024]{1,0:T(4,128)S(1)}, u32[]{:S(2)}, u32[]{:S(2)}) collective-permute-start(f32[4,1024]{1,0:T(4,128)S(1)} %get-tuple-element.93), channel_id=1, source_target_pairs={{0,1},{1,0},{2,3},{3,2},{4,5},{5,4},{6,7},{7,6},{8,9},{9,8},{10,11... | collective-permute-start | bytes 49160 | tf_op jit(solution)/shard_map/ppermute | solution.py:502
  51.6 18.3 %collective-permute-start.22 = (bf16[1024,256]{1,0:T(8,128)(2,1)S(1)}, bf16[1024,256]{1,0:T(8,128)(2,1)S(1)}, u32[]{:S(2)}, u32[]{:S(2)}) collective-permute-start(bf16[1024,256]{1,0:T(8,128)(2,1)S(1)} %get-tuple-element.100.refs_2_), channel_id=1, source_target_pairs={{0,1},{1,0},{2,3},{3,2},{4,5},{5,4},{6,7},{7,6},{8,9},{9,8},{10,11... | collective-permute-start | bytes 1572872 | tf_op jit(solution)/shard_map/ppermute | solution.py:478
  57.9 8.3 %collective-permute-start.18 = (f32[768,128]{1,0:T(8,128)S(1)}, f32[768,128]{1,0:T(8,128)S(1)}, u32[]{:S(2)}, u32[]{:S(2)}) collective-permute-start(f32[768,128]{1,0:T(8,128)S(1)} %get-tuple-element.97), channel_id=1, source_target_pairs={{0,2},{1,3},{2,0},{3,1},{4,6},{5,7},{6,4},{7,5},{8,10},{9,11},{10,... | collective-permute-start | bytes 1179656 | tf_op jit(solution)/shard_map/ppermute | solution.py:522
  60.5 17.1 %collective-permute-start.21 = (bf16[1024,256]{1,0:T(8,128)(2,1)S(1)}, bf16[1024,256]{1,0:T(8,128)(2,1)S(1)}, u32[]{:S(2)}, u32[]{:S(2)}) collective-permute-start(bf16[1024,256]{1,0:T(8,128)(2,1)S(1)} %get-tuple-element.99.refs_2_), channel_id=1, source_target_pairs={{0,1},{1,0},{2,3},{3,2},{4,5},{5,4},{6,7},{7,6},{8,9},{9,8},{10,11... | collective-permute-start | bytes 1572872 | tf_op jit(solution)/shard_map/ppermute | solution.py:478
  61.9 24.1 %collective-permute-start.20 = (bf16[1024,256]{1,0:T(8,128)(2,1)S(1)}, bf16[1024,256]{1,0:T(8,128)(2,1)S(1)}, u32[]{:S(2)}, u32[]{:S(2)}) collective-permute-start(bf16[1024,256]{1,0:T(8,128)(2,1)S(1)} %get-tuple-element.98.refs_2_), channel_id=1, source_target_pairs={{0,1},{1,0},{2,3},{3,2},{4,5},{5,4},{6,7},{7,6},{8,9},{9,8},{10,11... | collective-permute-start | bytes 1572872 | tf_op jit(solution)/shard_map/ppermute | solution.py:478
  66.3 27.4 %collective-permute-start.19 = (f32[384,128]{1,0:T(8,128)S(1)}, f32[384,128]{1,0:T(8,128)S(1)}, u32[]{:S(2)}, u32[]{:S(2)}) collective-permute-start(f32[384,128]{1,0:T(8,128)S(1)} %add.36), channel_id=1, source_target_pairs={{0,4},{1,5},{2,6},{3,7},{4,0},{5,1},{6,2},{7,3},{8,12},{9,13},{10,... | collective-permute-start | bytes 589832 | tf_op jit(solution)/shard_map/ppermute | solution.py:528
  74.7 37.0 %copy-start.4 = (f32[512,256]{1,0:T(8,128)}, f32[512,256]{1,0:T(8,128)S(1)}, u32[]{:S(2)}) copy-start(f32[512,256]{1,0:T(8,128)S(1)} %get-tuple-element.110.refs_0_.keep_ref) | copy-start | bytes 1572868
  82.4 29.2 %copy-start.6 = (f32[512,256]{1,0:T(8,128)}, f32[512,256]{1,0:T(8,128)S(1)}, u32[]{:S(2)}) copy-start(f32[512,256]{1,0:T(8,128)S(1)} %get-tuple-element.108.refs_2_.keep_ref) | copy-start | bytes 1572868
  90.7 10.6 %collective-permute-start.26 = (bf16[512,256]{1,0:T(8,128)(2,1)S(1)}, bf16[512,256]{1,0:T(8,128)(2,1)S(1)}, u32[]{:S(2)}, u32[]{:S(2)}) collective-permute-start(bf16[512,256]{1,0:T(8,128)(2,1)S(1)} %get-tuple-element.107), channel_id=1, source_target_pairs={{0,2},{1,3},{2,0},{3,1},{4,6},{5,7},{6,4},{7,5},{8,10},{9,11},{10,... | collective-permute-start | bytes 786440 | tf_op jit(solution)/shard_map/ppermute | solution.py:522
  91.7 14.5 %collective-permute-start.28 = (bf16[512,256]{1,0:T(8,128)(2,1)S(1)}, bf16[512,256]{1,0:T(8,128)(2,1)S(1)}, u32[]{:S(2)}, u32[]{:S(2)}) collective-permute-start(bf16[512,256]{1,0:T(8,128)(2,1)S(1)} %get-tuple-element.109), channel_id=1, source_target_pairs={{0,2},{1,3},{2,0},{3,1},{4,6},{5,7},{6,4},{7,5},{8,10},{9,11},{10,... | collective-permute-start | bytes 786440 | tf_op jit(solution)/shard_map/ppermute | solution.py:522
  92.8 18.9 %collective-permute-start.29 = (bf16[512,256]{1,0:T(8,128)(2,1)S(1)}, bf16[512,256]{1,0:T(8,128)(2,1)S(1)}, u32[]{:S(2)}, u32[]{:S(2)}) collective-permute-start(bf16[512,256]{1,0:T(8,128)(2,1)S(1)} %get-tuple-element.111), channel_id=1, source_target_pairs={{0,2},{1,3},{2,0},{3,1},{4,6},{5,7},{6,4},{7,5},{8,10},{9,11},{10,... | collective-permute-start | bytes 786440 | tf_op jit(solution)/shard_map/ppermute | solution.py:522
  101.4 28.1 %collective-permute-start.27 = (bf16[256,256]{1,0:T(8,128)(2,1)S(1)}, bf16[256,256]{1,0:T(8,128)(2,1)S(1)}, u32[]{:S(2)}, u32[]{:S(2)}) collective-permute-start(bf16[256,256]{1,0:T(8,128)(2,1)S(1)} %add.37), channel_id=1, source_target_pairs={{0,4},{1,5},{2,6},{3,7},{4,0},{5,1},{6,2},{7,3},{8,12},{9,13},{10,... | collective-permute-start | bytes 393224 | tf_op jit(solution)/shard_map/ppermute | solution.py:528
  111.7 15.9 %collective-permute-start.30 = (bf16[512,256]{1,0:T(8,128)(2,1)S(1)}, bf16[512,256]{1,0:T(8,128)(2,1)S(1)}, u32[]{:S(2)}, u32[]{:S(2)}) collective-permute-start(bf16[512,256]{1,0:T(8,128)(2,1)S(1)} %add.38), channel_id=1, source_target_pairs={{0,4},{1,5},{2,6},{3,7},{4,0},{5,1},{6,2},{7,3},{8,12},{9,13},{10,... | collective-permute-start | bytes 786440 | tf_op jit(solution)/shard_map/ppermute | solution.py:528
  117.5 7.8 %copy-start = (f32[8,1536]{1,0:T(8,128)}, f32[8,1536]{1,0:T(8,128)S(1)}, u32[]{:S(2)}) copy-start(f32[8,1536]{1,0:T(8,128)S(1)} %get-tuple-element.104.refs_0_) | copy-start | bytes 147460
  117.5 6.2 %collective-permute-start.23 = (f32[8,1536]{1,0:T(8,128)S(1)}, f32[8,1536]{1,0:T(8,128)S(1)}, u32[]{:S(2)}, u32[]{:S(2)}) collective-permute-start(f32[8,1536]{1,0:T(8,128)S(1)} %get-tuple-element.104.refs_0_), channel_id=1, source_target_pairs={{0,2},{1,3},{2,0},{3,1},{4,6},{5,7},{6,4},{7,5},{8,10},{9,11},{10,... | collective-permute-start | bytes 147464 | tf_op jit(solution)/shard_map/ppermute | solution.py:536
  118.4 5.9 %collective-permute-start.24 = (f32[8,1536]{1,0:T(8,128)S(1)}, f32[8,1536]{1,0:T(8,128)S(1)}, u32[]{:S(2)}, u32[]{:S(2)}) collective-permute-start(f32[8,1536]{1,0:T(8,128)S(1)} %get-tuple-element.104.refs_0_), channel_id=1, source_target_pairs={{0,4},{1,5},{2,6},{3,7},{4,0},{5,1},{6,2},{7,3},{8,12},{9,13},{10,... | collective-permute-start | bytes 147464 | tf_op jit(solution)/shard_map/ppermute | solution.py:536
  119.2 6.1 %collective-permute-start.25 = (f32[8,1536]{1,0:T(8,128)S(1)}, f32[8,1536]{1,0:T(8,128)}, u32[]{:S(2)}, u32[]{:S(2)}) collective-permute-start(f32[8,1536]{1,0:T(8,128)S(1)} %get-tuple-element.104.refs_0_), channel_id=1, source_target_pairs={{0,6},{1,7},{2,4},{3,5},{4,2},{5,3},{6,0},{7,1},{8,14},{9,15},{10,... | collective-permute-start | bytes 147464 | tf_op jit(solution)/shard_map/ppermute | solution.py:536
  123.8 1.6 copy-start.11
  124.3 1.0 copy-start.12
  126.9 2.1 %copy-start.7 = (f32[512,256]{1,0:T(8,128)S(1)}, f32[512,256]{1,0:T(8,128)}, u32[]{:S(2)}) copy-start(f32[512,256]{1,0:T(8,128)} %copy-done.6) | copy-start | bytes 1572868
  129.0 1.0 copy-start.5
  130.0 17.8 %collective-permute-start.4 = (f32[512,256]{1,0:T(8,128)}, f32[512,256]{1,0:T(8,128)S(1)}, u32[]{:S(2)}, u32[]{:S(2)}) collective-permute-start(f32[512,256]{1,0:T(8,128)} %get-tuple-element.40), channel_id=1, source_target_pairs={{0,2},{1,3},{2,0},{3,1},{4,6},{5,7},{6,4},{7,5},{8,10},{9,11},{10,... | collective-permute-start | bytes 1572872 | tf_op jit(solution)/shard_map/cond/branch_1_fun/ppermute | solution.py:546
  130.7 34.0 %collective-permute-start.2 = (f32[512,256]{1,0:T(8,128)}, f32[512,256]{1,0:T(8,128)S(1)}, u32[]{:S(2)}, u32[]{:S(2)}) collective-permute-start(f32[512,256]{1,0:T(8,128)} %get-tuple-element.38), channel_id=1, source_target_pairs={{0,2},{1,3},{2,0},{3,1},{4,6},{5,7},{6,4},{7,5},{8,10},{9,11},{10,... | collective-permute-start | bytes 1572872 | tf_op jit(solution)/shard_map/cond/branch_1_fun/ppermute | solution.py:546
  132.1 39.1 %collective-permute-start = (f32[512,256]{1,0:T(8,128)}, f32[512,256]{1,0:T(8,128)S(1)}, u32[]{:S(2)}, u32[]{:S(2)}) collective-permute-start(f32[512,256]{1,0:T(8,128)} %get-tuple-element.36), channel_id=1, source_target_pairs={{0,2},{1,3},{2,0},{3,1},{4,6},{5,7},{6,4},{7,5},{8,10},{9,11},{10,... | collective-permute-start | bytes 1572872 | tf_op jit(solution)/shard_map/cond/branch_1_fun/ppermute | solution.py:546
  147.9 23.6 %collective-permute-start.5 = (f32[256,256]{1,0:T(8,128)S(1)}, f32[256,256]{1,0:T(8,128)S(1)}, u32[]{:S(2)}, u32[]{:S(2)}) collective-permute-start(f32[256,256]{1,0:T(8,128)S(1)} %add.35), channel_id=1, source_target_pairs={{0,4},{1,5},{2,6},{3,7},{4,0},{5,1},{6,2},{7,3},{8,12},{9,13},{10,... | collective-permute-start | bytes 786440 | tf_op jit(solution)/shard_map/cond/branch_1_fun/ppermute | solution.py:547
  164.7 21.3 %collective-permute-start.3 = (f32[256,256]{1,0:T(8,128)S(1)}, f32[256,256]{1,0:T(8,128)S(1)}, u32[]{:S(2)}, u32[]{:S(2)}) collective-permute-start(f32[256,256]{1,0:T(8,128)S(1)} %add.34), channel_id=1, source_target_pairs={{0,4},{1,5},{2,6},{3,7},{4,0},{5,1},{6,2},{7,3},{8,12},{9,13},{10,... | collective-permute-start | bytes 786440 | tf_op jit(solution)/shard_map/cond/branch_1_fun/ppermute | solution.py:547
  171.2 17.7 %collective-permute-start.1 = (f32[256,256]{1,0:T(8,128)S(1)}, f32[256,256]{1,0:T(8,128)S(1)}, u32[]{:S(2)}, u32[]{:S(2)}) collective-permute-start(f32[256,256]{1,0:T(8,128)S(1)} %add.33), channel_id=1, source_target_pairs={{0,4},{1,5},{2,6},{3,7},{4,0},{5,1},{6,2},{7,3},{8,12},{9,13},{10,... | collective-permute-start | bytes 786440 | tf_op jit(solution)/shard_map/cond/branch_1_fun/ppermute | solution.py:547
  189.3 1.0 copy-start.3

commit v4 on v2

--- a/solution.py
+++ b/solution.py
@@ -172,15 +172,17 @@
 GRAM_TILES = 2
 
 
-def gram_kernel(parts, packed, each, *refs):
+def gram_kernel(parts, packed, each, begun, *refs):
     refs, (acc,) = refs[:-1], refs[-1:]
     outs = refs[parts * each :]
+    if begun:
+        begun_ref, *outs = outs
     keep_ref, send_ref = (outs[0], outs[1]) if packed else (outs[1], outs[2])
     step = pl.program_id(0)
 
     @pl.when(step == 0)
     def _():
-        acc[...] = jnp.zeros_like(acc)
+        acc[...] = begun_ref[...] if begun else jnp.zeros_like(acc)
 
     for p in range(parts):
         hi_ref, lo_ref, *rows_refs = refs[each * p : each * (p + 1)]
@@ -214,7 +216,36 @@
             )
 
 
-def partial_grams(weights, chunk_rows, before):
+def own_kernel(hi_ref, lo_ref, rows_ref, out_ref):
+    rows = rows_ref[...]
+    total = jnp.dot(lo_ref[...], rows, preferred_element_type=F32) + jnp.dot(hi_ref[...], rows, preferred_element_type=F32)
+
+    @pl.when(pl.program_id(0) == 0)
+    def _():
+        out_ref[...] = total
+
+    @pl.when(pl.program_id(0) > 0)
+    def _():
+        out_ref[...] += total
+
+
+def own_share(weight, block):
+    rows, width = block.shape
+    tile = rows // GRAM_TILES
+    weight_spec = pl.BlockSpec((NZ * PANEL, tile), lambda k: (0, k))
+    return pl.pallas_call(
+        own_kernel,
+        grid=(GRAM_TILES,),
+        in_specs=[weight_spec, weight_spec, pl.BlockSpec((tile, width), lambda k: (k, 0))],
+        out_specs=pl.BlockSpec((NZ * PANEL, width), lambda k: (0, 0)),
+        out_shape=jax.ShapeDtypeStruct((NZ * PANEL, width), F32),
+        compiler_params=params(),
+        cost_estimate=cost(4 * NZ * PANEL * rows * width, 4 * NZ * PANEL * (rows + width)),
+        name="share",
+    )(*weight, block)
+
+
+def partial_grams(weights, chunk_rows, before, begun=None):
     packed = before is None
     parts = len(chunk_rows)
     rows = chunk_rows[0][0].shape[0]
@@ -236,6 +267,9 @@
     out = pl.BlockSpec(shape, lambda k: (0, 0))
     out_specs = [out, out]
     out_shape = [jax.ShapeDtypeStruct(shape, F32)] * 2
+    if begun is not None:
+        operands.append(begun)
+        specs.append(pl.BlockSpec(begun.shape, lambda k: (0, 0)))
     if not packed:
         squares = pl.BlockSpec(before.shape, lambda k: (0, 0))
         operands.append(before)
@@ -243,7 +277,7 @@
         out_specs += [out, squares]
         out_shape += [jax.ShapeDtypeStruct(shape, BF16), jax.ShapeDtypeStruct(before.shape, F32)]
     return pl.pallas_call(
-        functools.partial(gram_kernel, parts, packed, each),
+        functools.partial(gram_kernel, parts, packed, each, begun is not None),
         grid=(parts * GRAM_TILES,),
         in_specs=specs,
         out_specs=tuple(out_specs),
@@ -507,10 +541,13 @@
         if i == 0:
             for p in range(nx):
                 weights.append(weigh(owner_counts[p], *sources[p]))
+        begun, first = None, 0
+        if 0 < i < len(groups) - 1:
+            begun, first = own_share(weights[0], sources[0][0]), 1
         if i == 0:
             keep, send = partial_grams(weights, sources, None)
         else:
-            keep, exact_send, send, squares = partial_grams(weights, sources, squares)
+            keep, exact_send, send, squares = partial_grams(weights[first:], sources[first:], squares, begun)
             precise.append((keep, exact_send))
         near = lax.ppermute(send, "blk", z_route(1))
         onward = far_sum(keep, near)

time: 193 us -> 188 us (0.974)
  waiting for transfers between devices: 102 us -> 89.9 us
  starting transfers between devices: 37.6 us -> 40.8 us
    ppermute x4, waiting for transfers between devices: 11.5 us -> 5.64 us  [per_device(): near = lax.ppermute(send, 'blk', z_route(1))]
    ppermute x5, waiting for transfers between devices: 20.3 us -> 17.7 us  [last_level(): lax.ppermute(own, 'wide', [(w, w ^ wide // 2) for w in range(wide)])]
    ppermute x1, waiting for transfers between devices: 2.62 us -> 0.01 us  [per_device(): owner_counts.append(lax.ppermute(counts[s], 'blk', x_shift(s)))]
    ppermute x3, waiting for transfers between devices: 6.97 us -> 4.68 us  [per_device(): guards.append(lax.ppermute(guard, 'blk', z_route(mask)))]
    pallas_call x4 -> x6, Pallas kernels: 18 us -> 18.1 us  [the longest x4 14.3 us: partial_grams(): pl.pallas_call(functools.partial(gram_kernel, parts, packed, each, begun...]
  transfers between devices with their start and end apart: 32 -> 32, of which waited for: 15 -> 16; matrix products, arithmetic and copies ran while one was open for 2% -> 2% of each run, Pallas kernels for 22% -> 25%
where the time goes in v4:
time: 188 us; the launch traced here: 187 us
  waiting for transfers between devices  89.9 us (48%)
  Pallas kernels  49.1 us (26%)
  starting transfers between devices  40.8 us (22%)
  other arithmetic  4.14 us (2%)
    ppermute x3, waiting for transfers between devices, exact(): near = lax.ppermute(send, 'blk', z_route(1))  38.3 us
    ppermute x5, waiting for transfers between devices, last_level(): lax.ppermute(own, 'wide', [(w, w ^ wide // 2) for w in range(wide)])  17.7 us
    ppermute x3, waiting for transfers between devices, exact(): far = lax.ppermute(far_sum(keep, near), 'blk', z_route(2))  15.3 us
    pallas_call x4, Pallas kernels, partial_grams(): pl.pallas_call(functools.partial(gram_kernel, parts, packed, each, begun...  14.3 us
    ppermute x4, starting transfers between devices, per_device(): far = lax.ppermute(onward, 'blk', z_route(2))  8.52 us
    ppermute x5, waiting for transfers between devices, last_level(): pieces.append(lax.ppermute(own, 'blk', x_shift(s)))  8.34 us
    pallas_call x2, Pallas kernels, mix_columns(): pl.pallas_call(mix_kernel, grid=(count,), in_specs=[pl.BlockSpec((1, rows...  7.67 us
    ppermute x5, starting transfers between devices, last_level(): lax.ppermute(own, 'wide', [(w, w ^ wide // 2) for w in range(wide)])  7.34 us
  transfers between devices with their start and end apart: 32, of which 16 were waited for; matrix products, arithmetic and copies ran while one was open for 2% of the time, Pallas kernels for 25%

profile of v4, /device:TPU:0, one launch (start us, length us, event | category | flops | bytes accessed | tf_op | source)
XLA Modules:
  0.0 187.2 jit_solution(1158585971824725443)
XLA Ops:
  0.6 2.8 %mix.3 = bf16[1024,256]{1,0:T(8,128)(2,1)} custom-call(s32[1,1024]{1,0:T(1,128)} %bitcast.9, bf16[256,256]{1,0:T(8,128)(2,1)} %constant.25.clone.had_ref, f32[1024,1024]{1,0:T(8,128)} %x_ref.3), custom_call_target="tpu_custom_call" | custom-call | flops 402653184 | bytes 1572864 | tf_op jit(solution)/shard_map/mix/pallas_call | solution.py:67
  3.9 4.9 %mix.2 = (bf16[1024,256]{1,0:T(8,128)(2,1)}, bf16[1024,256]{1,0:T(8,128)(2,1)}, bf16[1024,256]{1,0:T(8,128)(2,1)}) custom-call(s32[1,1024]{1,0:T(1,128)} %bitcast.10, bf16[256,256]{1,0:T(8,128)(2,1)} %constant.25.clone.had_ref, f32[1024,1024]{1,0:T(8,128)} %x_ref.3), custom_call_target="tpu_custom_call" | custom-call | flops 1207959552 | bytes 4718592 | tf_op jit(solution)/shard_map/mix/pallas_call | solution.py:67
  9.6 3.0 %collective-permute-start.14 = (bf16[1024,128]{1,0:T(8,128)(2,1)S(1)}, bf16[1024,128]{1,0:T(8,128)(2,1)S(1)}, u32[]{:S(2)}, u32[]{:S(2)}) collective-permute-start(bf16[1024,128]{1,0:T(8,128)(2,1)S(1)} %get-tuple-element.116.own_ref), channel_id=1, source_target_pairs={{0,16},{8,24},{16,0},{24,8},{1,17},{9,25},{17,1},{25,9},{2,18},{10... | collective-permute-start | bytes 786440 | tf_op jit(solution)/shard_map/ppermute | solution.py:501
  13.9 2.0 %collective-permute-start.11 = (bf16[1024,256]{1,0:T(8,128)(2,1)S(1)}, bf16[1024,256]{1,0:T(8,128)(2,1)S(1)}, u32[]{:S(2)}, u32[]{:S(2)}) collective-permute-start(bf16[1024,256]{1,0:T(8,128)(2,1)S(1)} %multiply_convert_fusion.own_ref), channel_id=1, source_target_pairs={{0,16},{8,24},{16,0},{24,8},{1,17},{9,25},{17,1},{25,9},{2,18},{10... | collective-permute-start | bytes 1572872 | tf_op jit(solution)/shard_map/ppermute | solution.py:501
  17.3 2.4 %collective-permute-done.14.other_ref = bf16[1024,128]{1,0:T(8,128)(2,1)S(1)} collective-permute-done((bf16[1024,128]{1,0:T(8,128)(2,1)S(1)}, bf16[1024,128]{1,0:T(8,128)(2,1)S(1)}, u32[]{:S(2)}, u32[]{:S(2)}) %collective-permute-start.14) | collective-permute-done | bytes 262176 | tf_op jit(solution)/shard_map/ppermute | solution.py:501
  20.5 4.8 %collective-permute-done.13.other_ref = bf16[1024,128]{1,0:T(8,128)(2,1)S(1)} collective-permute-done((bf16[1024,128]{1,0:T(8,128)(2,1)S(1)}, bf16[1024,128]{1,0:T(8,128)(2,1)S(1)}, u32[]{:S(2)}, u32[]{:S(2)}) %collective-permute-start.13) | collective-permute-done | bytes 262176 | tf_op jit(solution)/shard_map/ppermute | solution.py:501
  26.2 2.0 %collective-permute-start.17 = (bf16[1024,128]{1,0:T(8,128)(2,1)S(1)}, bf16[1024,128]{1,0:T(8,128)(2,1)S(1)}, u32[]{:S(2)}, u32[]{:S(2)}) collective-permute-start(bf16[1024,128]{1,0:T(8,128)(2,1)S(1)} %get-tuple-element.90.right_ref.refs_3_), channel_id=1, source_target_pairs={{0,1},{1,0},{2,3},{3,2},{4,5},{5,4},{6,7},{7,6},{8,9},{9,8},{10,11... | collective-permute-start | bytes 786440 | tf_op jit(solution)/shard_map/ppermute | solution.py:505
  28.2 1.4 multiply_convert_fusion.2.own_ref
  29.6 2.1 %collective-permute-start.7 = (bf16[1024,256]{1,0:T(8,128)(2,1)S(1)}, bf16[1024,256]{1,0:T(8,128)(2,1)}, u32[]{:S(2)}, u32[]{:S(2)}) collective-permute-start(bf16[1024,256]{1,0:T(8,128)(2,1)S(1)} %multiply_convert_fusion.2.own_ref), channel_id=1, source_target_pairs={{0,16},{8,24},{16,0},{24,8},{1,17},{9,25},{17,1},{25,9},{2,18},{10... | collective-permute-start | bytes 1572872 | tf_op jit(solution)/shard_map/ppermute | solution.py:501
  31.7 1.7 counts.1
  33.5 3.1 %collective-permute-done.11.other_ref = bf16[1024,256]{1,0:T(8,128)(2,1)S(1)} collective-permute-done((bf16[1024,256]{1,0:T(8,128)(2,1)S(1)}, bf16[1024,256]{1,0:T(8,128)(2,1)S(1)}, u32[]{:S(2)}, u32[]{:S(2)}) %collective-permute-start.11) | collective-permute-done | bytes 524320 | tf_op jit(solution)/shard_map/ppermute | solution.py:501
  36.6 2.0 %collective-permute-start.15 = (f32[4,1024]{1,0:T(4,128)S(1)}, f32[4,1024]{1,0:T(4,128)S(1)}, u32[]{:S(2)}, u32[]{:S(2)}) collective-permute-start(f32[4,1024]{1,0:T(4,128)S(1)} %get-tuple-element.93), channel_id=1, source_target_pairs={{0,1},{1,0},{2,3},{3,2},{4,5},{5,4},{6,7},{7,6},{8,9},{9,8},{10,11... | collective-permute-start | bytes 49160 | tf_op jit(solution)/shard_map/ppermute | solution.py:529
  40.7 7.2 %collective-permute-done.9.other_ref = bf16[1024,256]{1,0:T(8,128)(2,1)} collective-permute-done((bf16[1024,256]{1,0:T(8,128)(2,1)S(1)}, bf16[1024,256]{1,0:T(8,128)(2,1)}, u32[]{:S(2)}, u32[]{:S(2)}) %collective-permute-start.9) | collective-permute-done | bytes 524320 | tf_op jit(solution)/shard_map/ppermute | solution.py:501
  48.0 1.9 join.8
  49.8 2.0 %collective-permute-start.21 = (bf16[1024,256]{1,0:T(8,128)(2,1)S(1)}, bf16[1024,256]{1,0:T(8,128)(2,1)S(1)}, u32[]{:S(2)}, u32[]{:S(2)}) collective-permute-start(bf16[1024,256]{1,0:T(8,128)(2,1)S(1)} %get-tuple-element.99.rows_ref), channel_id=1, source_target_pairs={{0,1},{1,0},{2,3},{3,2},{4,5},{5,4},{6,7},{7,6},{8,9},{9,8},{10,11... | collective-permute-start | bytes 1572872 | tf_op jit(solution)/shard_map/ppermute | solution.py:505
  53.0 3.8 %grams.4 = (f32[768,128]{1,0:T(8,128)S(1)}, f32[768,128]{1,0:T(8,128)S(1)}) custom-call(bf16[1024,1024]{1,0:T(8,128)(2,1)S(1)} %get-tuple-element.91.refs_0_.hi_ref, bf16[1024,1024]{1,0:T(8,128)(2,1)S(1)} %get-tuple-element.92.refs_1_.lo_ref, bf16[1024,128]{1,0:T(8,128)(2,1)S(1)} %get-tuple-element.89.left_ref.refs_2_, ...), custom_call_target="tpu_custom_call" | custom-call | flops 2147483648 | bytes 9437184 | tf_op jit(solution)/shard_map/grams/pallas_call | solution.py:279
  56.8 2.1 %collective-permute-start.18 = (f32[768,128]{1,0:T(8,128)S(1)}, f32[768,128]{1,0:T(8,128)S(1)}, u32[]{:S(2)}, u32[]{:S(2)}) collective-permute-start(f32[768,128]{1,0:T(8,128)S(1)} %get-tuple-element.97), channel_id=1, source_target_pairs={{0,2},{1,3},{2,0},{3,1},{4,6},{5,7},{6,4},{7,5},{8,10},{9,11},{10,... | collective-permute-start | bytes 1179656 | tf_op jit(solution)/shard_map/ppermute | solution.py:552
  58.9 1.9 join.9
  60.8 1.5 collective-permute-start.20
  62.3 1.9 %share.3.refs_3_ = f32[1024,256]{1,0:T(8,128)S(1)} custom-call(bf16[1024,1024]{1,0:T(8,128)(2,1)S(1)} %get-tuple-element.91.refs_0_.hi_ref, bf16[1024,1024]{1,0:T(8,128)(2,1)S(1)} %get-tuple-element.92.refs_1_.lo_ref, bf16[1024,256]{1,0:T(8,128)(2,1)S(1)} %get-tuple-element.100.rows_ref), custom_call_target="tpu_custom_call" | custom-call | flops 1073741824 | bytes 5242880 | tf_op jit(solution)/shard_map/share/pallas_call | solution.py:236
  64.2 1.9 %share.2.refs_3_ = f32[1024,256]{1,0:T(8,128)S(1)} custom-call(bf16[1024,1024]{1,0:T(8,128)(2,1)S(1)} %get-tuple-element.91.refs_0_.hi_ref, bf16[1024,1024]{1,0:T(8,128)(2,1)S(1)} %get-tuple-element.92.refs_1_.lo_ref, bf16[1024,256]{1,0:T(8,128)(2,1)S(1)} %get-tuple-element.99.rows_ref), custom_call_target="tpu_custom_call" | custom-call | flops 1073741824 | bytes 5242880 | tf_op jit(solution)/shard_map/share/pallas_call | solution.py:236
  66.2 2.6 %collective-permute-start.19 = (f32[384,128]{1,0:T(8,128)S(1)}, f32[384,128]{1,0:T(8,128)S(1)}, u32[]{:S(2)}, u32[]{:S(2)}) collective-permute-start(f32[384,128]{1,0:T(8,128)S(1)} %add.37), channel_id=1, source_target_pairs={{0,4},{1,5},{2,6},{3,7},{4,0},{5,1},{6,2},{7,3},{8,12},{9,13},{10,... | collective-permute-start | bytes 589832 | tf_op jit(solution)/shard_map/ppermute | solution.py:554
  68.8 7.1 %collective-permute-done.22.refs_2_ = bf16[1024,256]{1,0:T(8,128)(2,1)S(1)} collective-permute-done((bf16[1024,256]{1,0:T(8,128)(2,1)S(1)}, bf16[1024,256]{1,0:T(8,128)(2,1)S(1)}, u32[]{:S(2)}, u32[]{:S(2)}) %collective-permute-start.22) | collective-permute-done | bytes 524320 | tf_op jit(solution)/shard_map/ppermute | solution.py:505
  75.9 2.9 %grams.5 = (f32[512,256]{1,0:T(8,128)S(1)}, f32[512,256]{1,0:T(8,128)}, bf16[512,256]{1,0:T(8,128)(2,1)S(1)}, f32[8,1024]{1,0:T(8,128)S(1)}) custom-call(bf16[1024,1024]{1,0:T(8,128)(2,1)S(1)} %get-tuple-element.94.refs_4_.refs_0_.refs_3_, bf16[1024,1024]{1,0:T(8,128)(2,1)S(1)} %get-tuple-element.95.refs_5_.refs_1_.refs_4_, ...), custom_call_target="tpu_custom_call" | custom-call | flops 1073741824 | bytes 4718592 | tf_op jit(solution)/shard_map/grams/pallas_call | solution.py:279
  78.7 2.1 %collective-permute-start.30 = (bf16[512,256]{1,0:T(8,128)(2,1)S(1)}, bf16[512,256]{1,0:T(8,128)(2,1)S(1)}, u32[]{:S(2)}, u32[]{:S(2)}) collective-permute-start(bf16[512,256]{1,0:T(8,128)(2,1)S(1)} %get-tuple-element.111), channel_id=1, source_target_pairs={{0,2},{1,3},{2,0},{3,1},{4,6},{5,7},{6,4},{7,5},{8,10},{9,11},{10,... | collective-permute-start | bytes 786440 | tf_op jit(solution)/shard_map/ppermute | solution.py:552
  80.8 2.9 %grams.6 = (f32[512,256]{1,0:T(8,128)S(1)}, f32[512,256]{1,0:T(8,128)}, bf16[512,256]{1,0:T(8,128)(2,1)S(1)}, f32[8,1024]{1,0:T(8,128)S(1)}) custom-call(bf16[1024,1024]{1,0:T(8,128)(2,1)S(1)} %get-tuple-element.94.refs_4_.refs_0_.refs_3_, bf16[1024,1024]{1,0:T(8,128)(2,1)S(1)} %get-tuple-element.95.refs_5_.refs_1_.refs_4_, ...), custom_call_target="tpu_custom_call" | custom-call | flops 1073741824 | bytes 4718592 | tf_op jit(solution)/shard_map/grams/pallas_call | solution.py:279
  83.7 1.2 collective-permute-done.20.refs_5_
  85.0 4.8 %grams.7 = (f32[512,256]{1,0:T(8,128)S(1)}, f32[512,256]{1,0:T(8,128)}, bf16[512,256]{1,0:T(8,128)(2,1)S(1)}, f32[8,1024]{1,0:T(8,128)S(1)}) custom-call(bf16[1024,1024]{1,0:T(8,128)(2,1)S(1)} %get-tuple-element.91.refs_0_.hi_ref, bf16[1024,1024]{1,0:T(8,128)(2,1)S(1)} %get-tuple-element.92.refs_1_.lo_ref, bf16[1024,256]{1,0:T(8,128)(2,1)S(1)} %get-tuple-element.98.refs_2_, ...), custom_call_target="tpu_custom_call" | custom-call | flops 2147483648 | bytes 9437184 | tf_op jit(solution)/shard_map/grams/pallas_call | solution.py:279
  89.7 1.5 collective-permute-start.26
  91.8 5.0 %factor_first.1.in_ref = f32[256,512]{1,0:T(8,128)S(1)} custom-call(f32[768,128]{1,0:T(8,128)S(1)} %get-tuple-element.96.keep_ref, f32[768,128]{1,0:T(8,128)S(1)} %collective-permute-done.18.near_ref, f32[384,128]{1,0:T(8,128)S(1)} %collective-permute-done.19.far_ref), custom_call_target="tpu_custom_call" | custom-call | flops 10000000000 | bytes 1048576 | tf_op jit(solution)/shard_map/factor_first/pallas_call | solution.py:382
  96.8 2.6 %collective-permute-start.31 = (bf16[256,256]{1,0:T(8,128)(2,1)S(1)}, bf16[256,256]{1,0:T(8,128)(2,1)S(1)}, u32[]{:S(2)}, u32[]{:S(2)}) collective-permute-start(bf16[256,256]{1,0:T(8,128)(2,1)S(1)} %add.40), channel_id=1, source_target_pairs={{0,4},{1,5},{2,6},{3,7},{4,0},{5,1},{6,2},{7,3},{8,12},{9,13},{10,... | collective-permute-start | bytes 393224 | tf_op jit(solution)/shard_map/ppermute | solution.py:554
  99.4 5.6 %collective-permute-done.28.near_ref = bf16[512,256]{1,0:T(8,128)(2,1)S(1)} collective-permute-done((bf16[512,256]{1,0:T(8,128)(2,1)S(1)}, bf16[512,256]{1,0:T(8,128)(2,1)S(1)}, u32[]{:S(2)}, u32[]{:S(2)}) %collective-permute-start.28) | collective-permute-done | bytes 262176 | tf_op jit(solution)/shard_map/ppermute | solution.py:552
  105.0 1.5 collective-permute-start.29
  106.4 4.4 %factor_last.1 = (f32[256,1024]{1,0:T(8,128)S(1)}, f32[256,256]{1,0:T(8,128)S(1)}, f32[8,1536]{1,0:T(8,128)S(1)}) custom-call(f32[256,512]{1,0:T(8,128)S(1)} %factor_first.1.in_ref, f32[8,1024]{1,0:T(8,128)S(1)} %get-tuple-element.103.squares_ref), custom_call_target="tpu_custom_call" | custom-call | flops 10000000000 | bytes 1048576 | tf_op jit(solution)/shard_map/factor_last/pallas_call | solution.py:400
  111.8 1.9 %collective-permute-start.27 = (bf16[256,256]{1,0:T(8,128)(2,1)S(1)}, bf16[256,256]{1,0:T(8,128)(2,1)S(1)}, u32[]{:S(2)}, u32[]{:S(2)}) collective-permute-start(bf16[256,256]{1,0:T(8,128)(2,1)S(1)} %add.38), channel_id=1, source_target_pairs={{0,4},{1,5},{2,6},{3,7},{4,0},{5,1},{6,2},{7,3},{8,12},{9,13},{10,... | collective-permute-start | bytes 393224 | tf_op jit(solution)/shard_map/ppermute | solution.py:554
  114.7 2.2 %collective-permute-done.25.refs_3_ = f32[8,1536]{1,0:T(8,128)S(1)} collective-permute-done((f32[8,1536]{1,0:T(8,128)S(1)}, f32[8,1536]{1,0:T(8,128)S(1)}, u32[]{:S(2)}, u32[]{:S(2)}) %collective-permute-start.25) | collective-permute-done | bytes 49184 | tf_op jit(solution)/shard_map/ppermute | solution.py:560
  116.9 2.2 %collective-permute-start.23 = (f32[8,1536]{1,0:T(8,128)S(1)}, f32[8,1536]{1,0:T(8,128)}, u32[]{:S(2)}, u32[]{:S(2)}) collective-permute-start(f32[8,1536]{1,0:T(8,128)S(1)} %get-tuple-element.104.refs_0_), channel_id=1, source_target_pairs={{0,2},{1,3},{2,0},{3,1},{4,6},{5,7},{6,4},{7,5},{8,10},{9,11},{10,... | collective-permute-start | bytes 147464 | tf_op jit(solution)/shard_map/ppermute | solution.py:560
  119.1 1.9 %collective-permute-done.24.refs_2_ = f32[8,1536]{1,0:T(8,128)S(1)} collective-permute-done((f32[8,1536]{1,0:T(8,128)S(1)}, f32[8,1536]{1,0:T(8,128)S(1)}, u32[]{:S(2)}, u32[]{:S(2)}) %collective-permute-start.24) | collective-permute-done | bytes 49184 | tf_op jit(solution)/shard_map/ppermute | solution.py:560
  121.7 1.6 judge.1
  125.4 60.8 %conditional.1 = (f32[256,1024]{1,0:T(8,128)S(1)}) conditional(s32[]{:T(128)} %bitcast.6, (f32[256,256]{1,0:T(8,128)S(1)}, f32[512,256]{1,0:T(8,128)S(1)}, bf16[512,256]{1,0:T(8,128)(2,1)S(1)}, bf16[256,256]{1,0:T(8,128)(2,1)S(1)}, f32[256,1024]{1,0:T(8,128)S(1)}) %tuple.21, (f32[512,256]{1,0:T(8,128)}, f32[512,256]{1,0:T(8,128)S(1)}, ...), branch_computations={%region_0.1_spmd, %region_1.2_spmd} | conditional | flops 604176384 | bytes 19923248 | solution.py:575
  125.4 1.7 collective-permute-start.4
  127.4 1.7 collective-permute-start
  129.1 14.1 %collective-permute-done.4.near_ref = f32[512,256]{1,0:T(8,128)S(1)} collective-permute-done((f32[512,256]{1,0:T(8,128)}, f32[512,256]{1,0:T(8,128)S(1)}, u32[]{:S(2)}, u32[]{:S(2)}) %collective-permute-start.4) | collective-permute-done | bytes 524320 | tf_op jit(solution)/shard_map/cond/branch_1_fun/ppermute | solution.py:570
  143.7 16.4 %collective-permute-done.2.near_ref = f32[512,256]{1,0:T(8,128)S(1)} collective-permute-done((f32[512,256]{1,0:T(8,128)}, f32[512,256]{1,0:T(8,128)S(1)}, u32[]{:S(2)}, u32[]{:S(2)}) %collective-permute-start.2) | collective-permute-done | bytes 524320 | tf_op jit(solution)/shard_map/cond/branch_1_fun/ppermute | solution.py:570
  160.2 7.8 %collective-permute-done.near_ref = f32[512,256]{1,0:T(8,128)S(1)} collective-permute-done((f32[512,256]{1,0:T(8,128)}, f32[512,256]{1,0:T(8,128)S(1)}, u32[]{:S(2)}, u32[]{:S(2)}) %collective-permute-start) | collective-permute-done | bytes 524320 | tf_op jit(solution)/shard_map/cond/branch_1_fun/ppermute | solution.py:570
  168.0 1.7 collective-permute-start.1
  170.1 12.6 %collective-permute-done.3.far_ref = f32[256,256]{1,0:T(8,128)S(1)} collective-permute-done((f32[256,256]{1,0:T(8,128)S(1)}, f32[256,256]{1,0:T(8,128)S(1)}, u32[]{:S(2)}, u32[]{:S(2)}) %collective-permute-start.3) | collective-permute-done | bytes 262176 | tf_op jit(solution)/shard_map/cond/branch_1_fun/ppermute | solution.py:571
  183.1 2.7 %collective-permute-done.1.far_ref = f32[256,256]{1,0:T(8,128)S(1)} collective-permute-done((f32[256,256]{1,0:T(8,128)S(1)}, f32[256,256]{1,0:T(8,128)S(1)}, u32[]{:S(2)}, u32[]{:S(2)}) %collective-permute-start.1) | collective-permute-done | bytes 262176 | tf_op jit(solution)/shard_map/cond/branch_1_fun/ppermute | solution.py:571
  (82 shorter events, 16.8 us)
Async XLA Ops:
  3.4 6.0 %copy-start.10 = (bf16[1024,256]{1,0:T(8,128)(2,1)S(1)}, bf16[1024,256]{1,0:T(8,128)(2,1)}, u32[]{:S(2)}) copy-start(bf16[1024,256]{1,0:T(8,128)(2,1)} %mix.3) | copy-start | bytes 1572868
  3.4 6.0 %collective-permute-start.12 = (bf16[1024,256]{1,0:T(8,128)(2,1)}, bf16[1024,256]{1,0:T(8,128)(2,1)S(1)}, u32[]{:S(2)}, u32[]{:S(2)}) collective-permute-start(bf16[1024,256]{1,0:T(8,128)(2,1)} %mix.3), channel_id=1, source_target_pairs={{0,8},{8,0},{16,24},{24,16},{1,9},{9,1},{17,25},{25,17},{2,10},{10... | collective-permute-start | bytes 1572872 | tf_op jit(solution)/shard_map/ppermute | solution.py:520
  8.8 7.1 %copy-start.11 = (bf16[1024,256]{1,0:T(8,128)(2,1)S(1)}, bf16[1024,256]{1,0:T(8,128)(2,1)}, u32[]{:S(2)}) copy-start(bf16[1024,256]{1,0:T(8,128)(2,1)} %get-tuple-element.81) | copy-start | bytes 1572868
  8.8 3.9 %collective-permute-start.10 = (bf16[1024,256]{1,0:T(8,128)(2,1)}, bf16[1024,256]{1,0:T(8,128)(2,1)S(1)}, u32[]{:S(2)}, u32[]{:S(2)}) collective-permute-start(bf16[1024,256]{1,0:T(8,128)(2,1)} %get-tuple-element.82), channel_id=1, source_target_pairs={{0,8},{8,0},{16,24},{24,16},{1,9},{9,1},{17,25},{25,17},{2,10},{10... | collective-permute-start | bytes 1572872 | tf_op jit(solution)/shard_map/ppermute | solution.py:514
  8.9 7.1 %collective-permute-start.8 = (bf16[1024,256]{1,0:T(8,128)(2,1)}, bf16[1024,256]{1,0:T(8,128)(2,1)}, u32[]{:S(2)}, u32[]{:S(2)}) collective-permute-start(bf16[1024,256]{1,0:T(8,128)(2,1)} %get-tuple-element.81), channel_id=1, source_target_pairs={{0,8},{8,0},{16,24},{24,16},{1,9},{9,1},{17,25},{25,17},{2,10},{10... | collective-permute-start | bytes 1572872 | tf_op jit(solution)/shard_map/ppermute | solution.py:514
  9.3 18.9 %collective-permute-start.6 = (bf16[1024,256]{1,0:T(8,128)(2,1)}, bf16[1024,256]{1,0:T(8,128)(2,1)}, u32[]{:S(2)}, u32[]{:S(2)}) collective-permute-start(bf16[1024,256]{1,0:T(8,128)(2,1)} %get-tuple-element.80), channel_id=1, source_target_pairs={{0,8},{8,0},{16,24},{24,16},{1,9},{9,1},{17,25},{25,17},{2,10},{10... | collective-permute-start | bytes 1572872 | tf_op jit(solution)/shard_map/ppermute | solution.py:514
  9.6 10.2 %collective-permute-start.14 = (bf16[1024,128]{1,0:T(8,128)(2,1)S(1)}, bf16[1024,128]{1,0:T(8,128)(2,1)S(1)}, u32[]{:S(2)}, u32[]{:S(2)}) collective-permute-start(bf16[1024,128]{1,0:T(8,128)(2,1)S(1)} %get-tuple-element.116.own_ref), channel_id=1, source_target_pairs={{0,16},{8,24},{16,0},{24,8},{1,17},{9,25},{17,1},{25,9},{2,18},{10... | collective-permute-start | bytes 786440 | tf_op jit(solution)/shard_map/ppermute | solution.py:501
  12.6 12.8 %collective-permute-start.13 = (bf16[1024,128]{1,0:T(8,128)(2,1)S(1)}, bf16[1024,128]{1,0:T(8,128)(2,1)S(1)}, u32[]{:S(2)}, u32[]{:S(2)}) collective-permute-start(bf16[1024,128]{1,0:T(8,128)(2,1)S(1)} %get-tuple-element.117.own_ref), channel_id=1, source_target_pairs={{0,16},{8,24},{16,0},{24,8},{1,17},{9,25},{17,1},{25,9},{2,18},{10... | collective-permute-start | bytes 786440 | tf_op jit(solution)/shard_map/ppermute | solution.py:501
  13.9 22.7 %collective-permute-start.11 = (bf16[1024,256]{1,0:T(8,128)(2,1)S(1)}, bf16[1024,256]{1,0:T(8,128)(2,1)S(1)}, u32[]{:S(2)}, u32[]{:S(2)}) collective-permute-start(bf16[1024,256]{1,0:T(8,128)(2,1)S(1)} %multiply_convert_fusion.own_ref), channel_id=1, source_target_pairs={{0,16},{8,24},{16,0},{24,8},{1,17},{9,25},{17,1},{25,9},{2,18},{10... | collective-permute-start | bytes 1572872 | tf_op jit(solution)/shard_map/ppermute | solution.py:501
  17.2 30.8 %collective-permute-start.9 = (bf16[1024,256]{1,0:T(8,128)(2,1)S(1)}, bf16[1024,256]{1,0:T(8,128)(2,1)}, u32[]{:S(2)}, u32[]{:S(2)}) collective-permute-start(bf16[1024,256]{1,0:T(8,128)(2,1)S(1)} %multiply_convert_fusion.1.own_ref), channel_id=1, source_target_pairs={{0,16},{8,24},{16,0},{24,8},{1,17},{9,25},{17,1},{25,9},{2,18},{10... | collective-permute-start | bytes 1572872 | tf_op jit(solution)/shard_map/ppermute | solution.py:501
  25.4 6.4 %copy-start.1 = (s32[2048]{0:T(1024)S(1)}, s32[2048]{0:T(1024)}, u32[]{:S(2)}) copy-start(s32[2048]{0:T(1024)} %param.9) | copy-start | bytes 24580
  25.4 6.4 %copy-start.2 = (s32[2048,1]{0,1:T(1,128)S(1)}, s32[2048,1]{0,1:T(1,128)}, u32[]{:S(2)}) copy-start(s32[2048,1]{0,1:T(1,128)} %param.10) | copy-start | bytes 24580
  26.2 25.7 %collective-permute-start.17 = (bf16[1024,128]{1,0:T(8,128)(2,1)S(1)}, bf16[1024,128]{1,0:T(8,128)(2,1)S(1)}, u32[]{:S(2)}, u32[]{:S(2)}) collective-permute-start(bf16[1024,128]{1,0:T(8,128)(2,1)S(1)} %get-tuple-element.90.right_ref.refs_3_), channel_id=1, source_target_pairs={{0,1},{1,0},{2,3},{3,2},{4,5},{5,4},{6,7},{7,6},{8,9},{9,8},{10,11... | collective-permute-start | bytes 786440 | tf_op jit(solution)/shard_map/ppermute | solution.py:505
  28.2 23.7 %collective-permute-start.16 = (bf16[1024,128]{1,0:T(8,128)(2,1)S(1)}, bf16[1024,128]{1,0:T(8,128)(2,1)S(1)}, u32[]{:S(2)}, u32[]{:S(2)}) collective-permute-start(bf16[1024,128]{1,0:T(8,128)(2,1)S(1)} %get-tuple-element.89.left_ref.refs_2_), channel_id=1, source_target_pairs={{0,1},{1,0},{2,3},{3,2},{4,5},{5,4},{6,7},{7,6},{8,9},{9,8},{10,11... | collective-permute-start | bytes 786440 | tf_op jit(solution)/shard_map/ppermute | solution.py:505
  29.6 29.3 %collective-permute-start.7 = (bf16[1024,256]{1,0:T(8,128)(2,1)S(1)}, bf16[1024,256]{1,0:T(8,128)(2,1)}, u32[]{:S(2)}, u32[]{:S(2)}) collective-permute-start(bf16[1024,256]{1,0:T(8,128)(2,1)S(1)} %multiply_convert_fusion.2.own_ref), channel_id=1, source_target_pairs={{0,16},{8,24},{16,0},{24,8},{1,17},{9,25},{17,1},{25,9},{2,18},{10... | collective-permute-start | bytes 1572872 | tf_op jit(solution)/shard_map/ppermute | solution.py:501
  36.6 15.2 %collective-permute-start.15 = (f32[4,1024]{1,0:T(4,128)S(1)}, f32[4,1024]{1,0:T(4,128)S(1)}, u32[]{:S(2)}, u32[]{:S(2)}) collective-permute-start(f32[4,1024]{1,0:T(4,128)S(1)} %get-tuple-element.93), channel_id=1, source_target_pairs={{0,1},{1,0},{2,3},{3,2},{4,5},{5,4},{6,7},{7,6},{8,9},{9,8},{10,11... | collective-permute-start | bytes 49160 | tf_op jit(solution)/shard_map/ppermute | solution.py:529
  49.8 31.0 %collective-permute-start.21 = (bf16[1024,256]{1,0:T(8,128)(2,1)S(1)}, bf16[1024,256]{1,0:T(8,128)(2,1)S(1)}, u32[]{:S(2)}, u32[]{:S(2)}) collective-permute-start(bf16[1024,256]{1,0:T(8,128)(2,1)S(1)} %get-tuple-element.99.rows_ref), channel_id=1, source_target_pairs={{0,1},{1,0},{2,3},{3,2},{4,5},{5,4},{6,7},{7,6},{8,9},{9,8},{10,11... | collective-permute-start | bytes 1572872 | tf_op jit(solution)/shard_map/ppermute | solution.py:505
  51.8 24.0 %collective-permute-start.22 = (bf16[1024,256]{1,0:T(8,128)(2,1)S(1)}, bf16[1024,256]{1,0:T(8,128)(2,1)S(1)}, u32[]{:S(2)}, u32[]{:S(2)}) collective-permute-start(bf16[1024,256]{1,0:T(8,128)(2,1)S(1)} %get-tuple-element.100.rows_ref), channel_id=1, source_target_pairs={{0,1},{1,0},{2,3},{3,2},{4,5},{5,4},{6,7},{7,6},{8,9},{9,8},{10,11... | collective-permute-start | bytes 1572872 | tf_op jit(solution)/shard_map/ppermute | solution.py:505
  56.8 9.3 %collective-permute-start.18 = (f32[768,128]{1,0:T(8,128)S(1)}, f32[768,128]{1,0:T(8,128)S(1)}, u32[]{:S(2)}, u32[]{:S(2)}) collective-permute-start(f32[768,128]{1,0:T(8,128)S(1)} %get-tuple-element.97), channel_id=1, source_target_pairs={{0,2},{1,3},{2,0},{3,1},{4,6},{5,7},{6,4},{7,5},{8,10},{9,11},{10,... | collective-permute-start | bytes 1179656 | tf_op jit(solution)/shard_map/ppermute | solution.py:552
  60.8 24.2 %collective-permute-start.20 = (bf16[1024,256]{1,0:T(8,128)(2,1)S(1)}, bf16[1024,256]{1,0:T(8,128)(2,1)S(1)}, u32[]{:S(2)}, u32[]{:S(2)}) collective-permute-start(bf16[1024,256]{1,0:T(8,128)(2,1)S(1)} %get-tuple-element.98.refs_2_), channel_id=1, source_target_pairs={{0,1},{1,0},{2,3},{3,2},{4,5},{5,4},{6,7},{7,6},{8,9},{9,8},{10,11... | collective-permute-start | bytes 1572872 | tf_op jit(solution)/shard_map/ppermute | solution.py:505
  66.2 25.6 %collective-permute-start.19 = (f32[384,128]{1,0:T(8,128)S(1)}, f32[384,128]{1,0:T(8,128)S(1)}, u32[]{:S(2)}, u32[]{:S(2)}) collective-permute-start(f32[384,128]{1,0:T(8,128)S(1)} %add.37), channel_id=1, source_target_pairs={{0,4},{1,5},{2,6},{3,7},{4,0},{5,1},{6,2},{7,3},{8,12},{9,13},{10,... | collective-permute-start | bytes 589832 | tf_op jit(solution)/shard_map/ppermute | solution.py:554
  78.7 18.0 %collective-permute-start.30 = (bf16[512,256]{1,0:T(8,128)(2,1)S(1)}, bf16[512,256]{1,0:T(8,128)(2,1)S(1)}, u32[]{:S(2)}, u32[]{:S(2)}) collective-permute-start(bf16[512,256]{1,0:T(8,128)(2,1)S(1)} %get-tuple-element.111), channel_id=1, source_target_pairs={{0,2},{1,3},{2,0},{3,1},{4,6},{5,7},{6,4},{7,5},{8,10},{9,11},{10,... | collective-permute-start | bytes 786440 | tf_op jit(solution)/shard_map/ppermute | solution.py:552
  83.7 21.2 %copy-start.4 = (f32[512,256]{1,0:T(8,128)}, f32[512,256]{1,0:T(8,128)S(1)}, u32[]{:S(2)}) copy-start(f32[512,256]{1,0:T(8,128)S(1)} %get-tuple-element.108.keep_ref) | copy-start | bytes 1572868
  89.7 22.0 %copy-start.6 = (f32[512,256]{1,0:T(8,128)}, f32[512,256]{1,0:T(8,128)S(1)}, u32[]{:S(2)}) copy-start(f32[512,256]{1,0:T(8,128)S(1)} %get-tuple-element.106.keep_ref) | copy-start | bytes 1572868
  89.7 22.0 %collective-permute-start.26 = (bf16[512,256]{1,0:T(8,128)(2,1)S(1)}, bf16[512,256]{1,0:T(8,128)(2,1)S(1)}, u32[]{:S(2)}, u32[]{:S(2)}) collective-permute-start(bf16[512,256]{1,0:T(8,128)(2,1)S(1)} %get-tuple-element.107), channel_id=1, source_target_pairs={{0,2},{1,3},{2,0},{3,1},{4,6},{5,7},{6,4},{7,5},{8,10},{9,11},{10,... | collective-permute-start | bytes 786440 | tf_op jit(solution)/shard_map/ppermute | solution.py:552
  91.3 13.7 %collective-permute-start.28 = (bf16[512,256]{1,0:T(8,128)(2,1)S(1)}, bf16[512,256]{1,0:T(8,128)(2,1)S(1)}, u32[]{:S(2)}, u32[]{:S(2)}) collective-permute-start(bf16[512,256]{1,0:T(8,128)(2,1)S(1)} %get-tuple-element.109), channel_id=1, source_target_pairs={{0,2},{1,3},{2,0},{3,1},{4,6},{5,7},{6,4},{7,5},{8,10},{9,11},{10,... | collective-permute-start | bytes 786440 | tf_op jit(solution)/shard_map/ppermute | solution.py:552
  96.8 27.1 %collective-permute-start.31 = (bf16[256,256]{1,0:T(8,128)(2,1)S(1)}, bf16[256,256]{1,0:T(8,128)(2,1)S(1)}, u32[]{:S(2)}, u32[]{:S(2)}) collective-permute-start(bf16[256,256]{1,0:T(8,128)(2,1)S(1)} %add.40), channel_id=1, source_target_pairs={{0,4},{1,5},{2,6},{3,7},{4,0},{5,1},{6,2},{7,3},{8,12},{9,13},{10,... | collective-permute-start | bytes 393224 | tf_op jit(solution)/shard_map/ppermute | solution.py:554
  105.0 19.4 %collective-permute-start.29 = (bf16[256,256]{1,0:T(8,128)(2,1)S(1)}, bf16[256,256]{1,0:T(8,128)(2,1)S(1)}, u32[]{:S(2)}, u32[]{:S(2)}) collective-permute-start(bf16[256,256]{1,0:T(8,128)(2,1)S(1)} %add.39), channel_id=1, source_target_pairs={{0,4},{1,5},{2,6},{3,7},{4,0},{5,1},{6,2},{7,3},{8,12},{9,13},{10,... | collective-permute-start | bytes 393224 | tf_op jit(solution)/shard_map/ppermute | solution.py:554
  110.8 10.8 %copy-start = (f32[8,1536]{1,0:T(8,128)}, f32[8,1536]{1,0:T(8,128)S(1)}, u32[]{:S(2)}) copy-start(f32[8,1536]{1,0:T(8,128)S(1)} %get-tuple-element.104.refs_0_) | copy-start | bytes 147460
  110.9 6.1 %collective-permute-start.25 = (f32[8,1536]{1,0:T(8,128)S(1)}, f32[8,1536]{1,0:T(8,128)S(1)}, u32[]{:S(2)}, u32[]{:S(2)}) collective-permute-start(f32[8,1536]{1,0:T(8,128)S(1)} %get-tuple-element.104.refs_0_), channel_id=1, source_target_pairs={{0,6},{1,7},{2,4},{3,5},{4,2},{5,3},{6,0},{7,1},{8,14},{9,15},{10,... | collective-permute-start | bytes 147464 | tf_op jit(solution)/shard_map/ppermute | solution.py:560
  111.8 13.1 %collective-permute-start.27 = (bf16[256,256]{1,0:T(8,128)(2,1)S(1)}, bf16[256,256]{1,0:T(8,128)(2,1)S(1)}, u32[]{:S(2)}, u32[]{:S(2)}) collective-permute-start(bf16[256,256]{1,0:T(8,128)(2,1)S(1)} %add.38), channel_id=1, source_target_pairs={{0,4},{1,5},{2,6},{3,7},{4,0},{5,1},{6,2},{7,3},{8,12},{9,13},{10,... | collective-permute-start | bytes 393224 | tf_op jit(solution)/shard_map/ppermute | solution.py:554
  113.7 7.4 %collective-permute-start.24 = (f32[8,1536]{1,0:T(8,128)S(1)}, f32[8,1536]{1,0:T(8,128)S(1)}, u32[]{:S(2)}, u32[]{:S(2)}) collective-permute-start(f32[8,1536]{1,0:T(8,128)S(1)} %get-tuple-element.104.refs_0_), channel_id=1, source_target_pairs={{0,4},{1,5},{2,6},{3,7},{4,0},{5,1},{6,2},{7,3},{8,12},{9,13},{10,... | collective-permute-start | bytes 147464 | tf_op jit(solution)/shard_map/ppermute | solution.py:560
  116.9 4.8 %copy-start.12 = (f32[8,1536]{1,0:T(8,128)}, f32[8,1536]{1,0:T(8,128)S(1)}, u32[]{:S(2)}) copy-start(f32[8,1536]{1,0:T(8,128)S(1)} %collective-permute-done.25.refs_3_) | copy-start | bytes 147460
  116.9 4.8 %collective-permute-start.23 = (f32[8,1536]{1,0:T(8,128)S(1)}, f32[8,1536]{1,0:T(8,128)}, u32[]{:S(2)}, u32[]{:S(2)}) collective-permute-start(f32[8,1536]{1,0:T(8,128)S(1)} %get-tuple-element.104.refs_0_), channel_id=1, source_target_pairs={{0,2},{1,3},{2,0},{3,1},{4,6},{5,7},{6,4},{7,5},{8,10},{9,11},{10,... | collective-permute-start | bytes 147464 | tf_op jit(solution)/shard_map/ppermute | solution.py:560
  121.1 0.6 copy-start.13
  123.2 1.1 copy-start.5
  124.4 1.0 copy-start.7
  125.4 2.0 %copy-start.8 = (f32[512,256]{1,0:T(8,128)}, f32[512,256]{1,0:T(8,128)S(1)}, u32[]{:S(2)}) copy-start(f32[512,256]{1,0:T(8,128)S(1)} %get-tuple-element.35.keep_ref) | copy-start | bytes 1572868 | tf_op jit(solution)/shard_map/cond
  125.4 17.8 %collective-permute-start.4 = (f32[512,256]{1,0:T(8,128)}, f32[512,256]{1,0:T(8,128)S(1)}, u32[]{:S(2)}, u32[]{:S(2)}) collective-permute-start(f32[512,256]{1,0:T(8,128)} %get-tuple-element.40), channel_id=1, source_target_pairs={{0,2},{1,3},{2,0},{3,1},{4,6},{5,7},{6,4},{7,5},{8,10},{9,11},{10,... | collective-permute-start | bytes 1572872 | tf_op jit(solution)/shard_map/cond/branch_1_fun/ppermute | solution.py:570
  127.1 33.0 %collective-permute-start.2 = (f32[512,256]{1,0:T(8,128)}, f32[512,256]{1,0:T(8,128)S(1)}, u32[]{:S(2)}, u32[]{:S(2)}) collective-permute-start(f32[512,256]{1,0:T(8,128)} %get-tuple-element.38), channel_id=1, source_target_pairs={{0,2},{1,3},{2,0},{3,1},{4,6},{5,7},{6,4},{7,5},{8,10},{9,11},{10,... | collective-permute-start | bytes 1572872 | tf_op jit(solution)/shard_map/cond/branch_1_fun/ppermute | solution.py:570
  127.4 40.5 %copy-start.9 = (f32[512,256]{1,0:T(8,128)S(1)}, f32[512,256]{1,0:T(8,128)}, u32[]{:S(2)}) copy-start(f32[512,256]{1,0:T(8,128)} %copy-done.8) | copy-start | bytes 1572868 | tf_op jit(solution)/shard_map/cond
  127.4 40.5 %collective-permute-start = (f32[512,256]{1,0:T(8,128)}, f32[512,256]{1,0:T(8,128)S(1)}, u32[]{:S(2)}, u32[]{:S(2)}) collective-permute-start(f32[512,256]{1,0:T(8,128)} %get-tuple-element.36), channel_id=1, source_target_pairs={{0,2},{1,3},{2,0},{3,1},{4,6},{5,7},{6,4},{7,5},{8,10},{9,11},{10,... | collective-permute-start | bytes 1572872 | tf_op jit(solution)/shard_map/cond/branch_1_fun/ppermute | solution.py:570
  143.3 26.4 %collective-permute-start.5 = (f32[256,256]{1,0:T(8,128)S(1)}, f32[256,256]{1,0:T(8,128)S(1)}, u32[]{:S(2)}, u32[]{:S(2)}) collective-permute-start(f32[256,256]{1,0:T(8,128)S(1)} %add.36), channel_id=1, source_target_pairs={{0,4},{1,5},{2,6},{3,7},{4,0},{5,1},{6,2},{7,3},{8,12},{9,13},{10,... | collective-permute-start | bytes 786440 | tf_op jit(solution)/shard_map/cond/branch_1_fun/ppermute | solution.py:571
  160.1 22.6 %collective-permute-start.3 = (f32[256,256]{1,0:T(8,128)S(1)}, f32[256,256]{1,0:T(8,128)S(1)}, u32[]{:S(2)}, u32[]{:S(2)}) collective-permute-start(f32[256,256]{1,0:T(8,128)S(1)} %add.35), channel_id=1, source_target_pairs={{0,4},{1,5},{2,6},{3,7},{4,0},{5,1},{6,2},{7,3},{8,12},{9,13},{10,... | collective-permute-start | bytes 786440 | tf_op jit(solution)/shard_map/cond/branch_1_fun/ppermute | solution.py:571
  168.0 17.8 %collective-permute-start.1 = (f32[256,256]{1,0:T(8,128)S(1)}, f32[256,256]{1,0:T(8,128)S(1)}, u32[]{:S(2)}, u32[]{:S(2)}) collective-permute-start(f32[256,256]{1,0:T(8,128)S(1)} %add.34), channel_id=1, source_target_pairs={{0,4},{1,5},{2,6},{3,7},{4,0},{5,1},{6,2},{7,3},{8,12},{9,13},{10,... | collective-permute-start | bytes 786440 | tf_op jit(solution)/shard_map/cond/branch_1_fun/ppermute | solution.py:571
  186.2 1.0 copy-start.3

commit v5 on v4

--- a/solution.py
+++ b/solution.py
@@ -369,11 +369,10 @@
     inverse = jnp.where(ri >= ci, work[:, PANEL:], 0.0)
     out_ref[...] = upper
     inverse_ref[...] = inverse
-    guard_ref[:, : NZ * PANEL] = squares_ref[...]
+    guard_ref[:, : NZ * PANEL] = squares_ref[:1, :]
     for place, part in enumerate((inverse, upper)):
         start = (NZ + place) * PANEL
-        norms = jnp.sum(part * part, axis=0, keepdims=True)
-        guard_ref[:, start : start + PANEL] = jnp.broadcast_to(norms, (8, PANEL))
+        guard_ref[:, start : start + PANEL] = jnp.sum(part * part, axis=0, keepdims=True)
 
 
 def factor_first(keep, near, far, scale):
@@ -396,7 +395,7 @@
     def resident(shape):
         return pl.BlockSpec(shape, lambda i: (0, 0))
 
-    square, guard = (PANEL, PANEL), (8, (NZ + 2) * PANEL)
+    square, guard = (PANEL, PANEL), (1, (NZ + 2) * PANEL)
     return pl.pallas_call(
         factor_last_kernel,
         grid=(1,),
@@ -447,7 +446,7 @@
         copy.start()
     for copy in copies:
         copy.wait()
-    worst = jnp.zeros((8, 1), F32)
+    worst = jnp.zeros((1, 1), F32)
     for owner in range(NZ):
         terms = []
         for sender in range(NZ):

time: 188 us -> 184 us (0.979)
  starting transfers between devices: 40.8 us -> 35.2 us
  transfers between devices with their start and end apart: 32 -> 32, of which waited for: 16 -> 18; matrix products, arithmetic and copies ran while one was open for 2% -> 2% of each run, Pallas kernels for 25% -> 25%
where the time goes in v5:
time: 184 us; the launch traced here: 183 us
  waiting for transfers between devices  91.3 us (50%)
  Pallas kernels  49 us (27%)
  starting transfers between devices  35.2 us (19%)
  other arithmetic  4.14 us (2%)
  local copies, waits for them, and re-layouts  2.25 us (1%)
    ppermute x3, waiting for transfers between devices, exact(): near = lax.ppermute(send, 'blk', z_route(1))  37.2 us
    ppermute x5, waiting for transfers between devices, last_level(): lax.ppermute(own, 'wide', [(w, w ^ wide // 2) for w in range(wide)])  17.7 us
    ppermute x3, waiting for transfers between devices, exact(): far = lax.ppermute(far_sum(keep, near), 'blk', z_route(2))  16.4 us
    pallas_call x4, Pallas kernels, partial_grams(): pl.pallas_call(functools.partial(gram_kernel, parts, packed, each, begun...  14.3 us
    ppermute x5, waiting for transfers between devices, last_level(): pieces.append(lax.ppermute(own, 'blk', x_shift(s)))  8.34 us
    pallas_call x2, Pallas kernels, mix_columns(): pl.pallas_call(mix_kernel, grid=(count,), in_specs=[pl.BlockSpec((1, rows...  7.67 us
    ppermute x5, starting transfers between devices, last_level(): lax.ppermute(own, 'wide', [(w, w ^ wide // 2) for w in range(wide)])  7.34 us
    ppermute x4, starting transfers between devices, per_device(): far = lax.ppermute(onward, 'blk', z_route(2))  6.66 us
  transfers between devices with their start and end apart: 32, of which 18 were waited for; matrix products, arithmetic and copies ran while one was open for 2% of the time, Pallas kernels for 25%

profile of v5, /device:TPU:0, one launch (start us, length us, event | category | flops | bytes accessed | tf_op | source)
XLA Modules:
  0.0 183.4 jit_solution(5964495978263724222)
XLA Ops:
  0.6 2.8 %mix.3 = bf16[1024,256]{1,0:T(8,128)(2,1)} custom-call(s32[1,1024]{1,0:T(1,128)} %bitcast.9, bf16[256,256]{1,0:T(8,128)(2,1)} %constant.25.clone.had_ref, f32[1024,1024]{1,0:T(8,128)} %x_ref.3), custom_call_target="tpu_custom_call" | custom-call | flops 402653184 | bytes 1572864 | tf_op jit(solution)/shard_map/mix/pallas_call | solution.py:67
  3.9 4.9 %mix.2 = (bf16[1024,256]{1,0:T(8,128)(2,1)}, bf16[1024,256]{1,0:T(8,128)(2,1)}, bf16[1024,256]{1,0:T(8,128)(2,1)}) custom-call(s32[1,1024]{1,0:T(1,128)} %bitcast.10, bf16[256,256]{1,0:T(8,128)(2,1)} %constant.25.clone.had_ref, f32[1024,1024]{1,0:T(8,128)} %x_ref.3), custom_call_target="tpu_custom_call" | custom-call | flops 1207959552 | bytes 4718592 | tf_op jit(solution)/shard_map/mix/pallas_call | solution.py:67
  9.6 3.0 %collective-permute-start.14 = (bf16[1024,128]{1,0:T(8,128)(2,1)S(1)}, bf16[1024,128]{1,0:T(8,128)(2,1)S(1)}, u32[]{:S(2)}, u32[]{:S(2)}) collective-permute-start(bf16[1024,128]{1,0:T(8,128)(2,1)S(1)} %get-tuple-element.116.own_ref), channel_id=1, source_target_pairs={{0,16},{8,24},{16,0},{24,8},{1,17},{9,25},{17,1},{25,9},{2,18},{10... | collective-permute-start | bytes 786440 | tf_op jit(solution)/shard_map/ppermute | solution.py:500
  12.7 1.2 multiply_convert_fusion.own_ref
  13.9 2.0 %collective-permute-start.11 = (bf16[1024,256]{1,0:T(8,128)(2,1)S(1)}, bf16[1024,256]{1,0:T(8,128)(2,1)S(1)}, u32[]{:S(2)}, u32[]{:S(2)}) collective-permute-start(bf16[1024,256]{1,0:T(8,128)(2,1)S(1)} %multiply_convert_fusion.own_ref), channel_id=1, source_target_pairs={{0,16},{8,24},{16,0},{24,8},{1,17},{9,25},{17,1},{25,9},{2,18},{10... | collective-permute-start | bytes 1572872 | tf_op jit(solution)/shard_map/ppermute | solution.py:500
  15.9 1.2 multiply_convert_fusion.1.own_ref
  17.3 2.4 %collective-permute-done.14.other_ref = bf16[1024,128]{1,0:T(8,128)(2,1)S(1)} collective-permute-done((bf16[1024,128]{1,0:T(8,128)(2,1)S(1)}, bf16[1024,128]{1,0:T(8,128)(2,1)S(1)}, u32[]{:S(2)}, u32[]{:S(2)}) %collective-permute-start.14) | collective-permute-done | bytes 262176 | tf_op jit(solution)/shard_map/ppermute | solution.py:500
  20.5 4.8 %collective-permute-done.13.other_ref = bf16[1024,128]{1,0:T(8,128)(2,1)S(1)} collective-permute-done((bf16[1024,128]{1,0:T(8,128)(2,1)S(1)}, bf16[1024,128]{1,0:T(8,128)(2,1)S(1)}, u32[]{:S(2)}, u32[]{:S(2)}) %collective-permute-start.13) | collective-permute-done | bytes 262176 | tf_op jit(solution)/shard_map/ppermute | solution.py:500
  26.2 2.0 %collective-permute-start.17 = (bf16[1024,128]{1,0:T(8,128)(2,1)S(1)}, bf16[1024,128]{1,0:T(8,128)(2,1)S(1)}, u32[]{:S(2)}, u32[]{:S(2)}) collective-permute-start(bf16[1024,128]{1,0:T(8,128)(2,1)S(1)} %get-tuple-element.90.right_ref.refs_3_), channel_id=1, source_target_pairs={{0,1},{1,0},{2,3},{3,2},{4,5},{5,4},{6,7},{7,6},{8,9},{9,8},{10,11... | collective-permute-start | bytes 786440 | tf_op jit(solution)/shard_map/ppermute | solution.py:504
  28.2 1.4 multiply_convert_fusion.2.own_ref
  29.6 2.1 %collective-permute-start.7 = (bf16[1024,256]{1,0:T(8,128)(2,1)S(1)}, bf16[1024,256]{1,0:T(8,128)(2,1)}, u32[]{:S(2)}, u32[]{:S(2)}) collective-permute-start(bf16[1024,256]{1,0:T(8,128)(2,1)S(1)} %multiply_convert_fusion.2.own_ref), channel_id=1, source_target_pairs={{0,16},{8,24},{16,0},{24,8},{1,17},{9,25},{17,1},{25,9},{2,18},{10... | collective-permute-start | bytes 1572872 | tf_op jit(solution)/shard_map/ppermute | solution.py:500
  31.7 1.7 counts.1
  33.5 3.1 %collective-permute-done.11.other_ref = bf16[1024,256]{1,0:T(8,128)(2,1)S(1)} collective-permute-done((bf16[1024,256]{1,0:T(8,128)(2,1)S(1)}, bf16[1024,256]{1,0:T(8,128)(2,1)S(1)}, u32[]{:S(2)}, u32[]{:S(2)}) %collective-permute-start.11) | collective-permute-done | bytes 524320 | tf_op jit(solution)/shard_map/ppermute | solution.py:500
  36.6 2.0 %collective-permute-start.15 = (f32[4,1024]{1,0:T(4,128)S(1)}, f32[4,1024]{1,0:T(4,128)S(1)}, u32[]{:S(2)}, u32[]{:S(2)}) collective-permute-start(f32[4,1024]{1,0:T(4,128)S(1)} %get-tuple-element.93), channel_id=1, source_target_pairs={{0,1},{1,0},{2,3},{3,2},{4,5},{5,4},{6,7},{7,6},{8,9},{9,8},{10,11... | collective-permute-start | bytes 49160 | tf_op jit(solution)/shard_map/ppermute | solution.py:528
  40.7 7.2 %collective-permute-done.9.other_ref = bf16[1024,256]{1,0:T(8,128)(2,1)} collective-permute-done((bf16[1024,256]{1,0:T(8,128)(2,1)S(1)}, bf16[1024,256]{1,0:T(8,128)(2,1)}, u32[]{:S(2)}, u32[]{:S(2)}) %collective-permute-start.9) | collective-permute-done | bytes 524320 | tf_op jit(solution)/shard_map/ppermute | solution.py:500
  48.0 1.9 %join.8 = (bf16[1024,256]{1,0:T(8,128)(2,1)S(1)}, bf16[1024,1024]{1,0:T(8,128)(2,1)}) custom-call(f32[1]{0:T(128)} %bitcast.sign_ref, bf16[1024,256]{1,0:T(8,128)(2,1)S(1)} %multiply_convert_fusion.1.own_ref, bf16[1024,256]{1,0:T(8,128)(2,1)} %collective-permute-done.9.other_ref, ...), custom_call_target="tpu_custom_call", output_to_operand_aliasing={{1}: (3, {})} | custom-call | flops 1048576 | bytes 2097152 | tf_op jit(solution)/shard_map/join/pallas_call | solution.py:99
  49.8 2.0 %collective-permute-start.21 = (bf16[1024,256]{1,0:T(8,128)(2,1)S(1)}, bf16[1024,256]{1,0:T(8,128)(2,1)S(1)}, u32[]{:S(2)}, u32[]{:S(2)}) collective-permute-start(bf16[1024,256]{1,0:T(8,128)(2,1)S(1)} %get-tuple-element.99.rows_ref), channel_id=1, source_target_pairs={{0,1},{1,0},{2,3},{3,2},{4,5},{5,4},{6,7},{7,6},{8,9},{9,8},{10,11... | collective-permute-start | bytes 1572872 | tf_op jit(solution)/shard_map/ppermute | solution.py:504
  53.0 3.8 %grams.4 = (f32[768,128]{1,0:T(8,128)S(1)}, f32[768,128]{1,0:T(8,128)S(1)}) custom-call(bf16[1024,1024]{1,0:T(8,128)(2,1)S(1)} %get-tuple-element.91.refs_0_.hi_ref, bf16[1024,1024]{1,0:T(8,128)(2,1)S(1)} %get-tuple-element.92.refs_1_.lo_ref, bf16[1024,128]{1,0:T(8,128)(2,1)S(1)} %get-tuple-element.89.left_ref.refs_2_, ...), custom_call_target="tpu_custom_call" | custom-call | flops 2147483648 | bytes 9437184 | tf_op jit(solution)/shard_map/grams/pallas_call | solution.py:279
  56.8 2.1 %collective-permute-start.18 = (f32[768,128]{1,0:T(8,128)S(1)}, f32[768,128]{1,0:T(8,128)S(1)}, u32[]{:S(2)}, u32[]{:S(2)}) collective-permute-start(f32[768,128]{1,0:T(8,128)S(1)} %get-tuple-element.97), channel_id=1, source_target_pairs={{0,2},{1,3},{2,0},{3,1},{4,6},{5,7},{6,4},{7,5},{8,10},{9,11},{10,... | collective-permute-start | bytes 1179656 | tf_op jit(solution)/shard_map/ppermute | solution.py:551
  58.9 1.9 %join.9 = (bf16[1024,256]{1,0:T(8,128)(2,1)S(1)}, bf16[1024,1024]{1,0:T(8,128)(2,1)}) custom-call(f32[1]{0:T(128)} %bitcast.sign_ref, bf16[1024,256]{1,0:T(8,128)(2,1)S(1)} %multiply_convert_fusion.2.own_ref, bf16[1024,256]{1,0:T(8,128)(2,1)} %collective-permute-done.7.other_ref, ...), custom_call_target="tpu_custom_call", output_to_operand_aliasing={{1}: (3, {})} | custom-call | flops 1048576 | bytes 2097152 | tf_op jit(solution)/shard_map/join/pallas_call | solution.py:99
  60.8 1.5 collective-permute-start.20
  62.3 1.9 %share.3.refs_3_ = f32[1024,256]{1,0:T(8,128)S(1)} custom-call(bf16[1024,1024]{1,0:T(8,128)(2,1)S(1)} %get-tuple-element.91.refs_0_.hi_ref, bf16[1024,1024]{1,0:T(8,128)(2,1)S(1)} %get-tuple-element.92.refs_1_.lo_ref, bf16[1024,256]{1,0:T(8,128)(2,1)S(1)} %get-tuple-element.100.rows_ref), custom_call_target="tpu_custom_call" | custom-call | flops 1073741824 | bytes 5242880 | tf_op jit(solution)/shard_map/share/pallas_call | solution.py:236
  64.2 1.9 %share.2.refs_3_ = f32[1024,256]{1,0:T(8,128)S(1)} custom-call(bf16[1024,1024]{1,0:T(8,128)(2,1)S(1)} %get-tuple-element.91.refs_0_.hi_ref, bf16[1024,1024]{1,0:T(8,128)(2,1)S(1)} %get-tuple-element.92.refs_1_.lo_ref, bf16[1024,256]{1,0:T(8,128)(2,1)S(1)} %get-tuple-element.99.rows_ref), custom_call_target="tpu_custom_call" | custom-call | flops 1073741824 | bytes 5242880 | tf_op jit(solution)/shard_map/share/pallas_call | solution.py:236
  66.2 2.6 %collective-permute-start.19 = (f32[384,128]{1,0:T(8,128)S(1)}, f32[384,128]{1,0:T(8,128)S(1)}, u32[]{:S(2)}, u32[]{:S(2)}) collective-permute-start(f32[384,128]{1,0:T(8,128)S(1)} %add.37), channel_id=1, source_target_pairs={{0,4},{1,5},{2,6},{3,7},{4,0},{5,1},{6,2},{7,3},{8,12},{9,13},{10,... | collective-permute-start | bytes 589832 | tf_op jit(solution)/shard_map/ppermute | solution.py:553
  68.8 7.1 %collective-permute-done.22.refs_2_ = bf16[1024,256]{1,0:T(8,128)(2,1)S(1)} collective-permute-done((bf16[1024,256]{1,0:T(8,128)(2,1)S(1)}, bf16[1024,256]{1,0:T(8,128)(2,1)S(1)}, u32[]{:S(2)}, u32[]{:S(2)}) %collective-permute-start.22) | collective-permute-done | bytes 524320 | tf_op jit(solution)/shard_map/ppermute | solution.py:504
  75.9 2.9 %grams.5 = (f32[512,256]{1,0:T(8,128)S(1)}, f32[512,256]{1,0:T(8,128)}, bf16[512,256]{1,0:T(8,128)(2,1)S(1)}, f32[8,1024]{1,0:T(8,128)S(1)}) custom-call(bf16[1024,1024]{1,0:T(8,128)(2,1)S(1)} %get-tuple-element.94.refs_4_.refs_0_.refs_3_, bf16[1024,1024]{1,0:T(8,128)(2,1)S(1)} %get-tuple-element.95.refs_5_.refs_1_.refs_4_, ...), custom_call_target="tpu_custom_call" | custom-call | flops 1073741824 | bytes 4718592 | tf_op jit(solution)/shard_map/grams/pallas_call | solution.py:279
  78.7 2.1 %collective-permute-start.30 = (bf16[512,256]{1,0:T(8,128)(2,1)S(1)}, bf16[512,256]{1,0:T(8,128)(2,1)S(1)}, u32[]{:S(2)}, u32[]{:S(2)}) collective-permute-start(bf16[512,256]{1,0:T(8,128)(2,1)S(1)} %get-tuple-element.111), channel_id=1, source_target_pairs={{0,2},{1,3},{2,0},{3,1},{4,6},{5,7},{6,4},{7,5},{8,10},{9,11},{10,... | collective-permute-start | bytes 786440 | tf_op jit(solution)/shard_map/ppermute | solution.py:551
  80.8 2.9 %grams.6 = (f32[512,256]{1,0:T(8,128)S(1)}, f32[512,256]{1,0:T(8,128)}, bf16[512,256]{1,0:T(8,128)(2,1)S(1)}, f32[8,1024]{1,0:T(8,128)S(1)}) custom-call(bf16[1024,1024]{1,0:T(8,128)(2,1)S(1)} %get-tuple-element.94.refs_4_.refs_0_.refs_3_, bf16[1024,1024]{1,0:T(8,128)(2,1)S(1)} %get-tuple-element.95.refs_5_.refs_1_.refs_4_, ...), custom_call_target="tpu_custom_call" | custom-call | flops 1073741824 | bytes 4718592 | tf_op jit(solution)/shard_map/grams/pallas_call | solution.py:279
  83.7 1.2 collective-permute-done.20.refs_5_
  85.0 4.8 %grams.7 = (f32[512,256]{1,0:T(8,128)S(1)}, f32[512,256]{1,0:T(8,128)}, bf16[512,256]{1,0:T(8,128)(2,1)S(1)}, f32[8,1024]{1,0:T(8,128)S(1)}) custom-call(bf16[1024,1024]{1,0:T(8,128)(2,1)S(1)} %get-tuple-element.91.refs_0_.hi_ref, bf16[1024,1024]{1,0:T(8,128)(2,1)S(1)} %get-tuple-element.92.refs_1_.lo_ref, bf16[1024,256]{1,0:T(8,128)(2,1)S(1)} %get-tuple-element.98.refs_2_, ...), custom_call_target="tpu_custom_call" | custom-call | flops 2147483648 | bytes 9437184 | tf_op jit(solution)/shard_map/grams/pallas_call | solution.py:279
  89.7 1.5 collective-permute-start.26
  91.8 5.0 %factor_first.1.in_ref = f32[256,512]{1,0:T(8,128)S(1)} custom-call(f32[768,128]{1,0:T(8,128)S(1)} %get-tuple-element.96.keep_ref, f32[768,128]{1,0:T(8,128)S(1)} %collective-permute-done.18.near_ref, f32[384,128]{1,0:T(8,128)S(1)} %collective-permute-done.19.far_ref), custom_call_target="tpu_custom_call" | custom-call | flops 10000000000 | bytes 1048576 | tf_op jit(solution)/shard_map/factor_first/pallas_call | solution.py:381
  96.8 2.6 %collective-permute-start.31 = (bf16[256,256]{1,0:T(8,128)(2,1)S(1)}, bf16[256,256]{1,0:T(8,128)(2,1)S(1)}, u32[]{:S(2)}, u32[]{:S(2)}) collective-permute-start(bf16[256,256]{1,0:T(8,128)(2,1)S(1)} %add.40), channel_id=1, source_target_pairs={{0,4},{1,5},{2,6},{3,7},{4,0},{5,1},{6,2},{7,3},{8,12},{9,13},{10,... | collective-permute-start | bytes 393224 | tf_op jit(solution)/shard_map/ppermute | solution.py:553
  99.4 1.4 collective-permute-done.26.near_ref
  101.5 4.8 %collective-permute-done.28.near_ref = bf16[512,256]{1,0:T(8,128)(2,1)S(1)} collective-permute-done((bf16[512,256]{1,0:T(8,128)(2,1)S(1)}, bf16[512,256]{1,0:T(8,128)(2,1)S(1)}, u32[]{:S(2)}, u32[]{:S(2)}) %collective-permute-start.28) | collective-permute-done | bytes 262176 | tf_op jit(solution)/shard_map/ppermute | solution.py:551
  107.2 4.4 %factor_last.1 = (f32[256,1024]{1,0:T(8,128)S(1)}, f32[256,256]{1,0:T(8,128)S(1)}, f32[1,1536]{1,0:T(1,128)S(1)}) custom-call(f32[256,512]{1,0:T(8,128)S(1)} %factor_first.1.in_ref, f32[8,1024]{1,0:T(8,128)S(1)} %get-tuple-element.103.squares_ref), custom_call_target="tpu_custom_call" | custom-call | flops 10000000000 | bytes 1048576 | tf_op jit(solution)/shard_map/factor_last/pallas_call | solution.py:399
  111.6 1.4 collective-permute-start.25
  113.0 1.8 collective-permute-start.24
  114.8 2.2 %collective-permute-done.25.refs_3_ = f32[1,1536]{1,0:T(1,128)S(1)} collective-permute-done((f32[1,1536]{1,0:T(1,128)S(1)}, f32[1,1536]{1,0:T(1,128)S(1)}, u32[]{:S(2)}, u32[]{:S(2)}) %collective-permute-start.25) | collective-permute-done | bytes 6176 | tf_op jit(solution)/shard_map/ppermute | solution.py:559
  118.1 2.7 %collective-permute-done.23.refs_1_ = f32[1,1536]{1,0:T(1,128)} collective-permute-done((f32[1,1536]{1,0:T(1,128)S(1)}, f32[1,1536]{1,0:T(1,128)}, u32[]{:S(2)}, u32[]{:S(2)}) %collective-permute-start.23) | collective-permute-done | bytes 6176 | tf_op jit(solution)/shard_map/ppermute | solution.py:559
  120.8 1.4 judge.1
  124.3 58.1 %conditional.1 = (f32[256,1024]{1,0:T(8,128)S(1)}) conditional(s32[]{:T(128)} %bitcast.6, (f32[256,256]{1,0:T(8,128)S(1)}, f32[512,256]{1,0:T(8,128)S(1)}, bf16[512,256]{1,0:T(8,128)(2,1)S(1)}, bf16[256,256]{1,0:T(8,128)(2,1)}, f32[256,1024]{1,0:T(8,128)S(1)}) %tuple.22, (f32[512,256]{1,0:T(8,128)}, f32[512,256]{1,0:T(8,128)S(1)}, ...), branch_computations={%region_0.1_spmd, %region_1.2_spmd} | conditional | flops 604176384 | bytes 19923248 | solution.py:574
  124.3 2.0 %collective-permute-start.2 = (f32[512,256]{1,0:T(8,128)}, f32[512,256]{1,0:T(8,128)S(1)}, u32[]{:S(2)}, u32[]{:S(2)}) collective-permute-start(f32[512,256]{1,0:T(8,128)} %get-tuple-element.38), channel_id=1, source_target_pairs={{0,2},{1,3},{2,0},{3,1},{4,6},{5,7},{6,4},{7,5},{8,10},{9,11},{10,... | collective-permute-start | bytes 1572872 | tf_op jit(solution)/shard_map/cond/branch_1_fun/ppermute | solution.py:569
  126.4 15.7 %collective-permute-done.4.near_ref = f32[512,256]{1,0:T(8,128)S(1)} collective-permute-done((f32[512,256]{1,0:T(8,128)}, f32[512,256]{1,0:T(8,128)S(1)}, u32[]{:S(2)}, u32[]{:S(2)}) %collective-permute-start.4) | collective-permute-done | bytes 524320 | tf_op jit(solution)/shard_map/cond/branch_1_fun/ppermute | solution.py:569
  142.3 15.9 %collective-permute-done.2.near_ref = f32[512,256]{1,0:T(8,128)S(1)} collective-permute-done((f32[512,256]{1,0:T(8,128)}, f32[512,256]{1,0:T(8,128)S(1)}, u32[]{:S(2)}, u32[]{:S(2)}) %collective-permute-start.2) | collective-permute-done | bytes 524320 | tf_op jit(solution)/shard_map/cond/branch_1_fun/ppermute | solution.py:569
  158.7 5.5 %collective-permute-done.near_ref = f32[512,256]{1,0:T(8,128)S(1)} collective-permute-done((f32[512,256]{1,0:T(8,128)}, f32[512,256]{1,0:T(8,128)S(1)}, u32[]{:S(2)}, u32[]{:S(2)}) %collective-permute-start) | collective-permute-done | bytes 524320 | tf_op jit(solution)/shard_map/cond/branch_1_fun/ppermute | solution.py:569
  165.4 13.8 %collective-permute-done.3.far_ref = f32[256,256]{1,0:T(8,128)S(1)} collective-permute-done((f32[256,256]{1,0:T(8,128)S(1)}, f32[256,256]{1,0:T(8,128)S(1)}, u32[]{:S(2)}, u32[]{:S(2)}) %collective-permute-start.3) | collective-permute-done | bytes 262176 | tf_op jit(solution)/shard_map/cond/branch_1_fun/ppermute | solution.py:570
  179.6 2.4 %collective-permute-done.1.far_ref = f32[256,256]{1,0:T(8,128)S(1)} collective-permute-done((f32[256,256]{1,0:T(8,128)S(1)}, f32[256,256]{1,0:T(8,128)S(1)}, u32[]{:S(2)}, u32[]{:S(2)}) %collective-permute-start.1) | collective-permute-done | bytes 262176 | tf_op jit(solution)/shard_map/cond/branch_1_fun/ppermute | solution.py:570
  (82 shorter events, 14.8 us)
Async XLA Ops:
  3.4 6.0 %copy-start.8 = (bf16[1024,256]{1,0:T(8,128)(2,1)S(1)}, bf16[1024,256]{1,0:T(8,128)(2,1)}, u32[]{:S(2)}) copy-start(bf16[1024,256]{1,0:T(8,128)(2,1)} %mix.3) | copy-start | bytes 1572868
  3.4 6.0 %collective-permute-start.12 = (bf16[1024,256]{1,0:T(8,128)(2,1)}, bf16[1024,256]{1,0:T(8,128)(2,1)S(1)}, u32[]{:S(2)}, u32[]{:S(2)}) collective-permute-start(bf16[1024,256]{1,0:T(8,128)(2,1)} %mix.3), channel_id=1, source_target_pairs={{0,8},{8,0},{16,24},{24,16},{1,9},{9,1},{17,25},{25,17},{2,10},{10... | collective-permute-start | bytes 1572872 | tf_op jit(solution)/shard_map/ppermute | solution.py:519
  8.8 7.1 %copy-start.11 = (bf16[1024,256]{1,0:T(8,128)(2,1)S(1)}, bf16[1024,256]{1,0:T(8,128)(2,1)}, u32[]{:S(2)}) copy-start(bf16[1024,256]{1,0:T(8,128)(2,1)} %get-tuple-element.81) | copy-start | bytes 1572868
  8.8 3.9 %collective-permute-start.10 = (bf16[1024,256]{1,0:T(8,128)(2,1)}, bf16[1024,256]{1,0:T(8,128)(2,1)S(1)}, u32[]{:S(2)}, u32[]{:S(2)}) collective-permute-start(bf16[1024,256]{1,0:T(8,128)(2,1)} %get-tuple-element.82), channel_id=1, source_target_pairs={{0,8},{8,0},{16,24},{24,16},{1,9},{9,1},{17,25},{25,17},{2,10},{10... | collective-permute-start | bytes 1572872 | tf_op jit(solution)/shard_map/ppermute | solution.py:513
  8.9 7.1 %collective-permute-start.8 = (bf16[1024,256]{1,0:T(8,128)(2,1)}, bf16[1024,256]{1,0:T(8,128)(2,1)}, u32[]{:S(2)}, u32[]{:S(2)}) collective-permute-start(bf16[1024,256]{1,0:T(8,128)(2,1)} %get-tuple-element.81), channel_id=1, source_target_pairs={{0,8},{8,0},{16,24},{24,16},{1,9},{9,1},{17,25},{25,17},{2,10},{10... | collective-permute-start | bytes 1572872 | tf_op jit(solution)/shard_map/ppermute | solution.py:513
  9.3 18.9 %collective-permute-start.6 = (bf16[1024,256]{1,0:T(8,128)(2,1)}, bf16[1024,256]{1,0:T(8,128)(2,1)}, u32[]{:S(2)}, u32[]{:S(2)}) collective-permute-start(bf16[1024,256]{1,0:T(8,128)(2,1)} %get-tuple-element.80), channel_id=1, source_target_pairs={{0,8},{8,0},{16,24},{24,16},{1,9},{9,1},{17,25},{25,17},{2,10},{10... | collective-permute-start | bytes 1572872 | tf_op jit(solution)/shard_map/ppermute | solution.py:513
  9.6 10.2 %collective-permute-start.14 = (bf16[1024,128]{1,0:T(8,128)(2,1)S(1)}, bf16[1024,128]{1,0:T(8,128)(2,1)S(1)}, u32[]{:S(2)}, u32[]{:S(2)}) collective-permute-start(bf16[1024,128]{1,0:T(8,128)(2,1)S(1)} %get-tuple-element.116.own_ref), channel_id=1, source_target_pairs={{0,16},{8,24},{16,0},{24,8},{1,17},{9,25},{17,1},{25,9},{2,18},{10... | collective-permute-start | bytes 786440 | tf_op jit(solution)/shard_map/ppermute | solution.py:500
  12.6 12.8 %collective-permute-start.13 = (bf16[1024,128]{1,0:T(8,128)(2,1)S(1)}, bf16[1024,128]{1,0:T(8,128)(2,1)S(1)}, u32[]{:S(2)}, u32[]{:S(2)}) collective-permute-start(bf16[1024,128]{1,0:T(8,128)(2,1)S(1)} %get-tuple-element.117.own_ref), channel_id=1, source_target_pairs={{0,16},{8,24},{16,0},{24,8},{1,17},{9,25},{17,1},{25,9},{2,18},{10... | collective-permute-start | bytes 786440 | tf_op jit(solution)/shard_map/ppermute | solution.py:500
  13.9 22.7 %collective-permute-start.11 = (bf16[1024,256]{1,0:T(8,128)(2,1)S(1)}, bf16[1024,256]{1,0:T(8,128)(2,1)S(1)}, u32[]{:S(2)}, u32[]{:S(2)}) collective-permute-start(bf16[1024,256]{1,0:T(8,128)(2,1)S(1)} %multiply_convert_fusion.own_ref), channel_id=1, source_target_pairs={{0,16},{8,24},{16,0},{24,8},{1,17},{9,25},{17,1},{25,9},{2,18},{10... | collective-permute-start | bytes 1572872 | tf_op jit(solution)/shard_map/ppermute | solution.py:500
  17.2 30.8 %collective-permute-start.9 = (bf16[1024,256]{1,0:T(8,128)(2,1)S(1)}, bf16[1024,256]{1,0:T(8,128)(2,1)}, u32[]{:S(2)}, u32[]{:S(2)}) collective-permute-start(bf16[1024,256]{1,0:T(8,128)(2,1)S(1)} %multiply_convert_fusion.1.own_ref), channel_id=1, source_target_pairs={{0,16},{8,24},{16,0},{24,8},{1,17},{9,25},{17,1},{25,9},{2,18},{10... | collective-permute-start | bytes 1572872 | tf_op jit(solution)/shard_map/ppermute | solution.py:500
  25.4 6.4 %copy-start.1 = (s32[2048]{0:T(1024)S(1)}, s32[2048]{0:T(1024)}, u32[]{:S(2)}) copy-start(s32[2048]{0:T(1024)} %param.9) | copy-start | bytes 24580
  25.4 6.4 %copy-start.2 = (s32[2048,1]{0,1:T(1,128)S(1)}, s32[2048,1]{0,1:T(1,128)}, u32[]{:S(2)}) copy-start(s32[2048,1]{0,1:T(1,128)} %param.10) | copy-start | bytes 24580
  26.2 25.7 %collective-permute-start.17 = (bf16[1024,128]{1,0:T(8,128)(2,1)S(1)}, bf16[1024,128]{1,0:T(8,128)(2,1)S(1)}, u32[]{:S(2)}, u32[]{:S(2)}) collective-permute-start(bf16[1024,128]{1,0:T(8,128)(2,1)S(1)} %get-tuple-element.90.right_ref.refs_3_), channel_id=1, source_target_pairs={{0,1},{1,0},{2,3},{3,2},{4,5},{5,4},{6,7},{7,6},{8,9},{9,8},{10,11... | collective-permute-start | bytes 786440 | tf_op jit(solution)/shard_map/ppermute | solution.py:504
  28.2 23.7 %collective-permute-start.16 = (bf16[1024,128]{1,0:T(8,128)(2,1)S(1)}, bf16[1024,128]{1,0:T(8,128)(2,1)S(1)}, u32[]{:S(2)}, u32[]{:S(2)}) collective-permute-start(bf16[1024,128]{1,0:T(8,128)(2,1)S(1)} %get-tuple-element.89.left_ref.refs_2_), channel_id=1, source_target_pairs={{0,1},{1,0},{2,3},{3,2},{4,5},{5,4},{6,7},{7,6},{8,9},{9,8},{10,11... | collective-permute-start | bytes 786440 | tf_op jit(solution)/shard_map/ppermute | solution.py:504
  29.6 29.3 %collective-permute-start.7 = (bf16[1024,256]{1,0:T(8,128)(2,1)S(1)}, bf16[1024,256]{1,0:T(8,128)(2,1)}, u32[]{:S(2)}, u32[]{:S(2)}) collective-permute-start(bf16[1024,256]{1,0:T(8,128)(2,1)S(1)} %multiply_convert_fusion.2.own_ref), channel_id=1, source_target_pairs={{0,16},{8,24},{16,0},{24,8},{1,17},{9,25},{17,1},{25,9},{2,18},{10... | collective-permute-start | bytes 1572872 | tf_op jit(solution)/shard_map/ppermute | solution.py:500
  36.6 15.2 %collective-permute-start.15 = (f32[4,1024]{1,0:T(4,128)S(1)}, f32[4,1024]{1,0:T(4,128)S(1)}, u32[]{:S(2)}, u32[]{:S(2)}) collective-permute-start(f32[4,1024]{1,0:T(4,128)S(1)} %get-tuple-element.93), channel_id=1, source_target_pairs={{0,1},{1,0},{2,3},{3,2},{4,5},{5,4},{6,7},{7,6},{8,9},{9,8},{10,11... | collective-permute-start | bytes 49160 | tf_op jit(solution)/shard_map/ppermute | solution.py:528
  49.8 31.0 %collective-permute-start.21 = (bf16[1024,256]{1,0:T(8,128)(2,1)S(1)}, bf16[1024,256]{1,0:T(8,128)(2,1)S(1)}, u32[]{:S(2)}, u32[]{:S(2)}) collective-permute-start(bf16[1024,256]{1,0:T(8,128)(2,1)S(1)} %get-tuple-element.99.rows_ref), channel_id=1, source_target_pairs={{0,1},{1,0},{2,3},{3,2},{4,5},{5,4},{6,7},{7,6},{8,9},{9,8},{10,11... | collective-permute-start | bytes 1572872 | tf_op jit(solution)/shard_map/ppermute | solution.py:504
  51.8 24.0 %collective-permute-start.22 = (bf16[1024,256]{1,0:T(8,128)(2,1)S(1)}, bf16[1024,256]{1,0:T(8,128)(2,1)S(1)}, u32[]{:S(2)}, u32[]{:S(2)}) collective-permute-start(bf16[1024,256]{1,0:T(8,128)(2,1)S(1)} %get-tuple-element.100.rows_ref), channel_id=1, source_target_pairs={{0,1},{1,0},{2,3},{3,2},{4,5},{5,4},{6,7},{7,6},{8,9},{9,8},{10,11... | collective-permute-start | bytes 1572872 | tf_op jit(solution)/shard_map/ppermute | solution.py:504
  56.8 9.3 %collective-permute-start.18 = (f32[768,128]{1,0:T(8,128)S(1)}, f32[768,128]{1,0:T(8,128)S(1)}, u32[]{:S(2)}, u32[]{:S(2)}) collective-permute-start(f32[768,128]{1,0:T(8,128)S(1)} %get-tuple-element.97), channel_id=1, source_target_pairs={{0,2},{1,3},{2,0},{3,1},{4,6},{5,7},{6,4},{7,5},{8,10},{9,11},{10,... | collective-permute-start | bytes 1179656 | tf_op jit(solution)/shard_map/ppermute | solution.py:551
  60.8 24.2 %collective-permute-start.20 = (bf16[1024,256]{1,0:T(8,128)(2,1)S(1)}, bf16[1024,256]{1,0:T(8,128)(2,1)S(1)}, u32[]{:S(2)}, u32[]{:S(2)}) collective-permute-start(bf16[1024,256]{1,0:T(8,128)(2,1)S(1)} %get-tuple-element.98.refs_2_), channel_id=1, source_target_pairs={{0,1},{1,0},{2,3},{3,2},{4,5},{5,4},{6,7},{7,6},{8,9},{9,8},{10,11... | collective-permute-start | bytes 1572872 | tf_op jit(solution)/shard_map/ppermute | solution.py:504
  66.2 25.6 %collective-permute-start.19 = (f32[384,128]{1,0:T(8,128)S(1)}, f32[384,128]{1,0:T(8,128)S(1)}, u32[]{:S(2)}, u32[]{:S(2)}) collective-permute-start(f32[384,128]{1,0:T(8,128)S(1)} %add.37), channel_id=1, source_target_pairs={{0,4},{1,5},{2,6},{3,7},{4,0},{5,1},{6,2},{7,3},{8,12},{9,13},{10,... | collective-permute-start | bytes 589832 | tf_op jit(solution)/shard_map/ppermute | solution.py:553
  78.7 18.0 %collective-permute-start.30 = (bf16[512,256]{1,0:T(8,128)(2,1)S(1)}, bf16[512,256]{1,0:T(8,128)(2,1)S(1)}, u32[]{:S(2)}, u32[]{:S(2)}) collective-permute-start(bf16[512,256]{1,0:T(8,128)(2,1)S(1)} %get-tuple-element.111), channel_id=1, source_target_pairs={{0,2},{1,3},{2,0},{3,1},{4,6},{5,7},{6,4},{7,5},{8,10},{9,11},{10,... | collective-permute-start | bytes 786440 | tf_op jit(solution)/shard_map/ppermute | solution.py:551
  89.7 11.0 %copy-start.4 = (f32[512,256]{1,0:T(8,128)}, f32[512,256]{1,0:T(8,128)S(1)}, u32[]{:S(2)}) copy-start(f32[512,256]{1,0:T(8,128)S(1)} %get-tuple-element.106.keep_ref) | copy-start | bytes 1572868
  89.7 11.0 %collective-permute-start.26 = (bf16[512,256]{1,0:T(8,128)(2,1)S(1)}, bf16[512,256]{1,0:T(8,128)(2,1)S(1)}, u32[]{:S(2)}, u32[]{:S(2)}) collective-permute-start(bf16[512,256]{1,0:T(8,128)(2,1)S(1)} %get-tuple-element.107), channel_id=1, source_target_pairs={{0,2},{1,3},{2,0},{3,1},{4,6},{5,7},{6,4},{7,5},{8,10},{9,11},{10,... | collective-permute-start | bytes 786440 | tf_op jit(solution)/shard_map/ppermute | solution.py:551
  91.3 15.1 %collective-permute-start.28 = (bf16[512,256]{1,0:T(8,128)(2,1)S(1)}, bf16[512,256]{1,0:T(8,128)(2,1)S(1)}, u32[]{:S(2)}, u32[]{:S(2)}) collective-permute-start(bf16[512,256]{1,0:T(8,128)(2,1)S(1)} %get-tuple-element.109), channel_id=1, source_target_pairs={{0,2},{1,3},{2,0},{3,1},{4,6},{5,7},{6,4},{7,5},{8,10},{9,11},{10,... | collective-permute-start | bytes 786440 | tf_op jit(solution)/shard_map/ppermute | solution.py:551
  96.8 26.0 %collective-permute-start.31 = (bf16[256,256]{1,0:T(8,128)(2,1)S(1)}, bf16[256,256]{1,0:T(8,128)(2,1)S(1)}, u32[]{:S(2)}, u32[]{:S(2)}) collective-permute-start(bf16[256,256]{1,0:T(8,128)(2,1)S(1)} %add.40), channel_id=1, source_target_pairs={{0,4},{1,5},{2,6},{3,7},{4,0},{5,1},{6,2},{7,3},{8,12},{9,13},{10,... | collective-permute-start | bytes 393224 | tf_op jit(solution)/shard_map/ppermute | solution.py:553
  100.8 10.8 %copy-start.9 = (bf16[512,256]{1,0:T(8,128)(2,1)}, bf16[512,256]{1,0:T(8,128)(2,1)S(1)}, u32[]{:S(2)}) copy-start(bf16[512,256]{1,0:T(8,128)(2,1)S(1)} %collective-permute-done.26.near_ref) | copy-start | bytes 786436
  100.8 22.9 %collective-permute-start.27 = (bf16[256,256]{1,0:T(8,128)(2,1)S(1)}, bf16[256,256]{1,0:T(8,128)(2,1)}, u32[]{:S(2)}, u32[]{:S(2)}) collective-permute-start(bf16[256,256]{1,0:T(8,128)(2,1)S(1)} %add.38), channel_id=1, source_target_pairs={{0,4},{1,5},{2,6},{3,7},{4,0},{5,1},{6,2},{7,3},{8,12},{9,13},{10,... | collective-permute-start | bytes 393224 | tf_op jit(solution)/shard_map/ppermute | solution.py:553
  106.4 16.8 %collective-permute-start.29 = (bf16[256,256]{1,0:T(8,128)(2,1)S(1)}, bf16[256,256]{1,0:T(8,128)(2,1)S(1)}, u32[]{:S(2)}, u32[]{:S(2)}) collective-permute-start(bf16[256,256]{1,0:T(8,128)(2,1)S(1)} %add.39), channel_id=1, source_target_pairs={{0,4},{1,5},{2,6},{3,7},{4,0},{5,1},{6,2},{7,3},{8,12},{9,13},{10,... | collective-permute-start | bytes 393224 | tf_op jit(solution)/shard_map/ppermute | solution.py:553
  111.6 9.2 %copy-start = (f32[1,1536]{1,0:T(1,128)}, f32[1,1536]{1,0:T(1,128)S(1)}, u32[]{:S(2)}) copy-start(f32[1,1536]{1,0:T(1,128)S(1)} %get-tuple-element.104.refs_0_) | copy-start | bytes 18436
  111.6 5.5 %collective-permute-start.25 = (f32[1,1536]{1,0:T(1,128)S(1)}, f32[1,1536]{1,0:T(1,128)S(1)}, u32[]{:S(2)}, u32[]{:S(2)}) collective-permute-start(f32[1,1536]{1,0:T(1,128)S(1)} %get-tuple-element.104.refs_0_), channel_id=1, source_target_pairs={{0,6},{1,7},{2,4},{3,5},{4,2},{5,3},{6,0},{7,1},{8,14},{9,15},{10,... | collective-permute-start | bytes 18440 | tf_op jit(solution)/shard_map/ppermute | solution.py:559
  113.0 4.5 %collective-permute-start.24 = (f32[1,1536]{1,0:T(1,128)S(1)}, f32[1,1536]{1,0:T(1,128)S(1)}, u32[]{:S(2)}, u32[]{:S(2)}) collective-permute-start(f32[1,1536]{1,0:T(1,128)S(1)} %get-tuple-element.104.refs_0_), channel_id=1, source_target_pairs={{0,4},{1,5},{2,6},{3,7},{4,0},{5,1},{6,2},{7,3},{8,12},{9,13},{10,... | collective-permute-start | bytes 18440 | tf_op jit(solution)/shard_map/ppermute | solution.py:559
  117.1 3.7 %copy-start.12 = (f32[1,1536]{1,0:T(1,128)}, f32[1,1536]{1,0:T(1,128)S(1)}, u32[]{:S(2)}) copy-start(f32[1,1536]{1,0:T(1,128)S(1)} %collective-permute-done.25.refs_3_) | copy-start | bytes 18436
  117.1 3.7 %collective-permute-start.23 = (f32[1,1536]{1,0:T(1,128)S(1)}, f32[1,1536]{1,0:T(1,128)}, u32[]{:S(2)}, u32[]{:S(2)}) collective-permute-start(f32[1,1536]{1,0:T(1,128)S(1)} %get-tuple-element.104.refs_0_), channel_id=1, source_target_pairs={{0,2},{1,3},{2,0},{3,1},{4,6},{5,7},{6,4},{7,5},{8,10},{9,11},{10,... | collective-permute-start | bytes 18440 | tf_op jit(solution)/shard_map/ppermute | solution.py:559
  117.5 0.6 copy-start.13
  123.2 1.0 copy-start.5
  123.2 1.1 copy-start.10
  124.3 2.0 %copy-start.6 = (f32[512,256]{1,0:T(8,128)}, f32[512,256]{1,0:T(8,128)S(1)}, u32[]{:S(2)}) copy-start(f32[512,256]{1,0:T(8,128)S(1)} %get-tuple-element.35.keep_ref) | copy-start | bytes 1572868 | tf_op jit(solution)/shard_map/cond
  124.3 17.8 %collective-permute-start.4 = (f32[512,256]{1,0:T(8,128)}, f32[512,256]{1,0:T(8,128)S(1)}, u32[]{:S(2)}, u32[]{:S(2)}) collective-permute-start(f32[512,256]{1,0:T(8,128)} %get-tuple-element.40), channel_id=1, source_target_pairs={{0,2},{1,3},{2,0},{3,1},{4,6},{5,7},{6,4},{7,5},{8,10},{9,11},{10,... | collective-permute-start | bytes 1572872 | tf_op jit(solution)/shard_map/cond/branch_1_fun/ppermute | solution.py:569
  124.3 33.8 %collective-permute-start.2 = (f32[512,256]{1,0:T(8,128)}, f32[512,256]{1,0:T(8,128)S(1)}, u32[]{:S(2)}, u32[]{:S(2)}) collective-permute-start(f32[512,256]{1,0:T(8,128)} %get-tuple-element.38), channel_id=1, source_target_pairs={{0,2},{1,3},{2,0},{3,1},{4,6},{5,7},{6,4},{7,5},{8,10},{9,11},{10,... | collective-permute-start | bytes 1572872 | tf_op jit(solution)/shard_map/cond/branch_1_fun/ppermute | solution.py:569
  126.4 37.9 %copy-start.7 = (f32[512,256]{1,0:T(8,128)S(1)}, f32[512,256]{1,0:T(8,128)}, u32[]{:S(2)}) copy-start(f32[512,256]{1,0:T(8,128)} %copy-done.6) | copy-start | bytes 1572868 | tf_op jit(solution)/shard_map/cond
  126.4 37.9 %collective-permute-start = (f32[512,256]{1,0:T(8,128)}, f32[512,256]{1,0:T(8,128)S(1)}, u32[]{:S(2)}, u32[]{:S(2)}) collective-permute-start(f32[512,256]{1,0:T(8,128)} %get-tuple-element.36), channel_id=1, source_target_pairs={{0,2},{1,3},{2,0},{3,1},{4,6},{5,7},{6,4},{7,5},{8,10},{9,11},{10,... | collective-permute-start | bytes 1572872 | tf_op jit(solution)/shard_map/cond/branch_1_fun/ppermute | solution.py:569
  142.2 22.8 %collective-permute-start.5 = (f32[256,256]{1,0:T(8,128)S(1)}, f32[256,256]{1,0:T(8,128)S(1)}, u32[]{:S(2)}, u32[]{:S(2)}) collective-permute-start(f32[256,256]{1,0:T(8,128)S(1)} %add.36), channel_id=1, source_target_pairs={{0,4},{1,5},{2,6},{3,7},{4,0},{5,1},{6,2},{7,3},{8,12},{9,13},{10,... | collective-permute-start | bytes 786440 | tf_op jit(solution)/shard_map/cond/branch_1_fun/ppermute | solution.py:570
  158.2 21.0 %collective-permute-start.3 = (f32[256,256]{1,0:T(8,128)S(1)}, f32[256,256]{1,0:T(8,128)S(1)}, u32[]{:S(2)}, u32[]{:S(2)}) collective-permute-start(f32[256,256]{1,0:T(8,128)S(1)} %add.35), channel_id=1, source_target_pairs={{0,4},{1,5},{2,6},{3,7},{4,0},{5,1},{6,2},{7,3},{8,12},{9,13},{10,... | collective-permute-start | bytes 786440 | tf_op jit(solution)/shard_map/cond/branch_1_fun/ppermute | solution.py:570
  164.3 17.7 %collective-permute-start.1 = (f32[256,256]{1,0:T(8,128)S(1)}, f32[256,256]{1,0:T(8,128)S(1)}, u32[]{:S(2)}, u32[]{:S(2)}) collective-permute-start(f32[256,256]{1,0:T(8,128)S(1)} %add.34), channel_id=1, source_target_pairs={{0,4},{1,5},{2,6},{3,7},{4,0},{5,1},{6,2},{7,3},{8,12},{9,13},{10,... | collective-permute-start | bytes 786440 | tf_op jit(solution)/shard_map/cond/branch_1_fun/ppermute | solution.py:570
  182.4 1.0 copy-start.3
